TPU v7x, 32 devices: a whole 2x2x4 slice. The times are simulated.
32 devices in a mesh: shard: 2 (over x), ctx: 4 (over z), tp: 4 (over y, core).
Axes of the slice: x: 2, y: 2, z: 4, core: 2. Of those that a mesh axis runs over, the one named last changes fastest.
Arguments:
- x_img: bfloat16 [6, 1024, 1536], P('shard', ('ctx', 'tp')), may hold values from -6 to 6
- x_txt: bfloat16 [6, 160, 1536], P('shard', ('ctx', 'tp')), may hold values from -6 to 6
- cond: bfloat16 [6, 1536], P('shard'), may hold values from -6 to 6
- lengths: int32 [6], P('shard'), may hold values from 77 to 154, as said below
- mod_w: bfloat16 [2, 1536, 6, 1536], P(None, ('shard', 'ctx'), None, 'tp'), may hold values from -0.15625 to 0.15625
- qkv_w: bfloat16 [2, 3, 1536, 1536], P(None, None, ('shard', 'ctx'), 'tp'), may hold values from -0.15625 to 0.15625
- o_w: bfloat16 [2, 1536, 1536], P(None, 'tp', ('shard', 'ctx')), may hold values from -0.875 to 0.875
- up_w: bfloat16 [2, 1536, 6144], P(None, ('shard', 'ctx'), 'tp'), may hold values from -0.15625 to 0.15625
- down_w: bfloat16 [2, 6144, 1536], P(None, 'tp', ('shard', 'ctx')), may hold values from -0.078125 to 0.078125
- norm_gain: float32 [2, 2, 64], replicated, may hold values from 1 to 1.6
- threshold: float32 [], replicated, may hold values from 1 to 2
- cot_img: bfloat16 [6, 1024, 1536], P('shard', ('ctx', 'tp')), may hold values from -6 to 6
- cot_txt: bfloat16 [6, 160, 1536], P('shard', ('ctx', 'tp')), may hold values from -6 to 6
Outputs:
- out_img: bfloat16 [6, 1024, 1536], P('shard', ('ctx', 'tp'))
- out_txt: bfloat16 [6, 160, 1536], P('shard', ('ctx', 'tp'))
- grad_img: float32 [6, 1024, 1536], P('shard', ('ctx', 'tp'))
- grad_txt: float32 [6, 160, 1536], P('shard', ('ctx', 'tp'))
- grad_cond: float32 [6, 1536], P('shard')
- grad_mod: float32 [2, 1536, 6, 1536], P(None, ('shard', 'ctx'), None, 'tp')
- grad_qkv: float32 [2, 3, 1536, 1536], P(None, None, ('shard', 'ctx'), 'tp')
- grad_o: float32 [2, 1536, 1536], P(None, 'tp', ('shard', 'ctx'))
- grad_up: float32 [2, 1536, 6144], P(None, ('shard', 'ctx'), 'tp')
- grad_down: float32 [2, 6144, 1536], P(None, 'tp', ('shard', 'ctx'))
- grad_gain: float32 [2, 2, 64], replicated
- clipped_qk: float32 [2, 2, 1536, 1536], P(None, None, ('shard', 'ctx'), 'tp')
- logit_peaks: float32 [24], P('tp')
Inputs may be any that keep to these rules, and one draw needn't show every extreme that they name: lengths: text tokens of a sequence; some sequence has exactly 154.
All inputs are finite; a program needn't handle non-finite values.
Results may differ from a plain program's by a relative error of at most 0.017.
Values may be sent and summed in bfloat16 or wider, within the bound.
No kernel may reach another device: no remote copies, remote signals or barrier semaphores. Data moves between devices by JAX's collectives and lax.ppermute only.
A program may use at most 256 MiB of HBM per device.

v0:
```python
import jax
import jax.numpy as jnp
from jax import lax
from jax.sharding import PartitionSpec as P

EPS = 1e-06
QUERY_SCALE = 0.125


def layer_norm(values):
    center = values - jnp.mean(values, axis=-1, keepdims=True)
    spread = jnp.mean(center * center, axis=-1, keepdims=True)
    return center * lax.rsqrt(spread + EPS)


def modulate(values, shift, scale):
    return layer_norm(values) * (1.0 + scale) + shift


def head_norm(values, gain_vec, factor):
    shape_in = values.shape
    split_heads = values.reshape(
        shape_in[:-1] + (shape_in[-1] // gain_vec.shape[0], gain_vec.shape[0])
    )
    square = jnp.mean(split_heads * split_heads, axis=-1, keepdims=True)
    return (split_heads * lax.rsqrt(square + EPS) * gain_vec * factor).reshape(shape_in)


def gelu_tanh(values):
    return jax.nn.gelu(values, approximate=True)


def gather_rows(first, second):
    return (
        lax.all_gather(first, "tp", axis=1, tiled=True),
        lax.all_gather(second, "tp", axis=1, tiled=True),
    )


def reduce_rows(first, second):
    return (
        lax.psum_scatter(first, "tp", scatter_dimension=1, tiled=True),
        lax.psum_scatter(second, "tp", scatter_dimension=1, tiled=True),
    )


def split_heads_major(values, head_dim):
    seq_count, row_count, columns = values.shape
    return values.reshape(seq_count, row_count, columns // head_dim, head_dim).transpose(2, 0, 1, 3)


def merge_heads(values):
    head_count, seq_count, row_count, head_dim = values.shape
    return values.transpose(1, 2, 0, 3).reshape(seq_count, row_count, head_count * head_dim)


def key_mask(lengths, img_member, txt_member, ctx_count):
    member_rows = img_member + txt_member
    key_place = jnp.arange(member_rows * ctx_count, dtype=jnp.int32)
    within = key_place % member_rows
    member = key_place // member_rows
    text_place = member * txt_member + within - img_member
    return (within < img_member)[None, :] | (text_place[None, :] < lengths[:, None])


def local(
    x_img,
    x_txt,
    cond,
    lengths,
    mod_w,
    qkv_w,
    o_w,
    up_w,
    down_w,
    norm_gain,
    threshold,
    cot_img,
    cot_txt,
):
    tp_count = lax.axis_size("tp")
    ctx_count = lax.axis_size("ctx")
    shard_count = lax.axis_size("shard")
    head_dim = norm_gain.shape[2]
    img_member = x_img.shape[1] * tp_count
    txt_member = x_txt.shape[1] * tp_count
    local_feat = mod_w.shape[3]
    owned_rows = mod_w.shape[1]
    gathered = (
        lax.all_gather(qkv_w, ("shard", "ctx"), axis=2, tiled=True),
        lax.all_gather(o_w, ("shard", "ctx"), axis=2, tiled=True),
        lax.all_gather(up_w, ("shard", "ctx"), axis=1, tiled=True),
        lax.all_gather(down_w, ("shard", "ctx"), axis=2, tiled=True),
    )
    qkv_all, out_all, up_all, down_all = gathered
    cond_float = cond.astype(jnp.float32)
    cond_act = jax.nn.silu(cond_float).astype(jnp.bfloat16)
    mod_all = lax.all_gather(mod_w, ("shard", "ctx"), axis=1, tiled=True)
    mod_local = jnp.einsum("sd,tdkf->tskf", cond_act, mod_all, preferred_element_type=jnp.float32)
    modulation = lax.all_gather(mod_local, "tp", axis=3, tiled=True)
    inputs = (x_img.astype(jnp.float32), x_txt.astype(jnp.float32))

    def entry(stream, index):
        return modulation[stream, :, index][:, None, :]

    first_low = [
        modulate(inputs[s], entry(s, 0), entry(s, 1)).astype(jnp.bfloat16) for s in range(2)
    ]
    first_in = gather_rows(first_low[0], first_low[1])
    projected = [
        jnp.einsum("srd,cdf->csrf", first_in[s], qkv_all[s], preferred_element_type=jnp.float32)
        for s in range(2)
    ]
    queries = jnp.concatenate(
        [head_norm(projected[s][0], norm_gain[s, 0], QUERY_SCALE) for s in range(2)], axis=1
    ).astype(jnp.bfloat16)
    keys_local = jnp.concatenate(
        [head_norm(projected[s][1], norm_gain[s, 1], 1.0) for s in range(2)], axis=1
    ).astype(jnp.bfloat16)
    values_local = jnp.concatenate([projected[s][2] for s in range(2)], axis=1).astype(jnp.bfloat16)
    keys_all, values_all = (
        lax.all_gather(keys_local, "ctx", axis=1, tiled=True),
        lax.all_gather(values_local, "ctx", axis=1, tiled=True),
    )
    key_masks = key_mask(lengths, img_member, txt_member, ctx_count)

    def attend_head(operands):
        query_head, key_head, value_head = operands
        scores = jnp.einsum(
            "sqd,skd->sqk", query_head, key_head, preferred_element_type=jnp.float32
        )
        masked = jnp.where(key_masks[:, None, :], scores, -jnp.inf)
        highest = jnp.max(masked, axis=-1, keepdims=True)
        weights_exp = jnp.exp(masked - highest)
        denominator = jnp.sum(weights_exp, axis=-1, keepdims=True)
        probabilities = (weights_exp / denominator).astype(jnp.bfloat16)
        mixed_out = jnp.einsum(
            "sqk,skd->sqd", probabilities, value_head, preferred_element_type=jnp.float32
        )
        return (
            mixed_out.astype(jnp.bfloat16),
            (highest + jnp.log(denominator))[..., 0],
            jnp.max(highest),
        )

    query_heads = split_heads_major(queries, head_dim)
    key_heads = split_heads_major(keys_all, head_dim)
    value_heads = split_heads_major(values_all, head_dim)
    attended, log_norm, head_peaks = lax.map(attend_head, (query_heads, key_heads, value_heads))
    peaks = lax.pmax(head_peaks, ("shard", "ctx"))
    attended = merge_heads(attended)
    segments = (attended[:, :img_member], attended[:, img_member:])
    attn_parts = [
        jnp.einsum("srf,fd->srd", segments[s], out_all[s], preferred_element_type=jnp.float32)
        for s in range(2)
    ]
    attn_out = reduce_rows(attn_parts[0], attn_parts[1])
    mid = [inputs[s] + entry(s, 2) * attn_out[s] for s in range(2)]
    second_low = [modulate(mid[s], entry(s, 3), entry(s, 4)).astype(jnp.bfloat16) for s in range(2)]
    second_in = gather_rows(second_low[0], second_low[1])
    hidden_pre = [
        jnp.einsum("srd,df->srf", second_in[s], up_all[s], preferred_element_type=jnp.float32)
        for s in range(2)
    ]
    hidden_low = [gelu_tanh(hidden_pre[s]).astype(jnp.bfloat16) for s in range(2)]
    mlp_parts = [
        jnp.einsum("srf,fd->srd", hidden_low[s], down_all[s], preferred_element_type=jnp.float32)
        for s in range(2)
    ]
    mlp_out = reduce_rows(mlp_parts[0], mlp_parts[1])
    results = [(mid[s] + entry(s, 5) * mlp_out[s]).astype(jnp.bfloat16) for s in range(2)]
    qkv_back, out_back, up_back, down_back = (
        lax.all_gather(qkv_w, ("shard", "ctx"), axis=2, tiled=True),
        lax.all_gather(o_w, ("shard", "ctx"), axis=2, tiled=True),
        lax.all_gather(up_w, ("shard", "ctx"), axis=1, tiled=True),
        lax.all_gather(down_w, ("shard", "ctx"), axis=2, tiled=True),
    )
    grad_out = (cot_img.astype(jnp.float32), cot_txt.astype(jnp.float32))
    mlp_grad_low = [(grad_out[s] * entry(s, 5)).astype(jnp.bfloat16) for s in range(2)]
    gate_two = [jnp.sum(grad_out[s] * mlp_out[s], axis=1) for s in range(2)]
    mlp_grad_in = gather_rows(mlp_grad_low[0], mlp_grad_low[1])
    grad_down = jnp.stack(
        [
            jnp.einsum(
                "srf,srd->fd", hidden_low[s], mlp_grad_in[s], preferred_element_type=jnp.float32
            )
            for s in range(2)
        ]
    )
    pre_grad = []
    for s in range(2):
        hidden_back = jnp.einsum(
            "srd,fd->srf", mlp_grad_in[s], down_back[s], preferred_element_type=jnp.float32
        )
        unused, gelu_vjp = jax.vjp(gelu_tanh, hidden_pre[s])
        pre_grad.append(gelu_vjp(hidden_back)[0].astype(jnp.bfloat16))
    grad_up = jnp.stack(
        [
            jnp.einsum("srd,srf->df", second_in[s], pre_grad[s], preferred_element_type=jnp.float32)
            for s in range(2)
        ]
    )
    second_parts = [
        jnp.einsum("srf,df->srd", pre_grad[s], up_back[s], preferred_element_type=jnp.float32)
        for s in range(2)
    ]
    second_grad = reduce_rows(second_parts[0], second_parts[1])
    mid_grad = []
    shift_two = []
    scale_two = []
    for s in range(2):
        unused, mod_vjp = jax.vjp(modulate, mid[s], entry(s, 3), entry(s, 4))
        mid_part, shift_part, scale_part = mod_vjp(second_grad[s])
        mid_grad.append(grad_out[s] + mid_part)
        shift_two.append(shift_part[:, 0])
        scale_two.append(scale_part[:, 0])
    attn_grad_low = [(mid_grad[s] * entry(s, 2)).astype(jnp.bfloat16) for s in range(2)]
    gate_one = [jnp.sum(mid_grad[s] * attn_out[s], axis=1) for s in range(2)]
    attn_grad_in = gather_rows(attn_grad_low[0], attn_grad_low[1])
    grad_outproj = jnp.stack(
        [
            jnp.einsum(
                "srf,srd->fd", segments[s], attn_grad_in[s], preferred_element_type=jnp.float32
            )
            for s in range(2)
        ]
    )
    mixed_grad = jnp.concatenate(
        [
            jnp.einsum(
                "srd,fd->srf", attn_grad_in[s], out_back[s], preferred_element_type=jnp.float32
            )
            for s in range(2)
        ],
        axis=1,
    ).astype(jnp.bfloat16)

    def attend_back(operands):
        query_head, key_head, value_head, grad_head, log_head = operands
        scores = jnp.einsum(
            "sqd,skd->sqk", query_head, key_head, preferred_element_type=jnp.float32
        )
        masked = jnp.where(key_masks[:, None, :], scores, -jnp.inf)
        probabilities = jnp.exp(masked - log_head[..., None])
        grad_prob = jnp.einsum(
            "sqd,skd->sqk", grad_head, value_head, preferred_element_type=jnp.float32
        )
        grad_score = (
            probabilities * (grad_prob - jnp.sum(probabilities * grad_prob, axis=-1, keepdims=True))
        ).astype(jnp.bfloat16)
        grad_query = jnp.einsum(
            "sqk,skd->sqd", grad_score, key_head, preferred_element_type=jnp.float32
        )
        grad_key = jnp.einsum(
            "sqk,sqd->skd", grad_score, query_head, preferred_element_type=jnp.float32
        )
        grad_value = jnp.einsum(
            "sqk,sqd->skd",
            probabilities.astype(jnp.bfloat16),
            grad_head,
            preferred_element_type=jnp.float32,
        )
        return (grad_query, grad_key, grad_value)

    query_grads, key_grads, value_grads = lax.map(
        attend_back,
        (query_heads, key_heads, value_heads, split_heads_major(mixed_grad, head_dim), log_norm),
    )
    key_sum, value_sum = (
        lax.psum_scatter(
            merge_heads(key_grads).astype(jnp.bfloat16), "ctx", scatter_dimension=1, tiled=True
        ).astype(jnp.float32),
        lax.psum_scatter(
            merge_heads(value_grads).astype(jnp.bfloat16), "ctx", scatter_dimension=1, tiled=True
        ).astype(jnp.float32),
    )
    query_sum = merge_heads(query_grads)
    bounds = ((0, img_member), (img_member, img_member + txt_member))
    grad_qkv_parts = []
    first_parts = []
    gain_terms = []
    for s in range(2):
        start_row, stop_row = bounds[s]
        unused, query_vjp = jax.vjp(
            lambda v, g: head_norm(v, g, QUERY_SCALE), projected[s][0], norm_gain[s, 0]
        )
        query_raw_grad, query_gain_grad = query_vjp(query_sum[:, start_row:stop_row])
        unused, key_vjp = jax.vjp(
            lambda v, g: head_norm(v, g, 1.0), projected[s][1], norm_gain[s, 1]
        )
        key_raw_grad, key_gain_grad = key_vjp(key_sum[:, start_row:stop_row])
        proj_grad = jnp.stack(
            [query_raw_grad, key_raw_grad, value_sum[:, start_row:stop_row]]
        ).astype(jnp.bfloat16)
        grad_qkv_parts.append(
            jnp.einsum("srd,csrf->cdf", first_in[s], proj_grad, preferred_element_type=jnp.float32)
        )
        first_parts.append(
            jnp.einsum("csrf,cdf->srd", proj_grad, qkv_back[s], preferred_element_type=jnp.float32)
        )
        gain_terms.append(jnp.stack([query_gain_grad, key_gain_grad]))
    first_grad = reduce_rows(first_parts[0], first_parts[1])
    input_grads = []
    mod_terms = []
    for s in range(2):
        unused, mod_vjp = jax.vjp(modulate, inputs[s], entry(s, 0), entry(s, 1))
        input_part, shift_part, scale_part = mod_vjp(first_grad[s])
        input_grads.append(mid_grad[s] + input_part)
        mod_terms.append(
            jnp.stack(
                [
                    shift_part[:, 0],
                    scale_part[:, 0],
                    gate_one[s],
                    shift_two[s],
                    scale_two[s],
                    gate_two[s],
                ],
                axis=1,
            )
        )
    mod_grad = lax.psum(jnp.stack(mod_terms).astype(jnp.bfloat16), ("ctx", "tp")).astype(
        jnp.float32
    )
    gain_grad = lax.psum(jnp.stack(gain_terms), ("shard", "ctx", "tp"))
    own_mod = lax.dynamic_slice_in_dim(
        mod_grad, lax.axis_index("tp") * local_feat, local_feat, axis=3
    ).astype(jnp.bfloat16)
    seq_count = cond_act.shape[0]
    cond_blocks = cond_act.reshape(seq_count, shard_count, ctx_count, owned_rows)
    cond_member = lax.dynamic_index_in_dim(
        cond_blocks, lax.axis_index("ctx"), axis=2, keepdims=False
    ).reshape(seq_count, shard_count * owned_rows)
    grad_mod_terms = jnp.einsum(
        "sd,tskf->tdkf", cond_member, own_mod, preferred_element_type=jnp.float32
    )
    grad_mod = lax.psum_scatter(
        grad_mod_terms.astype(jnp.bfloat16), "shard", scatter_dimension=1, tiled=True
    ).astype(jnp.float32)
    cond_part = jnp.einsum("tskf,tdkf->sd", own_mod, mod_all, preferred_element_type=jnp.float32)
    cond_total = lax.psum(cond_part, "tp")
    unused, silu_vjp = jax.vjp(jax.nn.silu, cond_float)
    grad_cond = silu_vjp(cond_total)[0]
    owned_grads = (
        lax.psum_scatter(
            jnp.stack(grad_qkv_parts), ("shard", "ctx"), scatter_dimension=2, tiled=True
        ),
        lax.psum_scatter(grad_outproj, ("shard", "ctx"), scatter_dimension=2, tiled=True),
        lax.psum_scatter(grad_up, ("shard", "ctx"), scatter_dimension=1, tiled=True),
        lax.psum_scatter(grad_down, ("shard", "ctx"), scatter_dimension=2, tiled=True),
    )
    factor = jnp.sqrt(threshold / jnp.maximum(peaks, threshold))
    columns = jnp.repeat(factor, head_dim)
    clipped = qkv_w[:, :2].astype(jnp.float32) * columns
    return (
        results[0],
        results[1],
        input_grads[0],
        input_grads[1],
        grad_cond,
        grad_mod,
        owned_grads[0],
        owned_grads[1],
        owned_grads[2],
        owned_grads[3],
        gain_grad,
        clipped,
        peaks,
    )


def solution(mesh):
    return jax.shard_map(
        local,
        mesh=mesh,
        in_specs=(
            P("shard", ("ctx", "tp"), None),
            P("shard", ("ctx", "tp"), None),
            P("shard", None),
            P("shard"),
            P(None, ("shard", "ctx"), None, "tp"),
            P(None, None, ("shard", "ctx"), "tp"),
            P(None, "tp", ("shard", "ctx")),
            P(None, ("shard", "ctx"), "tp"),
            P(None, "tp", ("shard", "ctx")),
            P(),
            P(),
            P("shard", ("ctx", "tp"), None),
            P("shard", ("ctx", "tp"), None),
        ),
        out_specs=(
            P("shard", ("ctx", "tp"), None),
            P("shard", ("ctx", "tp"), None),
            P("shard", ("ctx", "tp"), None),
            P("shard", ("ctx", "tp"), None),
            P("shard", None),
            P(None, ("shard", "ctx"), None, "tp"),
            P(None, None, ("shard", "ctx"), "tp"),
            P(None, "tp", ("shard", "ctx")),
            P(None, ("shard", "ctx"), "tp"),
            P(None, "tp", ("shard", "ctx")),
            P(),
            P(None, None, ("shard", "ctx"), "tp"),
            P("tp"),
        ),
        check_vma=False,
    )
```

profile of v0, /device:TPU:1, one launch (start us, length us, event | category | flops | bytes accessed | tf_op | source)
XLA Modules:
  0.0 3242.6 jit_solution(17155912777045053228)
XLA Ops:
  9.2 197.6 %all-gather.12.cloned.1.call-done = bf16[2,1536,6,384]{3,1,2,0:T(8,128)(2,1)} async-done(((bf16[2,192,6,384]{3,1,2,0:T(8,128)(2,1)}), bf16[2,1536,6,384]{3,1,2,0:T(8,128)(2,1)}) %all-gather.12.cloned.1.call-update) | async-done | bytes 14155792 | tf_op jit(solution)/shard_map/all_gather | solution.py:98
  233.2 81.9 %all-gather.16.cloned.1.call-done = bf16[2,3,1536,384]{3,2,1,0:T(8,128)(2,1)} async-done(((bf16[2,3,192,384]{3,2,1,0:T(8,128)(2,1)}), bf16[2,3,1536,384]{3,2,1,0:T(8,128)(2,1)}) %all-gather.16.cloned.1.call-update) | async-done | bytes 7077904 | tf_op jit(solution)/shard_map/all_gather | solution.py:90
  320.2 20.8 all-gather.14.cloned.1.call-done
  356.8 36.7 %all-gather.22.cloned.1.call-done = bf16[2,384,1536]{1,0,2:T(2,128)(2,1)} async-done(((bf16[2,384,192]{1,0,2:T(2,128)(2,1)}), bf16[2,384,1536]{1,0,2:T(2,128)(2,1)}) %all-gather.22.cloned.1.call-update) | async-done | bytes 2359312 | tf_op jit(solution)/shard_map/all_gather | solution.py:91
  410.5 41.4 %all-gather.18.cloned.1.call-done = bf16[3,1184,384]{2,1,0:T(8,128)(2,1)} async-done(((bf16[3,296,384]{2,1,0:T(8,128)(2,1)}), bf16[3,1184,384]{2,1,0:T(8,128)(2,1)}) %all-gather.18.cloned.1.call-update) | async-done | bytes 2727952 | tf_op jit(solution)/shard_map/all_gather | solution.py:122
  459.3 49.4 %all-gather.20.cloned.1.call-done = bf16[3,1184,384]{2,1,0:T(8,128)(2,1)} async-done(((bf16[3,296,384]{2,1,0:T(8,128)(2,1)}), bf16[3,1184,384]{2,1,0:T(8,128)(2,1)}) %all-gather.20.cloned.1.call-update) | async-done | bytes 2727952 | tf_op jit(solution)/shard_map/all_gather | solution.py:123
  517.7 53.4 %while.30 = (s32[]{:T(128)}, bf16[6,3,296,64]{2,3,1,0:T(8,128)(2,1)}, f32[6,3,296]{2,1,0:T(4,128)}, f32[6]{0:T(128)}, bf16[6,3,296,64]{2,3,1,0:T(8,128)(2,1)}, /...) while((s32[]{:T(128)}, ...), condition=%wide.region_12.13_spmd.clone, body=%wide.region_8.12_spmd.clone.sunk | while | flops 277630528 | bytes 13942453 | solution.py:149
  582.0 42.5 %reduce-scatter.8.cloned.1.call-done = f32[3,64,1536]{2,1,0:T(8,128)} async-done(((f32[3,256,1536]{2,1,0:T(8,128)}), f32[3,64,1536]{2,1,0:T(8,128)}) %reduce-scatter.8.cloned.1.call-update) | async-done | bytes 1179664 | tf_op jit(solution)/shard_map/reduce_scatter | solution.py:42
  636.6 127.3 %all-gather.28.cloned.1.call-done = bf16[2,1536,1536]{1,0,2:T(2,128)(2,1)} async-done(((bf16[2,1536,192]{1,0,2:T(2,128)(2,1)}), bf16[2,1536,1536]{1,0,2:T(2,128)(2,1)}) %all-gather.28.cloned.1.call-update) | async-done | bytes 9437200 | tf_op jit(solution)/shard_map/all_gather | solution.py:93
  763.8 19.1 fusion.191
  783.0 22.6 copy.359
  808.4 93.0 %all-gather.26.cloned.1.call-done = bf16[2,1536,1536]{2,1,0:T(8,128)(2,1)} async-done(((bf16[2,192,1536]{2,1,0:T(8,128)(2,1)}), bf16[2,1536,1536]{2,1,0:T(8,128)(2,1)}) %all-gather.26.cloned.1.call-update) | async-done | bytes 9437200 | tf_op jit(solution)/shard_map/all_gather | solution.py:92
  901.4 25.4 all-gather.24.cloned.1.call-done
  935.8 17.2 all-gather.30.cloned.1.call-done
  970.0 22.5 copy.364
  1020.5 21.5 reduce-scatter.12.cloned.1.call-done
  1046.7 33.2 %all-reduce.26.cloned.1.call-done = f32[3,40,1536]{2,0,1:T(4,128)} async-done(((f32[3,40,1536]{2,0,1:T(4,128)}), f32[3,40,1536]{2,0,1:T(4,128)}) %all-reduce.26.cloned.1.call-update) | async-done | bytes 737296
  1092.8 14.9 all-gather.32.cloned.1.call-done
  1110.9 73.6 %while.31 = (s32[]{:T(128)}, f32[6,3,296,64]{2,3,1,0:T(8,128)}, bf16[6,3,1184,64]{2,3,1,0:T(8,128)(2,1)}, bf16[6,3,1184,64]{2,3,1,0:T(8,128)(2,1)}, bf16[6,3,296...) while((s32[]{:T(128)}, f32[6,3,296,64]{2,3,1,0:T(8,128)}, ...), condition=%wide.region_29.30_spmd.clone, body=%wide.region_27.29_spmd.clone.sunk | while | flops 681308224 | bytes 36244180 | solution.py:265
  1237.3 161.0 %all-reduce.36.cloned.1.call-done = (bf16[3,1184,384]{2,1,0:T(8,128)(2,1)}, bf16[3,1184,384]{2,1,0:T(8,128)(2,1)}) async-done(((bf16[3,1184,384]{2,1,0:T(8,128)(2,1)}, bf16[3,1184,384]{2,1,0:T(8,128)(2,1)}), (bf16[3,1184,384]{2,1,0:T(8,128)(2,1)}, bf16[3,1184,384]{2,1,0:T(8,128)(2,1)})) %all-reduce.36.cloned.1.call-update) | async-done | bytes 5455888
  1490.8 41.6 %reduce-scatter.14.cloned.1.call-done = f32[3,64,1536]{2,1,0:T(8,128)} async-done(((f32[3,256,1536]{2,1,0:T(8,128)}), f32[3,64,1536]{2,1,0:T(8,128)}) %reduce-scatter.14.cloned.1.call-update) | async-done | bytes 1179664 | tf_op jit(solution)/shard_map/reduce_scatter | solution.py:42
  1538.1 44.8 %reduce-scatter.10.cloned.1.call-done = f32[3,64,1536]{2,1,0:T(8,128)} async-done(((f32[3,256,1536]{2,1,0:T(8,128)}), f32[3,64,1536]{2,1,0:T(8,128)}) %reduce-scatter.10.cloned.1.call-update) | async-done | bytes 1179664 | tf_op jit(solution)/shard_map/reduce_scatter | solution.py:42
  1591.3 14.6 pad_maximum_fusion.1
  1605.9 28.4 copy.329
  1634.6 45.4 %all-reduce.22.cloned.1.call-done = bf16[2,3,6,1536]{3,1,0,2:T(4,128)(2,1)} async-done(((bf16[2,3,6,1536]{3,1,0,2:T(4,128)(2,1)}), bf16[2,3,6,1536]{3,1,0,2:T(4,128)(2,1)}) %all-reduce.22.cloned.1.call-update) | async-done | bytes 110608 | tf_op jit(solution)/shard_map/psum | solution.py:322
  1747.9 21.5 copy.322
  1786.9 20.1 pmax.7
  1808.7 46.2 %psum.23 = f32[2,2,64]{2,1,0:T(2,128)} all-reduce(f32[2,2,64]{2,1,0:T(2,128)S(1)} %pad_maximum_fusion.13), channel_id=1, replica_groups=mesh['shard'=2,'ctx'=4,'tp'=4] {'shard','ctx','tp'}, use_global_device_ids=true, to_apply=%region_69.70 | all-reduce | flops 256 | bytes 2048 | tf_op jit(solution)/shard_map/psum | solution.py:325
  1854.9 399.2 %all-reduce.30.cloned.1.call-done = f32[2,1536,1536]{1,0,2:T(2,128)} async-done(((f32[2,1536,1536]{1,0,2:T(2,128)}), f32[2,1536,1536]{1,0,2:T(2,128)}) %all-reduce.30.cloned.1.call-update) | async-done | bytes 18874384
  2258.4 92.0 %all-reduce.28.cloned.1.call-done = bf16[2,384,6,384]{3,0,2,1:T(2,128)(2,1)} async-done(((bf16[2,384,6,384]{3,0,2,1:T(2,128)(2,1)}), bf16[2,384,6,384]{3,0,2,1:T(2,128)(2,1)}) %all-reduce.28.cloned.1.call-update) | async-done | bytes 3538960
  2355.2 566.9 %all-reduce.32.cloned.1.call-done = (f32[2,3,1536,384]{3,0,1,2:T(2,128)}, f32[2,384,1536]{1,0,2:T(2,128)}) async-done(((f32[2,3,1536,384]{3,0,1,2:T(2,128)}, f32[2,384,1536]{1,0,2:T(2,128)}), (f32[2,3,1536,384]{3,0,1,2:T(2,128)}, f32[2,384,1536]{1,0,2:T(2,128)})) %all-reduce.32.cloned.1.call-update) | async-done | bytes 18874384
  2927.7 307.6 %reduce-scatter.16.cloned.1.call-done = f32[2,192,1536]{2,1,0:T(8,128)} async-done(((f32[2,1536,1536]{2,1,0:T(8,128)}), f32[2,192,1536]{2,1,0:T(8,128)}) %reduce-scatter.16.cloned.1.call-update) | async-done | bytes 2359312 | tf_op jit(solution)/shard_map/reduce_scatter | solution.py:349
  (674 shorter events, 566.3 us)
Async XLA Ops:
  7.2 199.6 %copy-start.108 = (bf16[3,1536]{1,0:T(4,128)(2,1)S(1)}, bf16[3,1536]{1,0:T(4,128)(2,1)}, u32[]{:S(2)}) copy-start(bf16[3,1536]{1,0:T(4,128)(2,1)} %param.19) | copy-start | bytes 27652
  7.2 199.6 %all-gather.12.cloned.1.call-start = ((), (), s32[]{:S(2)}) async-start(), calls=%async_computation.5 | async-start | bytes 15925248 | tf_op jit(solution)/shard_map/all_gather | solution.py:98
  7.9 307.2 %all-gather.16.cloned.1.call-start = ((), (), s32[]{:S(2)}) async-start(), calls=%async_computation.7 | async-start | bytes 7962624 | tf_op jit(solution)/shard_map/all_gather | solution.py:90
  8.7 332.3 %all-gather.14.cloned.1.call-start = ((), (), s32[]{:S(2)}) async-start(), calls=%async_computation.6 | async-start | bytes 2949120 | tf_op jit(solution)/shard_map/all_gather | solution.py:35
  8.9 212.8 %copy-start.98 = (f32[3,64]{1,0:T(4,128)}, f32[3,64]{1,0:T(4,128)S(1)}, u32[]{:S(2)}) copy-start(f32[3,64]{1,0:T(4,128)S(1)} %broadcast_multiply_fusion.3) | copy-start | bytes 2308
  9.2 197.6 %copy-start.121 = (f32[3,64]{1,0:T(4,128)}, f32[3,64]{1,0:T(4,128)S(1)}, u32[]{:S(2)}) copy-start(f32[3,64]{1,0:T(4,128)S(1)} %fusion.97) | copy-start | bytes 2308
  9.2 212.5 %copy-start.117 = (f32[3,64]{1,0:T(4,128)}, f32[3,64]{1,0:T(4,128)S(1)}, u32[]{:S(2)}) copy-start(f32[3,64]{1,0:T(4,128)S(1)} %fusion.177) | copy-start | bytes 2308
  223.0 170.4 %all-gather.22.cloned.1.call-start = ((), (), s32[]{:S(2)}) async-start(), calls=%async_computation.10 | async-start | bytes 2654208 | tf_op jit(solution)/shard_map/all_gather | solution.py:91
  224.1 227.7 %all-gather.18.cloned.1.call-start = ((), (), s32[]{:S(2)}) async-start(), calls=%async_computation.8 | async-start | bytes 3409920 | tf_op jit(solution)/shard_map/all_gather | solution.py:122
  225.0 125.9 %copy-start.118 = (f32[384]{0:T(512)}, f32[384]{0:T(512)S(1)}, u32[]{:S(2)}) copy-start(f32[384]{0:T(512)S(1)} %mul.904) | copy-start | bytes 4612
  353.8 154.8 %all-gather.20.cloned.1.call-start = ((), (), s32[]{:S(2)}) async-start(), calls=%async_computation.9 | async-start | bytes 3409920 | tf_op jit(solution)/shard_map/all_gather | solution.py:123
  356.2 268.3 %reduce-scatter.8.cloned.1.call-start = ((), (), s32[]{:S(2)}) async-start(), calls=%async_computation.11 | async-start | bytes 5898240 | tf_op jit(solution)/shard_map/reduce_scatter | solution.py:42
  577.7 186.1 %all-gather.28.cloned.1.call-start = ((), (), s32[]{:S(2)}) async-start(), calls=%async_computation.14 | async-start | bytes 10616832 | tf_op jit(solution)/shard_map/all_gather | solution.py:93
  581.2 320.3 %all-gather.26.cloned.1.call-start = ((), (), s32[]{:S(2)}) async-start(), calls=%async_computation.13 | async-start | bytes 10616832 | tf_op jit(solution)/shard_map/all_gather | solution.py:92
  581.9 344.9 %all-gather.24.cloned.1.call-start = ((), (), s32[]{:S(2)}) async-start(), calls=%async_computation.12 | async-start | bytes 2949120 | tf_op jit(solution)/shard_map/all_gather | solution.py:35
  629.4 323.6 %all-gather.30.cloned.1.call-start = ((), (), s32[]{:S(2)}) async-start(), calls=%async_computation.16 | async-start | bytes 2949120 | tf_op jit(solution)/shard_map/all_gather | solution.py:35
  631.5 368.2 %all-reduce.24.cloned.1.call-start = ((), (), s32[]{:S(2)}) async-start(), calls=%async_computation.22 | async-start | bytes 1966080
  808.4 233.6 %reduce-scatter.12.cloned.1.call-start = ((), (), s32[]{:S(2)}) async-start(), calls=%async_computation.17 | async-start | bytes 5898240 | tf_op jit(solution)/shard_map/reduce_scatter | solution.py:42
  968.1 111.8 %all-reduce.26.cloned.1.call-start = ((), (), s32[]{:S(2)}) async-start(), calls=%async_computation.23 | async-start | bytes 1966080
  1020.2 87.5 %all-gather.32.cloned.1.call-start = ((), (), s32[]{:S(2)}) async-start(), calls=%async_computation.18 | async-start | bytes 2949120 | tf_op jit(solution)/shard_map/all_gather | solution.py:35
  1046.6 351.7 %all-reduce.36.cloned.1.call-start = ((), (), s32[]{:S(2)}) async-start(), calls=%async_computation.28 | async-start | bytes 10911744
  1202.7 279.3 %all-reduce.34.cloned.1.call-start = ((), (), s32[]{:S(2)}) async-start(), calls=%async_computation.27 | async-start | bytes 3932160
  1227.3 172.2 %copy-start.4 = (f32[3,256,384]{2,1,0:T(8,128)S(1)}, f32[3,256,384]{2,1,0:T(8,128)}, u32[]{:S(2)}) copy-start(f32[3,256,384]{2,1,0:T(8,128)} %copy-done.3) | copy-start | bytes 3538948
  1433.7 98.7 %reduce-scatter.14.cloned.1.call-start = ((), (), s32[]{:S(2)}) async-start(), calls=%async_computation.19 | async-start | bytes 5898240 | tf_op jit(solution)/shard_map/reduce_scatter | solution.py:42
  1447.5 135.4 %reduce-scatter.10.cloned.1.call-start = ((), (), s32[]{:S(2)}) async-start(), calls=%async_computation.15 | async-start | bytes 5898240 | tf_op jit(solution)/shard_map/reduce_scatter | solution.py:42
  1457.8 222.2 %all-reduce.22.cloned.1.call-start = ((), (), s32[]{:S(2)}) async-start(), calls=%async_computation.20 | async-start | bytes 294912 | tf_op jit(solution)/shard_map/psum | solution.py:322
  1487.2 95.7 %copy-start.21 = (bf16[3,64,1536]{2,1,0:T(8,128)(2,1)S(1)}, bf16[3,64,1536]{2,1,0:T(8,128)(2,1)}, u32[]{:S(2)}) copy-start(bf16[3,64,1536]{2,1,0:T(8,128)(2,1)} %param.28) | copy-start | bytes 1769476
  1591.3 662.9 %all-reduce.30.cloned.1.call-start = ((), (), s32[]{:S(2)}) async-start(), calls=%async_computation.25 | async-start | bytes 37748736
  1634.3 716.1 %all-reduce.28.cloned.1.call-start = ((), (), s32[]{:S(2)}) async-start(), calls=%async_computation.24 | async-start | bytes 7077888
  1710.6 1211.5 %all-reduce.32.cloned.1.call-start = ((), (), s32[]{:S(2)}) async-start(), calls=%async_computation.26 | async-start | bytes 37748736
  1769.5 1465.8 %reduce-scatter.16.cloned.1.call-start = ((), (), s32[]{:S(2)}) async-start(), calls=%async_computation.21 | async-start | bytes 21233664 | tf_op jit(solution)/shard_map/reduce_scatter | solution.py:349
  1807.0 449.6 %copy-start.146 = (f32[6]{0:T(128)}, f32[6]{0:T(128)S(1)}, u32[]{:S(2)}) copy-start(f32[6]{0:T(128)S(1)} %pmax.7) | copy-start | bytes 76
  (144 other events, 1977.5 us)
Sparse Core Ops, SparseCore 0:
  10.1 196.6 all-gather.11
  209.0 106.1 all-gather.15
  317.2 23.6 all-gather.13
  343.5 49.9 all-gather.21
  395.5 56.3 all-gather.17
  453.3 55.2 all-gather.19
  577.8 46.5 reduce-scatter.7
  627.1 136.6 all-gather.27
  766.0 135.4 all-gather.25
  903.4 23.3 all-gather.23
  928.9 24.0 all-gather.29
  955.9 34.4 all-reduce.23
  992.9 48.9 reduce-scatter.11
  1044.8 35.0 all-reduce.25
  1081.9 25.7 all-gather.31
  1202.8 195.4 all-reduce.35
  1433.8 48.1 all-reduce.33
  1484.4 47.9 reduce-scatter.13
  1535.0 47.8 reduce-scatter.9
  1591.4 88.6 all-reduce.21
  1684.1 569.9 all-reduce.29
  2257.0 93.4 all-reduce.27
  2354.7 567.4 all-reduce.31
  2926.4 308.7 reduce-scatter.15
where the time goes:
time: 3260 us; the launch traced here: 3240 us
  waiting for transfers between devices  2470 us (76%)
  local copies, waits for them, and re-layouts  293 us (9%)
  matrix products  216 us (7%)
  other arithmetic  127 us (4%)
  blocking collectives  114 us (3%)
    unnamed x31, waiting for transfers between devices  1260 us
    reduce_scatter x1, waiting for transfers between devices, local(): lax.psum_scatter(grad_up, ('shard', 'ctx'), scatter_dimension=1, tiled=True)  308 us
    all_gather x1, waiting for transfers between devices, local(): mod_all = lax.all_gather(mod_w, ('shard', 'ctx'), axis=1, tiled=True)  198 us
    reduce_scatter x4, waiting for transfers between devices, reduce_rows(): lax.psum_scatter(first, 'tp', scatter_dimension=1, tiled=True)  150 us
    all_gather x1, waiting for transfers between devices, local(): lax.all_gather(down_w, ('shard', 'ctx'), axis=2, tiled=True)  127 us
    unnamed x337, local copies, waits for them, and re-layouts  105 us
    all_gather x1, waiting for transfers between devices, local(): lax.all_gather(up_w, ('shard', 'ctx'), axis=1, tiled=True)  93 us
    all_gather x1, waiting for transfers between devices, local(): lax.all_gather(qkv_w, ('shard', 'ctx'), axis=2, tiled=True)  81.9 us
  transfers between devices with their start and end apart: 24, of which 23 were waited for; matrix products, arithmetic and copies ran while one was open for 13% of the time, Pallas kernels for 0%

commit v1 on v0

v1 whole, which is shorter than its diff:
```python
import functools

import jax
import jax.numpy as jnp
from jax import lax
from jax.experimental import pallas as pl
from jax.experimental.pallas import tpu as pltpu
from jax.sharding import Mesh, PartitionSpec as P

EPS = 1e-06
QUERY_SCALE = 0.125
BF16 = jnp.bfloat16
F32 = jnp.float32
MASKED = -1e30


def layer_norm(values):
    center = values - jnp.mean(values, axis=-1, keepdims=True)
    spread = jnp.mean(center * center, axis=-1, keepdims=True)
    return center * lax.rsqrt(spread + EPS)


def modulate(values, shift, scale):
    return layer_norm(values) * (1.0 + scale) + shift


def gelu_tanh(values):
    return jax.nn.gelu(values, approximate=True)


def trade(values, axis):
    return lax.ppermute(values, axis, [(0, 1), (1, 0)])


def cross(values):
    return lax.ppermute(values, ("l", "c"), [(0, 0), (1, 2), (2, 1), (3, 3)])


def feature_order(width, shard_count):
    place = jnp.arange(width, dtype=jnp.int32)
    block = width // (shard_count * 4)
    inner = place % block
    h = (place // block) % 2 ^ lax.axis_index("h")
    s = (place // (2 * block)) % shard_count
    if shard_count == 2:
        s = s ^ lax.axis_index("s")
    low = place // (2 * block * shard_count) ^ lax.axis_index("c")
    return ((s * 2 + h) * 2 + low) * block + inner


def one_hot(source):
    width = source.shape[0]
    rows = lax.broadcasted_iota(jnp.int32, (width, width), 0)
    return (rows == source[None, :]).astype(BF16)


def permute_exact(values, matrix, dims):
    high = lax.reduce_precision(values, 8, 7)
    rest = values - high
    middle = lax.reduce_precision(rest, 8, 7)
    low = rest - middle
    parts = [
        lax.dot_general(part.astype(BF16), matrix, (dims, ((), ())), preferred_element_type=F32)
        for part in (high, middle, low)
    ]
    return parts[0] + (parts[1] + parts[2])


def gather_weight(shard, shard_count):
    own = cross(shard)
    pair = jnp.concatenate([own, trade(own, "h")], axis=1)
    if shard_count == 2:
        near = jnp.concatenate([pair, trade(pair, "s")], axis=1)
    else:
        near = lax.all_gather(pair, "s", axis=1, tiled=True)
    return near, trade(near, "c")


def scatter_grad(near, far, shard_count):
    total = near + trade(far, "c").astype(F32)
    half = total.shape[1] // 2
    if shard_count == 2:
        moved = trade(total[:, half:].astype(BF16), "s")
        total = total[:, :half] + moved.astype(F32)
    else:
        total = lax.psum_scatter(total, "s", scatter_dimension=1, tiled=True)
    half = total.shape[1] // 2
    moved = trade(total[:, half:].astype(BF16), "h")
    total = total[:, :half] + moved.astype(F32)
    return cross(total.astype(BF16)).astype(F32)


def gather_rows(image, text):
    half = image.shape[1] // 2
    rows = image.shape[0]
    both = jnp.concatenate([image, text], axis=0)
    first, second = both[:, :half], both[:, half:]
    first_pair = jnp.stack([first, trade(first, "y")])
    second_pair = jnp.stack([second, trade(second, "l")])
    first_far = trade(first_pair, "l")
    second_far = trade(second_pair, "y")
    near = [first_pair[0], first_pair[1], first_far[1], first_far[0]]
    far = [second_pair[0], second_far[0], second_far[1], second_pair[1]]
    return [
        (
            jnp.concatenate([block[:rows] for block in blocks], axis=0),
            jnp.concatenate([block[rows:] for block in blocks], axis=0),
        )
        for blocks in (near, far)
    ]


def reduce_rows(near, far):
    def blocks(pair, which):
        image, text = pair
        rows_i, rows_t = image.shape[0] // 4, text.shape[0] // 4
        return jnp.stack(
            [
                jnp.concatenate(
                    [image[k * rows_i : (k + 1) * rows_i], text[k * rows_t : (k + 1) * rows_t]]
                )
                for k in which
            ]
        )

    rows_i = near[0].shape[0] // 4
    first_in = trade(blocks(near, (2, 3)).astype(BF16), "l").astype(F32)
    second_in = trade(blocks(far, (1, 2)).astype(BF16), "y").astype(F32)
    first_keep = blocks(near, (0, 1))
    second_keep = blocks(far, (0, 3))
    first_last = trade((first_keep[1] + first_in[0]).astype(BF16), "y")
    second_last = trade((second_keep[1] + second_in[1]).astype(BF16), "l")
    first = first_keep[0] + first_in[1] + first_last.astype(F32)
    second = second_keep[0] + second_in[0] + second_last.astype(F32)
    total = jnp.concatenate([first, second], axis=1)
    return total[:rows_i], total[rows_i:]


def head_mean(values, head_dim):
    width = values.shape[-1]
    rows = lax.broadcasted_iota(jnp.int32, (width, width), 0) // head_dim
    cols = lax.broadcasted_iota(jnp.int32, (width, width), 1) // head_dim
    spread = jnp.where(rows == cols, 1.0 / head_dim, 0.0).astype(BF16)
    high = lax.reduce_precision(values, 8, 7)
    low = (values - high).astype(BF16)
    return jnp.dot(high.astype(BF16), spread, preferred_element_type=F32) + jnp.dot(
        low, spread, preferred_element_type=F32
    )


def two_sided(pair, weights, form):
    return jnp.einsum(form, pair[0], weights[0], preferred_element_type=F32) + jnp.einsum(
        form, pair[1], weights[1], preferred_element_type=F32
    )


def sequence_rows(ref, seq, sizes):
    img, txt, seqs = sizes
    parts = [ref[pl.ds(pl.multiple_of((b * seqs + seq) * img, 16), img), :] for b in range(4)]
    base = 4 * seqs * img
    parts += [
        ref[pl.ds(pl.multiple_of(base + (b * seqs + seq) * txt, 16), txt), :] for b in range(4)
    ]
    return jnp.concatenate(parts, axis=0)


def store_rows(ref, seq, sizes, value):
    img, txt, seqs = sizes
    base = 4 * seqs * img
    for b in range(4):
        ref[pl.ds(pl.multiple_of((b * seqs + seq) * img, 16), img), :] = value[
            b * img : (b + 1) * img
        ]
        ref[pl.ds(pl.multiple_of(base + (b * seqs + seq) * txt, 16), txt), :] = value[
            4 * img + b * txt : 4 * img + (b + 1) * txt
        ]


def both_heads(rows, head_dim):
    lane = lax.broadcasted_iota(jnp.int32, rows.shape, 1)
    zero = jnp.zeros_like(rows)
    return jnp.concatenate(
        [jnp.where(lane < head_dim, rows, zero), jnp.where(lane >= head_dim, rows, zero)], axis=0
    )


def join_heads(stacked, head_dim):
    count = stacked.shape[0] // 2
    lane = lax.broadcasted_iota(jnp.int32, (count, stacked.shape[1]), 1)
    return jnp.where(lane < head_dim, stacked[:count], stacked[count:])


NT = (((1,), (1,)), ((), ()))
TN = (((0,), (0,)), ((), ()))
NN = (((1,), (0,)), ((), ()))


def attend_kernel(sizes, head_dim, *refs):
    q_ref, k_refs, v_refs = refs[0], refs[1:5], refs[5:9]
    bias_ref, out_ref, norm_ref, peak_ref = refs[9:]
    seq = pl.program_id(1)
    query = both_heads(sequence_rows(q_ref, seq, sizes), head_dim)
    keys = jnp.concatenate([sequence_rows(r, seq, sizes) for r in k_refs], axis=0)
    values = jnp.concatenate([sequence_rows(r, seq, sizes) for r in v_refs], axis=0)
    scores = lax.dot_general(keys, query, NT, preferred_element_type=F32) + bias_ref[0]
    highest = jnp.max(scores, axis=0, keepdims=True)
    weights = jnp.exp(scores - highest)
    total = jnp.sum(weights, axis=0, keepdims=True)
    mixed = lax.dot_general(values, weights.astype(BF16), TN, preferred_element_type=F32)
    mixed = jnp.transpose(mixed * (1.0 / total))
    store_rows(out_ref, seq, sizes, join_heads(mixed, head_dim).astype(BF16))
    norm_ref[0] = highest + jnp.log(total)
    peak_ref[0] = highest


def attend_back_kernel(sizes, head_dim, *refs):
    q_ref, k_refs, v_refs = refs[0], refs[1:5], refs[5:9]
    bias_ref, norm_ref, grad_ref = refs[9:12]
    gq_ref, gk_refs, gv_refs = refs[12], refs[13:17], refs[17:21]
    seq = pl.program_id(1)
    query = both_heads(sequence_rows(q_ref, seq, sizes), head_dim)
    grad = both_heads(sequence_rows(grad_ref, seq, sizes), head_dim)
    keys = jnp.concatenate([sequence_rows(r, seq, sizes) for r in k_refs], axis=0)
    values = jnp.concatenate([sequence_rows(r, seq, sizes) for r in v_refs], axis=0)
    scores = lax.dot_general(keys, query, NT, preferred_element_type=F32) + bias_ref[0]
    probs = jnp.exp(scores - norm_ref[0])
    grad_probs = lax.dot_general(values, grad, NT, preferred_element_type=F32)
    inner = jnp.sum(probs * grad_probs, axis=0, keepdims=True)
    grad_scores = (probs * (grad_probs - inner)).astype(BF16)
    grad_values = lax.dot_general(probs.astype(BF16), grad, NN, preferred_element_type=F32)
    grad_keys = lax.dot_general(grad_scores, query, NN, preferred_element_type=F32)
    grad_query = lax.dot_general(keys, grad_scores, TN, preferred_element_type=F32)
    store_rows(gq_ref, seq, sizes, join_heads(jnp.transpose(grad_query), head_dim))
    count = keys.shape[0] // 4
    for j in range(4):
        store_rows(gk_refs[j], seq, sizes, grad_keys[j * count : (j + 1) * count].astype(BF16))
        store_rows(gv_refs[j], seq, sizes, grad_values[j * count : (j + 1) * count].astype(BF16))


def attention_specs(rows, seqs, keys, pair_count):
    q_spec = pl.BlockSpec((rows, 128), lambda p, s: (0, p))
    k_specs = [pl.BlockSpec((rows, 128), lambda p, s: (0, p)) for _ in range(4)]
    v_specs = [pl.BlockSpec((rows, 128), lambda p, s: (0, pair_count + p)) for _ in range(4)]
    bias_spec = pl.BlockSpec((1, keys, 1), lambda p, s: (s, 0, 0))
    return q_spec, k_specs, v_specs, bias_spec


def attend(queries, key_values, bias, sizes, head_dim):
    rows, width = queries.shape
    seqs, keys = bias.shape[0], bias.shape[1]
    pairs = width // 128
    lanes = 2 * (keys // 4)
    q_spec, k_specs, v_specs, bias_spec = attention_specs(rows, seqs, keys, pairs)
    line = pl.BlockSpec((1, 1, lanes), lambda p, s: (p * seqs + s, 0, 0))
    return pl.pallas_call(
        functools.partial(attend_kernel, sizes, head_dim),
        grid=(pairs, seqs),
        in_specs=[q_spec, *k_specs, *v_specs, bias_spec],
        out_specs=[q_spec, line, line],
        out_shape=[
            jax.ShapeDtypeStruct((rows, width), BF16),
            jax.ShapeDtypeStruct((pairs * seqs, 1, lanes), F32),
            jax.ShapeDtypeStruct((pairs * seqs, 1, lanes), F32),
        ],
        cost_estimate=pl.CostEstimate(
            flops=pairs * seqs * keys * lanes * 128 * 4,
            bytes_accessed=rows * width * 20,
            transcendentals=pairs * seqs * keys * lanes,
        ),
        compiler_params=pltpu.CompilerParams(vmem_limit_bytes=60 << 20),
    )(queries, *key_values, *key_values, bias)


def attend_back(queries, key_values, bias, norms, grads, sizes, head_dim):
    rows, width = queries.shape
    seqs, keys = bias.shape[0], bias.shape[1]
    pairs = width // 128
    lanes = 2 * (keys // 4)
    q_spec, k_specs, v_specs, bias_spec = attention_specs(rows, seqs, keys, pairs)
    line = pl.BlockSpec((1, 1, lanes), lambda p, s: (p * seqs + s, 0, 0))
    out = pl.pallas_call(
        functools.partial(attend_back_kernel, sizes, head_dim),
        grid=(pairs, seqs),
        in_specs=[q_spec, *k_specs, *v_specs, bias_spec, line, q_spec],
        out_specs=[q_spec] * 9,
        out_shape=[jax.ShapeDtypeStruct((rows, width), F32)]
        + [jax.ShapeDtypeStruct((rows, width), BF16)] * 8,
        cost_estimate=pl.CostEstimate(
            flops=pairs * seqs * keys * lanes * 128 * 10,
            bytes_accessed=rows * width * 40,
            transcendentals=pairs * seqs * keys * lanes,
        ),
        compiler_params=pltpu.CompilerParams(vmem_limit_bytes=60 << 20),
    )(queries, *key_values, *key_values, bias, norms, grads)
    return out[0], out[1:5], out[5:9]


def local(
    x_img,
    x_txt,
    cond,
    lengths,
    mod_w,
    qkv_w,
    o_w,
    up_w,
    down_w,
    norm_gain,
    threshold,
    cot_img,
    cot_txt,
):
    shard_count = lax.axis_size("s")
    head_dim = norm_gain.shape[2]
    seqs, img_rows, width = x_img.shape
    txt_real = x_txt.shape[1]
    txt_rows = -(-txt_real // 16) * 16
    sizes = (img_rows, txt_rows, seqs)
    shapes = ((seqs, img_rows, width), (seqs, txt_rows, width))
    feat = mod_w.shape[3]
    block = mod_w.shape[1]
    heads = qkv_w.shape[3] // head_dim
    own = {name: lax.axis_index(name) for name in ("s", "h", "l", "y", "c")}

    weights = {
        "qkv": gather_weight(qkv_w.reshape(6, block, -1), shard_count),
        "o": gather_weight(jnp.swapaxes(o_w, 1, 2), shard_count),
        "up": gather_weight(up_w, shard_count),
        "down": gather_weight(jnp.swapaxes(down_w, 1, 2), shard_count),
    }

    source = feature_order(width, shard_count)
    order = one_hot(source)

    def pad_text(values):
        return jnp.pad(values, ((0, 0), (0, txt_rows - txt_real), (0, 0)))

    def arrange(image, text):
        both = jnp.concatenate(
            [image.reshape(-1, width), pad_text(text).reshape(-1, width)], axis=0
        )
        moved = jnp.dot(both, order, preferred_element_type=F32)
        count = seqs * img_rows
        return [moved[:count].reshape(shapes[0]), moved[count:].reshape(shapes[1])]

    inputs = arrange(x_img, x_txt)
    grad_out = arrange(cot_img, cot_txt)

    cond_float = cond.astype(F32)
    cond_act = jax.nn.silu(cond_float).astype(BF16)
    cond_all = lax.all_gather(cond_act, "s", axis=0, tiled=True)
    cond_rows = lax.dynamic_index_in_dim(
        cond_all.reshape(cond_all.shape[0], -1, block),
        (own["s"] * 2 + own["h"]) * 2 + own["l"],
        axis=1,
        keepdims=False,
    )
    mod_part = jnp.einsum("sd,tdkf->stkf", cond_rows, mod_w, preferred_element_type=F32)
    if shard_count == 2:
        mine = lax.dynamic_slice_in_dim(mod_part, own["s"] * seqs, seqs, axis=0)
        other = lax.dynamic_slice_in_dim(mod_part, (1 - own["s"]) * seqs, seqs, axis=0)
        mod_sum = mine + trade(other, "s")
    else:
        mod_sum = lax.psum_scatter(mod_part, "s", scatter_dimension=0, tiled=True)
    mod_sum = mod_sum + trade(mod_sum, "h")
    mod_sum = mod_sum + trade(mod_sum, "l")
    mod_full = lax.all_gather(mod_sum, ("y", "c"), axis=3, tiled=True)
    modulation = permute_exact(mod_full.reshape(-1, width), order, ((1,), (0,))).reshape(
        seqs, 2, 6, width
    )

    def entry(stream, index):
        return modulation[:, stream, index][:, None, :]

    def flat(pair):
        return [v.reshape(-1, width) for v in pair]

    def unflat(pair):
        return [v.reshape(shape) for v, shape in zip(pair, shapes)]

    first_low = [modulate(inputs[s], entry(s, 0), entry(s, 1)).astype(BF16) for s in range(2)]
    first_near, first_far = gather_rows(*flat(first_low))
    qkv_near, qkv_far = weights["qkv"]
    projected = []
    for s in range(2):
        pair = (first_near[s], first_far[s])
        projected.append(
            [
                two_sided(pair, (qkv_near[3 * s + c], qkv_far[3 * s + c]), "rd,df->rf")
                for c in range(3)
            ]
        )
    scales = (QUERY_SCALE, 1.0)
    roots = [
        [lax.rsqrt(head_mean(projected[s][c] * projected[s][c], head_dim) + EPS) for c in range(2)]
        for s in range(2)
    ]
    gains = [[jnp.tile(norm_gain[s, c], heads) * scales[c] for c in range(2)] for s in range(2)]
    normed = [
        [(projected[s][c] * roots[s][c] * gains[s][c]).astype(BF16) for c in range(2)]
        for s in range(2)
    ]
    queries = jnp.concatenate([normed[0][0], normed[1][0]], axis=0)
    own_kv = jnp.concatenate(
        [
            jnp.concatenate([normed[s][1], projected[s][2].astype(BF16)], axis=1)
            for s in range(2)
        ],
        axis=0,
    )
    h_kv = trade(own_kv, "h")
    key_values = [own_kv, trade(own_kv, "c"), h_kv, trade(h_kv, "c")]

    text_bias = []
    for jh, jc in ((0, 0), (0, 1), (1, 0), (1, 1)):
        member = [jnp.zeros((seqs, 4 * img_rows), F32)]
        for jy, jl in ((0, 0), (1, 0), (1, 1), (0, 1)):
            ctx_at = (own["h"] ^ jh) * 2 + (own["l"] ^ jl)
            tp_at = (own["y"] ^ jy) * 2 + (own["c"] ^ jc)
            row = jnp.arange(txt_rows, dtype=jnp.int32)
            slot = (ctx_at * 4 + tp_at) * txt_real + row
            allowed = (row < txt_real)[None, :] & (slot[None, :] < lengths[:, None])
            member.append(jnp.where(allowed, 0.0, MASKED))
        text_bias.append(jnp.concatenate(member, axis=1))
    bias = jnp.concatenate(text_bias, axis=1)[:, :, None]

    attended, log_norm, highest = attend(queries, key_values, bias, sizes, head_dim)
    count_i = 4 * seqs * img_rows
    attended_s = (attended[:count_i], attended[count_i:])
    o_near, o_far = weights["o"]
    attn_out = unflat(
        reduce_rows(
            *[
                [
                    jnp.einsum("rf,df->rd", attended_s[s], w[s], preferred_element_type=F32)
                    for s in range(2)
                ]
                for w in (o_near, o_far)
            ]
        )
    )
    mid = [inputs[s] + entry(s, 2) * attn_out[s] for s in range(2)]
    second_low = [modulate(mid[s], entry(s, 3), entry(s, 4)).astype(BF16) for s in range(2)]
    second_near, second_far = gather_rows(*flat(second_low))
    up_near, up_far = weights["up"]
    down_near, down_far = weights["down"]
    hidden_pre = [
        two_sided((second_near[s], second_far[s]), (up_near[s], up_far[s]), "rd,df->rf")
        for s in range(2)
    ]
    hidden_low = [gelu_tanh(hidden_pre[s]).astype(BF16) for s in range(2)]

    mlp_grad_low = [(grad_out[s] * entry(s, 5)).astype(BF16) for s in range(2)]
    mlp_near, mlp_far = gather_rows(*flat(mlp_grad_low))
    pre_grad = []
    for s in range(2):
        hidden_back = two_sided((mlp_near[s], mlp_far[s]), (down_near[s], down_far[s]), "rd,df->rf")
        unused, gelu_vjp = jax.vjp(gelu_tanh, hidden_pre[s])
        pre_grad.append(gelu_vjp(hidden_back)[0].astype(BF16))
    second_grad = unflat(
        reduce_rows(
            *[
                [
                    jnp.einsum("rf,df->rd", pre_grad[s], w[s], preferred_element_type=F32)
                    for s in range(2)
                ]
                for w in (up_near, up_far)
            ]
        )
    )
    mlp_out = unflat(
        reduce_rows(
            *[
                [
                    jnp.einsum("rf,df->rd", hidden_low[s], w[s], preferred_element_type=F32)
                    for s in range(2)
                ]
                for w in (down_near, down_far)
            ]
        )
    )
    results = [(mid[s] + entry(s, 5) * mlp_out[s]).astype(BF16) for s in range(2)]
    gate_two = [jnp.sum(grad_out[s] * mlp_out[s], axis=1) for s in range(2)]

    def weight_grad(left_near, left_far, right):
        near, far = [
            jnp.stack(
                [
                    jnp.einsum("rd,rf->df", left[s], right[s], preferred_element_type=F32)
                    for s in range(2)
                ]
            )
            for left in (left_near, left_far)
        ]
        return scatter_grad(near, far.astype(BF16), shard_count)

    grad_down = weight_grad(mlp_near, mlp_far, hidden_low)
    grad_up = weight_grad(second_near, second_far, pre_grad)

    mid_grad = []
    shift_two = []
    scale_two = []
    for s in range(2):
        unused, mod_vjp = jax.vjp(modulate, mid[s], entry(s, 3), entry(s, 4))
        mid_part, shift_part, scale_part = mod_vjp(second_grad[s])
        mid_grad.append(grad_out[s] + mid_part)
        shift_two.append(shift_part[:, 0])
        scale_two.append(scale_part[:, 0])
    attn_grad_low = [(mid_grad[s] * entry(s, 2)).astype(BF16) for s in range(2)]
    gate_one = [jnp.sum(mid_grad[s] * attn_out[s], axis=1) for s in range(2)]
    attn_near, attn_far = gather_rows(*flat(attn_grad_low))
    grad_o = weight_grad(attn_near, attn_far, attended_s)
    mixed_grad = jnp.concatenate(
        [
            two_sided((attn_near[s], attn_far[s]), (o_near[s], o_far[s]), "rd,df->rf")
            for s in range(2)
        ],
        axis=0,
    ).astype(BF16)
    query_sum, key_grads, value_grads = attend_back(
        queries, key_values, bias, log_norm, mixed_grad, sizes, head_dim
    )

    kv_grads = [jnp.concatenate([key_grads[j], value_grads[j]], axis=1) for j in range(4)]
    own_sum = kv_grads[0].astype(F32) + trade(kv_grads[1], "c").astype(F32)
    h_sum = kv_grads[2].astype(F32) + trade(kv_grads[3], "c").astype(F32)
    kv_sum = own_sum + trade(h_sum.astype(BF16), "h").astype(F32)
    inner_width = queries.shape[1]
    key_sum, value_sum = kv_sum[:, :inner_width], kv_sum[:, inner_width:]

    bounds = ((0, count_i), (count_i, queries.shape[0]))
    qkv_near_parts, qkv_far_parts = [], []
    first_near_parts, first_far_parts = [], []
    gain_terms = []
    for s in range(2):
        start, stop = bounds[s]
        grads = []
        gain_pair = []
        for c, grad_sum in ((0, query_sum), (1, key_sum)):
            grad = grad_sum[start:stop]
            unit = projected[s][c] * roots[s][c]
            gain_pair.append(
                jnp.sum(jnp.sum(grad * unit, axis=0).reshape(heads, head_dim), axis=0) * scales[c]
            )
            scaled = grad * gains[s][c]
            grads.append(roots[s][c] * (scaled - unit * head_mean(scaled * unit, head_dim)))
        grads.append(value_sum[start:stop])
        low = [g.astype(BF16) for g in grads]
        gain_terms.append(jnp.stack(gain_pair))
        for c in range(3):
            for parts, left in ((qkv_near_parts, first_near), (qkv_far_parts, first_far)):
                parts.append(jnp.einsum("rd,rf->df", left[s], low[c], preferred_element_type=F32))
        for parts, w in ((first_near_parts, qkv_near), (first_far_parts, qkv_far)):
            parts.append(
                sum(
                    jnp.einsum("rf,df->rd", low[c], w[3 * s + c], preferred_element_type=F32)
                    for c in range(3)
                )
            )
    grad_qkv = scatter_grad(
        jnp.stack(qkv_near_parts), jnp.stack(qkv_far_parts).astype(BF16), shard_count
    ).reshape(qkv_w.shape)
    first_grad = unflat(reduce_rows(first_near_parts, first_far_parts))

    input_grads = []
    mod_terms = []
    for s in range(2):
        unused, mod_vjp = jax.vjp(modulate, inputs[s], entry(s, 0), entry(s, 1))
        input_part, shift_part, scale_part = mod_vjp(first_grad[s])
        input_grads.append(mid_grad[s] + input_part)
        mod_terms.append(
            jnp.stack(
                [
                    shift_part[:, 0],
                    scale_part[:, 0],
                    gate_one[s],
                    shift_two[s],
                    scale_two[s],
                    gate_two[s],
                ],
                axis=1,
            )
        )

    back = ((1,), (1,))

    def restore(pair, dtype):
        both = jnp.concatenate(flat(pair), axis=0)
        if dtype == BF16:
            moved = lax.dot_general(both, order, (back, ((), ())), preferred_element_type=BF16)
        else:
            moved = permute_exact(both, order, back)
        count = seqs * img_rows
        return (
            moved[:count].reshape(shapes[0]),
            moved[count:].reshape(shapes[1])[:, :txt_real],
        )

    out_img, out_txt = restore(results, BF16)
    grad_img, grad_txt = restore(input_grads, F32)

    mod_low = jnp.stack(mod_terms).astype(BF16).reshape(-1, width)
    mod_low = lax.dot_general(mod_low, order, (back, ((), ())), preferred_element_type=BF16)
    mod_grad = lax.psum(mod_low, ("h", "l", "y", "c")).astype(F32).reshape(2, seqs, 6, width)
    own_mod = lax.dynamic_slice_in_dim(
        mod_grad, (own["y"] * 2 + own["c"]) * feat, feat, axis=3
    ).astype(BF16)
    mod_seqs = lax.all_gather(own_mod, "s", axis=1, tiled=True)
    grad_mod = jnp.einsum("sd,tskf->tdkf", cond_rows, mod_seqs, preferred_element_type=F32)
    cond_part = jnp.einsum("tskf,tdkf->sd", mod_seqs, mod_w, preferred_element_type=F32)
    cond_part = lax.psum(cond_part, ("y", "c"))
    cond_cols = lax.all_gather(cond_part, ("s", "h", "l"), axis=1, tiled=True)
    cond_total = lax.dynamic_slice_in_dim(cond_cols, own["s"] * seqs, seqs, axis=0)
    unused, silu_vjp = jax.vjp(jax.nn.silu, cond_float)
    grad_cond = silu_vjp(cond_total)[0]

    gain_grad = lax.psum(jnp.stack(gain_terms), ("s", "h", "l", "y", "c"))

    lanes = highest.shape[2] // 2
    row = jnp.arange(lanes, dtype=jnp.int32)
    valid = (row < 4 * img_rows) | ((row - 4 * img_rows) % txt_rows < txt_real)
    tops = highest.reshape(-1, seqs, 2, lanes)
    tops = jnp.max(jnp.where(valid, tops, -jnp.inf), axis=(1, 3)).reshape(heads)
    slots = jnp.where(jnp.arange(2)[:, None] == own["l"], tops[None, :], -jnp.inf)
    slots = lax.pmax(slots, ("s", "h", "l", "c"))
    peaks = lax.dynamic_index_in_dim(slots, own["c"], axis=0, keepdims=False)
    factor = jnp.sqrt(threshold / jnp.maximum(peaks, threshold))
    columns = jnp.repeat(factor, head_dim)
    clipped = qkv_w[:, :2].astype(F32) * columns
    return (
        out_img,
        out_txt,
        grad_img,
        grad_txt,
        grad_cond,
        grad_mod,
        grad_qkv,
        jnp.swapaxes(grad_o, 1, 2),
        grad_up,
        jnp.swapaxes(grad_down, 1, 2),
        gain_grad,
        clipped,
        peaks,
    )


def solution(mesh):
    shard, ctx, tp = (mesh.shape[name] for name in ("shard", "ctx", "tp"))
    fine = Mesh(mesh.devices.reshape(shard, ctx // 2, 2, tp // 2, 2), ("s", "h", "l", "y", "c"))
    ctx_axes, tp_axes = ("h", "l"), ("y", "c")
    rows = P("s", ctx_axes + tp_axes, None)
    weight = ("s",) + ctx_axes
    mod = P(None, weight, None, tp_axes)
    qkv = P(None, None, weight, tp_axes)
    inward = P(None, tp_axes, weight)
    outward = P(None, weight, tp_axes)
    return jax.shard_map(
        local,
        mesh=fine,
        in_specs=(
            rows,
            rows,
            P("s", None),
            P("s"),
            mod,
            qkv,
            inward,
            outward,
            inward,
            P(),
            P(),
            rows,
            rows,
        ),
        out_specs=(
            rows,
            rows,
            rows,
            rows,
            P("s", None),
            mod,
            qkv,
            inward,
            outward,
            inward,
            P(),
            qkv,
            P(tp_axes),
        ),
        check_vma=False,
    )
```

time: 3260 us -> 1210 us (0.37)
  waiting for transfers between devices: 2470 us -> 448 us
  local copies, waits for them, and re-layouts: 293 us -> 102 us
  starting transfers between devices: 2.88 us -> 123 us
  Pallas kernels: 0 us -> 45.7 us
  matrix products: 216 us -> 180 us
  blocking collectives: 114 us -> 147 us
    unnamed x31 -> x1, waiting for transfers between devices: 1260 us -> 0.02 us
    all_gather x11 -> x0, waiting for transfers between devices: 706 us -> none  [the longest x1 198 us: local(): mod_all = lax.all_gather(mod_w, ('shard', 'ctx'), axis=1, tiled=True)]
    reduce_scatter x5 -> x0, waiting for transfers between devices: 458 us -> none  [the longest x1 308 us: local(): lax.psum_scatter(grad_up, ('shard', 'ctx'), scatter_dimension=1, tiled=True)]
    ppermute x0 -> x73, waiting for transfers between devices: none -> 304 us  [the longest x65 301 us: trade(): return lax.ppermute(values, axis, [(0, 1), (1, 0)])]
    ppermute x0 -> x73, starting transfers between devices: none -> 123 us  [the longest x65 90.7 us: trade(): return lax.ppermute(values, axis, [(0, 1), (1, 0)])]
    psum x1, waiting for transfers between devices: 45.4 us -> 144 us  [local(): lax.psum(mod_low, ('h', 'l', 'y', 'c')).astype(F32)]
    unnamed x337 -> x553, local copies, waits for them, and re-layouts: 105 us -> 30.2 us
    another operation x9 -> x6, local copies, waits for them, and re-layouts: 62 us -> 2.57 us  [the longest x4 2.53 us: local(): jnp.tile(norm_gain[s, c], heads) * scales[c]]
  transfers between devices with their start and end apart: 24 -> 74, of which waited for: 23 -> 25; matrix products, arithmetic and copies ran while one was open for 13% -> 27% of each run, Pallas kernels for 0% -> 4%
where the time goes in v1:
time: 1210 us; the launch traced here: 1200 us
  waiting for transfers between devices  448 us (37%)
  matrix products  180 us (15%)
  blocking collectives  147 us (12%)
  other arithmetic  133 us (11%)
  starting transfers between devices  123 us (10%)
  local copies, waits for them, and re-layouts  102 us (8%)
  Pallas kernels  45.7 us (4%)
  between operations  19.3 us (2%)
    ppermute x65, waiting for transfers between devices, trade(): return lax.ppermute(values, axis, [(0, 1), (1, 0)])  301 us
    psum x1, waiting for transfers between devices, local(): lax.psum(mod_low, ('h', 'l', 'y', 'c')).astype(F32)  144 us
    ppermute x65, starting transfers between devices, trade(): return lax.ppermute(values, axis, [(0, 1), (1, 0)])  90.7 us
    all_gather x1, blocking collectives, local(): cond_cols = lax.all_gather(cond_part, ('s', 'h', 'l'), axis=1, tiled=True)  47.1 us
    psum x1, blocking collectives, local(): gain_grad = lax.psum(jnp.stack(gain_terms), ('s', 'h', 'l', 'y', 'c'))  41.8 us
    pmax x1, blocking collectives, local(): slots = lax.pmax(slots, ('s', 'h', 'l', 'c'))  32.3 us
    ppermute x8, starting transfers between devices, cross(): return lax.ppermute(values, ('l', 'c'), [(0, 0), (1, 2), (2, 1), (3, 3)])  31.9 us
    unnamed x553, local copies, waits for them, and re-layouts  30.2 us
  transfers between devices with their start and end apart: 74, of which 25 were waited for; matrix products, arithmetic and copies ran while one was open for 27% of the time, Pallas kernels for 4%

profile of v1, /device:TPU:1, one launch (start us, length us, event | category | flops | bytes accessed | tf_op | source)
XLA Modules:
  0.0 1198.4 jit_solution(14873543999798780840)
XLA Ops:
  46.5 10.8 collective-permute-start.2
  71.2 8.0 all_gather.13
  99.9 37.1 %collective-permute-done.6 = bf16[6,192,384]{2,1,0:T(8,128)(2,1)S(1)} collective-permute-done((bf16[6,192,384]{2,1,0:T(8,128)(2,1)}, bf16[6,192,384]{2,1,0:T(8,128)(2,1)S(1)}, u32[]{:S(2)}, u32[]{:S(2)}) %collective-permute-start.6) | collective-permute-done | bytes 884768 | tf_op jit(solution)/shard_map/ppermute | solution.py:32
  168.5 8.7 collective-permute-done.7
  183.0 6.9 collective-permute-done.16
  192.1 24.2 %collective-permute-done.31 = bf16[2,192,1536]{2,1,0:T(8,128)(2,1)S(1)} collective-permute-done((bf16[2,192,1536]{2,1,0:T(8,128)(2,1)}, bf16[2,192,1536]{2,1,0:T(8,128)(2,1)S(1)}, u32[]{:S(2)}, u32[]{:S(2)}) %collective-permute-start.31) | collective-permute-done | bytes 1179680 | tf_op jit(solution)/shard_map/ppermute | solution.py:32
  219.5 12.3 %collective-permute-done.39 = bf16[2,240,768]{2,1,0:T(8,128)(2,1)S(1)} collective-permute-done((bf16[2,240,768]{2,1,0:T(8,128)(2,1)S(1)}, bf16[2,240,768]{2,1,0:T(8,128)(2,1)S(1)}, u32[]{:S(2)}, u32[]{:S(2)}) %collective-permute-start.39) | collective-permute-done | bytes 737312 | tf_op jit(solution)/shard_map/ppermute | solution.py:32
  233.6 38.2 %collective-permute-done.25 = bf16[2,192,1536]{2,1,0:T(8,128)(2,1)S(1)} collective-permute-done((bf16[2,192,1536]{2,1,0:T(8,128)(2,1)S(1)}, bf16[2,192,1536]{2,1,0:T(8,128)(2,1)S(1)}, u32[]{:S(2)}, u32[]{:S(2)}) %collective-permute-start.25) | collective-permute-done | bytes 1179680 | tf_op jit(solution)/shard_map/ppermute | solution.py:32
  285.4 37.8 %collective-permute-done.26 = bf16[2,384,1536]{2,1,0:T(8,128)(2,1)S(1)} collective-permute-done((bf16[2,384,1536]{2,1,0:T(8,128)(2,1)S(1)}, bf16[2,384,1536]{2,1,0:T(8,128)(2,1)S(1)}, u32[]{:S(2)}, u32[]{:S(2)}) %collective-permute-start.26) | collective-permute-done | bytes 2359328 | tf_op jit(solution)/shard_map/ppermute | solution.py:32
  330.0 21.4 %collective-permute-done.12.refs_3_.refs_7_ = bf16[960,768]{1,0:T(8,128)(2,1)S(1)} collective-permute-done((bf16[960,768]{1,0:T(8,128)(2,1)S(1)}, bf16[960,768]{1,0:T(8,128)(2,1)S(1)}, u32[]{:S(2)}, u32[]{:S(2)}) %collective-permute-start.12) | collective-permute-done | bytes 1474592 | tf_op jit(solution)/shard_map/ppermute | solution.py:32
  362.7 18.4 %shard_map.228 = (bf16[960,384]{1,0:T(8,128)(2,1)}, f32[9,1,640]{2,1,0:T(1,128)}, f32[9,1,640]{2,1,0:T(1,128)}) custom-call(bf16[960,384]{1,0:T(8,128)(2,1)} %pad_maximum_fusion.19.refs_0_, bf16[960,768]{1,0:T(8,128)(2,1)} %copy-done.10, bf16[960,768]{1,0:T(8,128)(2,1)} %copy-done.21, bf16[960,768]{1,0:T(8,128)(2,1)} %copy-done.20, ...), custom_call_target="tpu_custom_call" | custom-call | flops 3774873600 | bytes 7372800 | tf_op jit(solution)/shard_map/pallas_call | solution.py:255
  398.9 11.4 collective-permute-done.20
  432.5 32.3 %pmax.7 = f32[2,6]{1,0:T(2,128)} all-reduce(f32[2,6]{1,0:T(2,128)} %broadcast_select_fusion), channel_id=1, replica_groups=mesh['s'=2,'h'=2,'l'=2,'y'=2,'c'=2] {'s','h','l','c'}, use_global_device_ids=true, to_apply=%region_40.41 | all-reduce | flops 12 | bytes 96 | tf_op jit(solution)/shard_map/pmax | solution.py:625
  479.5 6.5 collective-permute-done.28
  510.5 8.0 multiply_convert_fusion
  518.6 7.5 fusion.16
  581.3 7.8 collective-permute-done.36
  590.1 6.9 collective-permute-done.45
  650.2 27.4 %shard_map.229 = (f32[960,384]{1,0:T(8,128)}, bf16[960,384]{1,0:T(8,128)(2,1)}, bf16[960,384]{1,0:T(8,128)(2,1)}, bf16[960,384]{1,0:T(8,128)(2,1)}, bf16[960,384...) custom-call(bf16[960,384]{1,0:T(8,128)(2,1)} %pad_maximum_fusion.19., ...), custom_call_target="tpu_custom_call" | custom-call | flops 9437184000 | bytes 14745600 | tf_op jit(solution)/shard_map/pallas_call | solution.py:281
  680.3 7.0 collective-permute-start.51
  713.0 7.8 collective-permute-done.62
  721.0 7.5 collective-permute-start.63
  730.4 11.8 collective-permute-done.63
  751.5 9.0 maximum_add_fusion
  764.5 10.3 maximum_add_fusion.1
  780.4 32.7 %collective-permute-done.52 = bf16[960,768]{1,0:T(8,128)(2,1)} collective-permute-done((bf16[960,768]{1,0:T(8,128)(2,1)}, bf16[960,768]{1,0:T(8,128)(2,1)}, u32[]{:S(2)}, u32[]{:S(2)}) %collective-permute-start.52) | collective-permute-done | bytes 1474592 | tf_op jit(solution)/shard_map/ppermute | solution.py:32
  857.1 41.8 %psum.23 = f32[2,2,64]{2,1,0:T(2,128)} all-reduce(f32[2,2,64]{2,1,0:T(2,128)S(1)} %pad_maximum_fusion.77), channel_id=1, replica_groups=mesh['s'=2,'h'=2,'l'=2,'y'=2,'c'=2] {'s','h','l','y','c'}, use_global_device_ids=true, to_apply=%region_38.39 | all-reduce | flops 256 | bytes 2048 | tf_op jit(solution)/shard_map/psum | solution.py:617
  921.6 8.3 convert_add_fusion
  945.4 143.8 %all-reduce.4.cloned.1.call-done = bf16[2,3,6,1536]{3,0,2,1:T(2,128)(2,1)} async-done(((bf16[2,3,6,1536]{3,0,2,1:T(2,128)(2,1)}), bf16[2,3,6,1536]{3,0,2,1:T(2,128)(2,1)}) %all-reduce.4.cloned.1.call-update) | async-done | bytes 110608 | tf_op jit(solution)/shard_map/psum | solution.py:604
  1101.9 6.5 collective-permute-start.68
  1113.7 10.7 psum.22
  1124.3 47.1 %all-gather.1 = f32[8,192,6]{1,2,0:T(8,128)S(1)} all-gather(f32[1,192,6]{1,2,0:T(8,128)S(1)} %bitcast.704), channel_id=1, replica_groups=mesh['s'=2,'h'=2,'l'=2,'y'=2,'c'=2] {'s','h','l'}, dimensions={0}, use_global_device_ids=true | all-gather | bytes 41472 | tf_op jit(solution)/shard_map/all_gather | solution.py:612
  (1105 shorter events, 503.3 us)
Async XLA Ops:
  7.2 1082.0 %all-reduce.4.cloned.1.call-start = ((), (), s32[]{:S(2)}) async-start(), calls=%async_computation | async-start | bytes 221184 | tf_op jit(solution)/shard_map/psum | solution.py:604
  14.5 124.9 %collective-permute-start.14 = (bf16[2,192,384]{2,1,0:T(8,128)(2,1)}, bf16[2,192,384]{2,1,0:T(8,128)(2,1)}, u32[]{:S(2)}, u32[]{:S(2)}) collective-permute-start(bf16[2,192,384]{2,1,0:T(8,128)(2,1)} %bitcast.39), channel_id=1, source_target_pairs={{0,0},{1,4},{4,1},{5,5},{2,2},{3,6},{6,3},{7,7},{8,8},{9,12},{12,9... | collective-permute-start | bytes 884744 | tf_op jit(solution)/shard_map/ppermute | solution.py:36
  19.7 76.5 %collective-permute-start.5 = (bf16[6,192,384]{2,1,0:T(8,128)(2,1)}, bf16[6,192,384]{2,1,0:T(8,128)(2,1)}, u32[]{:S(2)}, u32[]{:S(2)}) collective-permute-start(bf16[6,192,384]{2,1,0:T(8,128)(2,1)} %bitcast.13), channel_id=1, source_target_pairs={{0,0},{1,4},{4,1},{5,5},{2,2},{3,6},{6,3},{7,7},{8,8},{9,12},{12,9... | collective-permute-start | bytes 2654216 | tf_op jit(solution)/shard_map/ppermute | solution.py:36
  21.7 141.3 %collective-permute-start.30 = (bf16[2,192,1536]{2,1,0:T(8,128)(2,1)}, bf16[2,192,1536]{2,1,0:T(8,128)(2,1)}, u32[]{:S(2)}, u32[]{:S(2)}) collective-permute-start(bf16[2,192,1536]{2,1,0:T(8,128)(2,1)} %bitcast.68), channel_id=1, source_target_pairs={{0,0},{1,4},{4,1},{5,5},{2,2},{3,6},{6,3},{7,7},{8,8},{9,12},{12,9... | collective-permute-start | bytes 3538952 | tf_op jit(solution)/shard_map/ppermute | solution.py:36
  89.7 49.7 %collective-permute-start.8 = (bf16[240,768]{1,0:T(8,128)(2,1)S(1)}, bf16[240,768]{1,0:T(8,128)(2,1)S(1)}, u32[]{:S(2)}, u32[]{:S(2)}) collective-permute-start(bf16[240,768]{1,0:T(8,128)(2,1)S(1)} %get-tuple-element.167), channel_id=1, source_target_pairs={{0,4},{4,0},{1,5},{5,1},{2,6},{6,2},{3,7},{7,3},{8,12},{12,8},{9,1... | collective-permute-start | bytes 1105928 | tf_op jit(solution)/shard_map/ppermute | solution.py:32
  91.5 50.7 %collective-permute-start.3 = (bf16[240,768]{1,0:T(8,128)(2,1)S(1)}, bf16[240,768]{1,0:T(8,128)(2,1)S(1)}, u32[]{:S(2)}, u32[]{:S(2)}) collective-permute-start(bf16[240,768]{1,0:T(8,128)(2,1)S(1)} %get-tuple-element.166), channel_id=1, source_target_pairs={{0,2},{2,0},{1,3},{3,1},{4,6},{6,4},{5,7},{7,5},{8,10},{10,8},{9,1... | collective-permute-start | bytes 1105928 | tf_op jit(solution)/shard_map/ppermute | solution.py:32
  162.9 53.3 %collective-permute-start.31 = (bf16[2,192,1536]{2,1,0:T(8,128)(2,1)}, bf16[2,192,1536]{2,1,0:T(8,128)(2,1)S(1)}, u32[]{:S(2)}, u32[]{:S(2)}) collective-permute-start(bf16[2,192,1536]{2,1,0:T(8,128)(2,1)} %collective-permute-done.30), channel_id=1, source_target_pairs={{0,8},{8,0},{1,9},{9,1},{2,10},{10,2},{3,11},{11,3},{4,12},{12,4},... | collective-permute-start | bytes 3538952 | tf_op jit(solution)/shard_map/ppermute | solution.py:32
  177.2 41.2 %collective-permute-start.4 = (bf16[2,240,768]{2,1,0:T(8,128)(2,1)S(1)}, bf16[2,240,768]{2,1,0:T(8,128)(2,1)S(1)}, u32[]{:S(2)}, u32[]{:S(2)}) collective-permute-start(bf16[2,240,768]{2,1,0:T(8,128)(2,1)S(1)} %pad_maximum_fusion.17), channel_id=1, source_target_pairs={{0,4},{4,0},{1,5},{5,1},{2,6},{6,2},{3,7},{7,3},{8,12},{12,8},{9,1... | collective-permute-start | bytes 2211848 | tf_op jit(solution)/shard_map/ppermute | solution.py:32
  177.6 98.5 %collective-permute-start.10 = (bf16[6,768,384]{2,1,0:T(8,128)(2,1)S(1)}, bf16[6,768,384]{2,1,0:T(8,128)(2,1)S(1)}, u32[]{:S(2)}, u32[]{:S(2)}) collective-permute-start(bf16[6,768,384]{2,1,0:T(8,128)(2,1)S(1)} %constant_dynamic-update-slice_fusion), channel_id=1, source_target_pairs={{0,1},{1,0},{2,3},{3,2},{4,5},{5,4},{6,7},{7,6},{8,9},{9,8},{10,11... | collective-permute-start | bytes 10616840 | tf_op jit(solution)/shard_map/ppermute | solution.py:32
  216.3 170.6 %collective-permute-start.19 = (bf16[2,768,384]{2,1,0:T(8,128)(2,1)}, bf16[2,768,384]{2,1,0:T(8,128)(2,1)}, u32[]{:S(2)}, u32[]{:S(2)}) collective-permute-start(bf16[2,768,384]{2,1,0:T(8,128)(2,1)} %constant_dynamic-update-slice_fusion.3), channel_id=1, source_target_pairs={{0,1},{1,0},{2,3},{3,2},{4,5},{5,4},{6,7},{7,6},{8,9},{9,8},{10,11... | collective-permute-start | bytes 3538952 | tf_op jit(solution)/shard_map/ppermute | solution.py:32
  218.4 56.0 %collective-permute-start.32 = (bf16[2,384,1536]{2,1,0:T(8,128)(2,1)S(1)}, bf16[2,384,1536]{2,1,0:T(8,128)(2,1)S(1)}, u32[]{:S(2)}, u32[]{:S(2)}) collective-permute-start(bf16[2,384,1536]{2,1,0:T(8,128)(2,1)S(1)} %pad_maximum_fusion.3), channel_id=1, source_target_pairs={{0,16},{16,0},{1,17},{17,1},{2,18},{18,2},{3,19},{19,3},{4,20},{20... | collective-permute-start | bytes 7077896 | tf_op jit(solution)/shard_map/ppermute | solution.py:32
  218.7 53.0 %collective-permute-start.25 = (bf16[2,192,1536]{2,1,0:T(8,128)(2,1)S(1)}, bf16[2,192,1536]{2,1,0:T(8,128)(2,1)S(1)}, u32[]{:S(2)}, u32[]{:S(2)}) collective-permute-start(bf16[2,192,1536]{2,1,0:T(8,128)(2,1)S(1)} %collective-permute-done.24), channel_id=1, source_target_pairs={{0,8},{8,0},{1,9},{9,1},{2,10},{10,2},{3,11},{11,3},{4,12},{12,4},... | collective-permute-start | bytes 3538952 | tf_op jit(solution)/shard_map/ppermute | solution.py:32
  271.9 51.3 %collective-permute-start.26 = (bf16[2,384,1536]{2,1,0:T(8,128)(2,1)S(1)}, bf16[2,384,1536]{2,1,0:T(8,128)(2,1)S(1)}, u32[]{:S(2)}, u32[]{:S(2)}) collective-permute-start(bf16[2,384,1536]{2,1,0:T(8,128)(2,1)S(1)} %pad_maximum_fusion.2), channel_id=1, source_target_pairs={{0,16},{16,0},{1,17},{17,1},{2,18},{18,2},{3,19},{19,3},{4,20},{20... | collective-permute-start | bytes 7077896 | tf_op jit(solution)/shard_map/ppermute | solution.py:32
  274.5 83.0 %collective-permute-start.35 = (bf16[2,768,1536]{2,1,0:T(8,128)(2,1)S(1)}, bf16[2,768,1536]{2,1,0:T(8,128)(2,1)S(1)}, u32[]{:S(2)}, u32[]{:S(2)}) collective-permute-start(bf16[2,768,1536]{2,1,0:T(8,128)(2,1)S(1)} %constant_dynamic-update-slice_fusion.9), channel_id=1, source_target_pairs={{0,1},{1,0},{2,3},{3,2},{4,5},{5,4},{6,7},{7,6},{8,9},{9,8},{10,11... | collective-permute-start | bytes 14155784 | tf_op jit(solution)/shard_map/ppermute | solution.py:32
  285.3 66.1 %collective-permute-start.12 = (bf16[960,768]{1,0:T(8,128)(2,1)S(1)}, bf16[960,768]{1,0:T(8,128)(2,1)S(1)}, u32[]{:S(2)}, u32[]{:S(2)}) collective-permute-start(bf16[960,768]{1,0:T(8,128)(2,1)S(1)} %maximum_maximum_fusion.refs_1_.refs_5_), channel_id=1, source_target_pairs={{0,8},{8,0},{1,9},{9,1},{2,10},{10,2},{3,11},{11,3},{4,12},{12,4},... | collective-permute-start | bytes 4423688 | tf_op jit(solution)/shard_map/ppermute | solution.py:32
  324.7 164.9 %collective-permute-start.29 = (bf16[2,768,1536]{2,1,0:T(8,128)(2,1)}, bf16[2,768,1536]{2,1,0:T(8,128)(2,1)}, u32[]{:S(2)}, u32[]{:S(2)}) collective-permute-start(bf16[2,768,1536]{2,1,0:T(8,128)(2,1)} %constant_dynamic-update-slice_fusion.6), channel_id=1, source_target_pairs={{0,1},{1,0},{2,3},{3,2},{4,5},{5,4},{6,7},{7,6},{8,9},{9,8},{10,11... | collective-permute-start | bytes 14155784 | tf_op jit(solution)/shard_map/ppermute | solution.py:32
  568.8 182.6 %collective-permute-start.65 = (bf16[2,768,1536]{2,1,0:T(8,128)(2,1)}, bf16[2,768,1536]{2,1,0:T(8,128)(2,1)}, u32[]{:S(2)}, u32[]{:S(2)}) collective-permute-start(bf16[2,768,1536]{2,1,0:T(8,128)(2,1)} %pad_maximum_fusion), channel_id=1, source_target_pairs={{0,1},{1,0},{2,3},{3,2},{4,5},{5,4},{6,7},{7,6},{8,9},{9,8},{10,11... | collective-permute-start | bytes 14155784 | tf_op jit(solution)/shard_map/ppermute | solution.py:32
  576.6 187.9 %collective-permute-start.69 = (bf16[2,768,1536]{2,1,0:T(8,128)(2,1)}, bf16[2,768,1536]{2,1,0:T(8,128)(2,1)}, u32[]{:S(2)}, u32[]{:S(2)}) collective-permute-start(bf16[2,768,1536]{2,1,0:T(8,128)(2,1)} %pad_maximum_fusion.1), channel_id=1, source_target_pairs={{0,1},{1,0},{2,3},{3,2},{4,5},{5,4},{6,7},{7,6},{8,9},{9,8},{10,11... | collective-permute-start | bytes 14155784 | tf_op jit(solution)/shard_map/ppermute | solution.py:32
  680.3 64.4 %collective-permute-start.51 = (bf16[960,768]{1,0:T(8,128)(2,1)}, bf16[960,768]{1,0:T(8,128)(2,1)}, u32[]{:S(2)}, u32[]{:S(2)}) collective-permute-start(bf16[960,768]{1,0:T(8,128)(2,1)} %pad_maximum_fusion.6), channel_id=1, source_target_pairs={{0,1},{1,0},{2,3},{3,2},{4,5},{5,4},{6,7},{7,6},{8,9},{9,8},{10,11... | collective-permute-start | bytes 4423688 | tf_op jit(solution)/shard_map/ppermute | solution.py:32
  688.5 92.0 %collective-permute-start.50 = (bf16[960,768]{1,0:T(8,128)(2,1)}, bf16[960,768]{1,0:T(8,128)(2,1)}, u32[]{:S(2)}, u32[]{:S(2)}) collective-permute-start(bf16[960,768]{1,0:T(8,128)(2,1)} %pad_maximum_fusion.5), channel_id=1, source_target_pairs={{0,1},{1,0},{2,3},{3,2},{4,5},{5,4},{6,7},{7,6},{8,9},{9,8},{10,11... | collective-permute-start | bytes 4423688 | tf_op jit(solution)/shard_map/ppermute | solution.py:32
  747.6 65.6 %collective-permute-start.52 = (bf16[960,768]{1,0:T(8,128)(2,1)}, bf16[960,768]{1,0:T(8,128)(2,1)}, u32[]{:S(2)}, u32[]{:S(2)}) collective-permute-start(bf16[960,768]{1,0:T(8,128)(2,1)} %add_convert_fusion), channel_id=1, source_target_pairs={{0,8},{8,0},{1,9},{9,1},{2,10},{10,2},{3,11},{11,3},{4,12},{12,4},... | collective-permute-start | bytes 4423688 | tf_op jit(solution)/shard_map/ppermute | solution.py:32
  764.5 170.5 %collective-permute-start.66 = (bf16[2,384,1536]{2,1,0:T(8,128)(2,1)}, bf16[2,384,1536]{2,1,0:T(8,128)(2,1)}, u32[]{:S(2)}, u32[]{:S(2)}) collective-permute-start(bf16[2,384,1536]{2,1,0:T(8,128)(2,1)} %slice.1818), channel_id=1, source_target_pairs={{0,16},{16,0},{1,17},{17,1},{2,18},{18,2},{3,19},{19,3},{4,20},{20... | collective-permute-start | bytes 7077896 | tf_op jit(solution)/shard_map/ppermute | solution.py:32
  779.0 159.2 %collective-permute-start.70 = (bf16[2,384,1536]{2,1,0:T(8,128)(2,1)}, bf16[2,384,1536]{2,1,0:T(8,128)(2,1)}, u32[]{:S(2)}, u32[]{:S(2)}) collective-permute-start(bf16[2,384,1536]{2,1,0:T(8,128)(2,1)} %slice.1817), channel_id=1, source_target_pairs={{0,16},{16,0},{1,17},{17,1},{2,18},{18,2},{3,19},{19,3},{4,20},{20... | collective-permute-start | bytes 7077896 | tf_op jit(solution)/shard_map/ppermute | solution.py:32
  844.7 76.8 %collective-permute-start.57 = (bf16[6,768,384]{2,1,0:T(8,128)(2,1)}, bf16[6,768,384]{2,1,0:T(8,128)(2,1)}, u32[]{:S(2)}, u32[]{:S(2)}) collective-permute-start(bf16[6,768,384]{2,1,0:T(8,128)(2,1)} %fusion.84), channel_id=1, source_target_pairs={{0,1},{1,0},{2,3},{3,2},{4,5},{5,4},{6,7},{7,6},{8,9},{9,8},{10,11... | collective-permute-start | bytes 10616840 | tf_op jit(solution)/shard_map/ppermute | solution.py:32
  850.5 48.5 %collective-permute-start.56 = (bf16[240,768]{1,0:T(8,128)(2,1)}, bf16[240,768]{1,0:T(8,128)(2,1)}, u32[]{:S(2)}, u32[]{:S(2)}) collective-permute-start(bf16[240,768]{1,0:T(8,128)(2,1)} %fusion.136), channel_id=1, source_target_pairs={{0,4},{4,0},{1,5},{5,1},{2,6},{6,2},{3,7},{7,3},{8,12},{12,8},{9,1... | collective-permute-start | bytes 1105928 | tf_op jit(solution)/shard_map/ppermute | solution.py:32
  855.4 45.0 %collective-permute-start.54 = (bf16[240,768]{1,0:T(8,128)(2,1)}, bf16[240,768]{1,0:T(8,128)(2,1)}, u32[]{:S(2)}, u32[]{:S(2)}) collective-permute-start(bf16[240,768]{1,0:T(8,128)(2,1)} %fusion.140), channel_id=1, source_target_pairs={{0,2},{2,0},{1,3},{3,1},{4,6},{6,4},{5,7},{7,5},{8,10},{10,8},{9,1... | collective-permute-start | bytes 1105928 | tf_op jit(solution)/shard_map/ppermute | solution.py:32
  934.2 159.3 %collective-permute-start.58 = (bf16[6,384,384]{2,1,0:T(8,128)(2,1)}, bf16[6,384,384]{2,1,0:T(8,128)(2,1)}, u32[]{:S(2)}, u32[]{:S(2)}) collective-permute-start(bf16[6,384,384]{2,1,0:T(8,128)(2,1)} %slice.1819), channel_id=1, source_target_pairs={{0,16},{16,0},{1,17},{17,1},{2,18},{18,2},{3,19},{19,3},{4,20},{20... | collective-permute-start | bytes 5308424 | tf_op jit(solution)/shard_map/ppermute | solution.py:32
  938.0 160.7 %collective-permute-start.67 = (bf16[2,192,1536]{2,1,0:T(8,128)(2,1)S(1)}, bf16[2,192,1536]{2,1,0:T(8,128)(2,1)}, u32[]{:S(2)}, u32[]{:S(2)}) collective-permute-start(bf16[2,192,1536]{2,1,0:T(8,128)(2,1)S(1)} %slice.1821), channel_id=1, source_target_pairs={{0,8},{8,0},{1,9},{9,1},{2,10},{10,2},{3,11},{11,3},{4,12},{12,4},... | collective-permute-start | bytes 3538952 | tf_op jit(solution)/shard_map/ppermute | solution.py:32
  944.5 164.0 %collective-permute-start.71 = (bf16[2,192,1536]{2,1,0:T(8,128)(2,1)}, bf16[2,192,1536]{2,1,0:T(8,128)(2,1)}, u32[]{:S(2)}, u32[]{:S(2)}) collective-permute-start(bf16[2,192,1536]{2,1,0:T(8,128)(2,1)} %slice.1820), channel_id=1, source_target_pairs={{0,8},{8,0},{1,9},{9,1},{2,10},{10,2},{3,11},{11,3},{4,12},{12,4},... | collective-permute-start | bytes 3538952 | tf_op jit(solution)/shard_map/ppermute | solution.py:32
  1097.5 74.1 %collective-permute-start.59 = (bf16[6,192,384]{2,1,0:T(8,128)(2,1)}, bf16[6,192,384]{2,1,0:T(8,128)(2,1)}, u32[]{:S(2)}, u32[]{:S(2)}) collective-permute-start(bf16[6,192,384]{2,1,0:T(8,128)(2,1)} %slice.1822), channel_id=1, source_target_pairs={{0,8},{8,0},{1,9},{9,1},{2,10},{10,2},{3,11},{11,3},{4,12},{12,4},... | collective-permute-start | bytes 2654216 | tf_op jit(solution)/shard_map/ppermute | solution.py:32
  1101.9 80.5 %collective-permute-start.68 = (bf16[2,192,1536]{2,1,0:T(8,128)(2,1)}, bf16[2,192,1536]{2,1,0:T(8,128)(2,1)S(1)}, u32[]{:S(2)}, u32[]{:S(2)}) collective-permute-start(bf16[2,192,1536]{2,1,0:T(8,128)(2,1)} %fusion.34), channel_id=1, source_target_pairs={{0,0},{1,4},{4,1},{5,5},{2,2},{3,6},{6,3},{7,7},{8,8},{9,12},{12,9... | collective-permute-start | bytes 3538952 | tf_op jit(solution)/shard_map/ppermute | solution.py:36
  1111.2 72.9 %collective-permute-start.72 = (bf16[2,192,1536]{2,1,0:T(8,128)(2,1)}, bf16[2,192,1536]{2,1,0:T(8,128)(2,1)}, u32[]{:S(2)}, u32[]{:S(2)}) collective-permute-start(bf16[2,192,1536]{2,1,0:T(8,128)(2,1)} %fusion.33), channel_id=1, source_target_pairs={{0,0},{1,4},{4,1},{5,5},{2,2},{3,6},{6,3},{7,7},{8,8},{9,12},{12,9... | collective-permute-start | bytes 3538952 | tf_op jit(solution)/shard_map/ppermute | solution.py:36
  (305 other events, 5874.6 us)
Sparse Core Ops, SparseCore 0:
  921.6 167.5 all-reduce.3

commit v2 on v1

v2 whole, which is shorter than its diff:
```python
import functools

import jax
import jax.numpy as jnp
from jax import lax
from jax.experimental import pallas as pl
from jax.experimental.pallas import tpu as pltpu
from jax.sharding import Mesh, PartitionSpec as P

EPS = 1e-06
QUERY_SCALE = 0.125
BF16 = jnp.bfloat16
F32 = jnp.float32
MASKED = -1e30
NT = (((1,), (1,)), ((), ()))
TN = (((0,), (0,)), ((), ()))
NN = (((1,), (0,)), ((), ()))


def trade(values, axis):
    return lax.ppermute(values, axis, [(0, 1), (1, 0)])


def cross(values):
    moved = lax.ppermute(values, ("l", "c"), [(1, 2), (2, 1)])
    return jnp.where(lax.axis_index("l") == lax.axis_index("c"), values, moved)


def in_order(values, axis, dim):
    other = trade(values, axis)
    first = lax.axis_index(axis) == 0
    return jnp.concatenate(
        [jnp.where(first, values, other), jnp.where(first, other, values)], axis=dim
    )


def total_over(values, axes):
    for axis in axes:
        values = values + trade(values, axis)
    return values


def highest_over(values, axes):
    for axis in axes:
        values = jnp.maximum(values, trade(values, axis))
    return values


def after(values, others):
    return lax.optimization_barrier((values, others))[0]


def feature_order(width, shard_count):
    place = jnp.arange(width, dtype=jnp.int32)
    block = width // (shard_count * 4)
    member = place // block
    low = member // (shard_count * 2) ^ lax.axis_index("c")
    return (member % (shard_count * 2) * 2 + low) * block + place % block


def one_hot(source):
    width = source.shape[0]
    rows = lax.broadcasted_iota(jnp.int32, (width, width), 0)
    return (rows == source[None, :]).astype(BF16)


def permute_exact(values, matrix, dims):
    high = lax.reduce_precision(values, 8, 7)
    rest = values - high
    middle = lax.reduce_precision(rest, 8, 7)
    low = rest - middle
    parts = [
        lax.dot_general(part.astype(BF16), matrix, (dims, ((), ())), preferred_element_type=F32)
        for part in (high, middle, low)
    ]
    return parts[0] + (parts[1] + parts[2])


def gather_weight(shard, others=None):
    own = cross(shard)
    if others is not None:
        own = after(own, others)
    return lax.all_gather(own, ("s", "h"), axis=1, tiled=True)


def dot(left, right, dims):
    return lax.dot_general(left, right, dims, preferred_element_type=F32)


def row_groups(sizes):
    img, txt, seqs = sizes
    base = seqs * img
    groups = [(s * img, (s + 1) * img, 0, s) for s in range(seqs)]
    return groups + [(base + s * txt, base + (s + 1) * txt, 1, s) for s in range(seqs)]


def stream_parts(sizes, stream):
    img, txt, seqs = sizes
    per = seqs * (img + txt)
    lo, hi = ((0, seqs * img), (seqs * img, per))[stream]
    return [(b * per + lo, b * per + hi) for b in range(4)]


def stream_rows(ref, sizes, stream):
    return jnp.concatenate([ref[a:b, :] for a, b in stream_parts(sizes, stream)], axis=0)


def put_stream(ref, sizes, stream, value):
    at = 0
    for a, b in stream_parts(sizes, stream):
        ref[a:b, :] = value[at : at + b - a].astype(ref.dtype)
        at += b - a


def vec(ref, stream, seq, k):
    row = (seq * 2 + stream) * 6 + k
    return ref[row : row + 1, :]


def normal(values):
    center = values - jnp.mean(values, axis=-1, keepdims=True)
    inv = lax.rsqrt(jnp.mean(center * center, axis=-1, keepdims=True) + EPS)
    return center * inv, inv


def normal_back(grad, unit, inv):
    mean = jnp.mean(grad, axis=-1, keepdims=True)
    return inv * (grad - mean - unit * jnp.mean(grad * unit, axis=-1, keepdims=True))


def put_halves(near_ref, far_ref, a, b, value):
    half = value.shape[1] // 2
    near_ref[a:b, :] = value[:, :half].astype(near_ref.dtype)
    far_ref[a:b, :] = value[:, half:].astype(far_ref.dtype)


def first_kernel(sizes, x_ref, cot_ref, mod_ref, n1_ref, f1_ref, n2_ref, f2_ref):
    for a, b, t, s in row_groups(sizes):
        unit, _ = normal(x_ref[a:b, :].astype(F32))
        put_halves(n1_ref, f1_ref, a, b, unit * (1.0 + vec(mod_ref, t, s, 1)) + vec(mod_ref, t, s, 0))
        put_halves(n2_ref, f2_ref, a, b, cot_ref[a:b, :].astype(F32) * vec(mod_ref, t, s, 5))


def middle_kernel(sizes, x_ref, attn_ref, mod_ref, mid_ref, n_ref, f_ref):
    for a, b, t, s in row_groups(sizes):
        mid = x_ref[a:b, :].astype(F32) + vec(mod_ref, t, s, 2) * attn_ref[a:b, :]
        mid_ref[a:b, :] = mid
        unit, _ = normal(mid)
        put_halves(n_ref, f_ref, a, b, unit * (1.0 + vec(mod_ref, t, s, 4)) + vec(mod_ref, t, s, 3))


def last_kernel(sizes, mid_ref, mlp_ref, cot_ref, mod_ref, out_ref, sum_ref):
    for a, b, t, s in row_groups(sizes):
        mlp = mlp_ref[a:b, :]
        out_ref[a:b, :] = (mid_ref[a:b, :] + vec(mod_ref, t, s, 5) * mlp).astype(BF16)
        row = t * sizes[2] + s
        sum_ref[row : row + 1, :] = jnp.sum(
            cot_ref[a:b, :].astype(F32) * mlp, axis=0, keepdims=True
        )


def middle_back_kernel(
    sizes, mid_ref, cot_ref, grad_ref, attn_ref, mod_ref, out_ref, n_ref, f_ref, sum_ref
):
    count = 2 * sizes[2]
    for a, b, t, s in row_groups(sizes):
        row = t * sizes[2] + s
        unit, inv = normal(mid_ref[a:b, :])
        grad = grad_ref[a:b, :]
        sum_ref[row : row + 1, :] = jnp.sum(grad, axis=0, keepdims=True)
        sum_ref[count + row : count + row + 1, :] = jnp.sum(grad * unit, axis=0, keepdims=True)
        back = normal_back(grad * (1.0 + vec(mod_ref, t, s, 4)), unit, inv)
        total = cot_ref[a:b, :].astype(F32) + back
        out_ref[a:b, :] = total
        put_halves(n_ref, f_ref, a, b, total * vec(mod_ref, t, s, 2))
        sum_ref[2 * count + row : 2 * count + row + 1, :] = jnp.sum(
            total * attn_ref[a:b, :], axis=0, keepdims=True
        )


def first_back_kernel(sizes, x_ref, mid_grad_ref, grad_ref, mod_ref, out_ref, sum_ref):
    count = 2 * sizes[2]
    for a, b, t, s in row_groups(sizes):
        row = t * sizes[2] + s
        unit, inv = normal(x_ref[a:b, :].astype(F32))
        grad = grad_ref[a:b, :]
        sum_ref[row : row + 1, :] = jnp.sum(grad, axis=0, keepdims=True)
        sum_ref[count + row : count + row + 1, :] = jnp.sum(grad * unit, axis=0, keepdims=True)
        back = normal_back(grad * (1.0 + vec(mod_ref, t, s, 1)), unit, inv)
        out_ref[a:b, :] = mid_grad_ref[a:b, :] + back


def call(kernel, outs, *args, flops=1 << 20):
    return pl.pallas_call(
        kernel,
        out_shape=[jax.ShapeDtypeStruct(shape, dtype) for shape, dtype in outs],
        cost_estimate=pl.CostEstimate(flops=flops, bytes_accessed=1 << 20, transcendentals=0),
        compiler_params=pltpu.CompilerParams(vmem_limit_bytes=48 << 20),
    )(*args)


def head_spread(width, head_dim):
    rows = lax.broadcasted_iota(jnp.int32, (width, width), 0) // head_dim
    cols = lax.broadcasted_iota(jnp.int32, (width, width), 1) // head_dim
    return jnp.where(rows == cols, 1.0 / head_dim, 0.0).astype(BF16)


def head_mean(values, spread):
    high = values.astype(BF16)
    low = (values - high.astype(F32)).astype(BF16)
    return dot(high, spread, NN) + dot(low, spread, NN)


def qkv_kernel(sizes, head_dim, near_ref, far_ref, wn_ref, wf_ref, gain_ref, q_ref, kv_ref, raw_ref):
    spread = head_spread(q_ref.shape[1], head_dim)

    def part(c):
        for t in range(2):
            left = stream_rows(near_ref, sizes, t), stream_rows(far_ref, sizes, t)
            total = dot(left[0], wn_ref[t, 0], NN) + dot(left[1], wf_ref[t, 0], NN)
            if c < 2:
                put_stream(raw_ref.at[0], sizes, t, total)
                root = lax.rsqrt(head_mean(total * total, spread) + EPS)
                total = total * root * gain_ref[2 * t + c : 2 * t + c + 1, :]
            put_stream(q_ref if c == 0 else kv_ref.at[0], sizes, t, total)

    for c in range(3):
        pl.when(pl.program_id(0) == c)(functools.partial(part, c))


def qkv_project(near, far, w_near, w_far, gains, sizes, head_dim):
    rows, half = near.shape
    width = gains.shape[1]
    whole = pl.BlockSpec((rows, half), lambda c: (0, 0))
    weight = pl.BlockSpec((2, 1, half, width), lambda c: (0, c, 0, 0))
    return pl.pallas_call(
        functools.partial(qkv_kernel, sizes, head_dim),
        grid=(3,),
        in_specs=[whole, whole, weight, weight, pl.BlockSpec((4, width), lambda c: (0, 0))],
        out_specs=[
            pl.BlockSpec((rows, width), lambda c: (0, 0)),
            pl.BlockSpec((1, rows, width), lambda c: (jnp.maximum(c - 1, 0), 0, 0)),
            pl.BlockSpec((1, rows, width), lambda c: (jnp.minimum(c, 1), 0, 0)),
        ],
        out_shape=[
            jax.ShapeDtypeStruct((rows, width), BF16),
            jax.ShapeDtypeStruct((2, rows, width), BF16),
            jax.ShapeDtypeStruct((2, rows, width), F32),
        ],
        cost_estimate=pl.CostEstimate(flops=1 << 20, bytes_accessed=1 << 20, transcendentals=0),
        compiler_params=pltpu.CompilerParams(vmem_limit_bytes=48 << 20),
    )(
        near,
        far,
        w_near.reshape(2, 3, half, width),
        w_far.reshape(2, 3, half, width),
        gains,
    )


def qkv_back_kernel(
    sizes, head_dim, q_ref, own_ref, c_ref, h_ref, raw_ref, gain_ref, low_ref, sum_ref
):
    width = q_ref.shape[1]
    spread = head_spread(width, head_dim)
    for t in range(2):
        for c in range(2):
            gain = gain_ref[2 * t + c : 2 * t + c + 1, :]
            total = jnp.zeros((1, width), F32)
            for a, b in stream_parts(sizes, t):
                if c == 0:
                    grad = q_ref[a:b, :]
                else:
                    grad = own_ref[0, a:b, :].astype(F32) + c_ref[0, a:b, :].astype(F32)
                    grad = grad + h_ref[0, a:b, :].astype(F32)
                raw = raw_ref[c, a:b, :]
                root = lax.rsqrt(head_mean(raw * raw, spread) + EPS)
                unit = raw * root
                total = total + jnp.sum(grad * unit, axis=0, keepdims=True)
                scaled = grad * gain
                back = root * (scaled - unit * head_mean(scaled * unit, spread))
                low_ref[a:b, c * width : (c + 1) * width] = back.astype(BF16)
            sum_ref[2 * t + c : 2 * t + c + 1, :] = total
        for a, b in stream_parts(sizes, t):
            grad = own_ref[1, a:b, :].astype(F32) + c_ref[1, a:b, :].astype(F32)
            low_ref[a:b, 2 * width :] = (grad + h_ref[1, a:b, :].astype(F32)).astype(BF16)


def mixed_kernel(sizes, near_ref, far_ref, wn_ref, wf_ref, out_ref):
    for t in range(2):
        total = dot(stream_rows(near_ref, sizes, t), wn_ref[t], NN)
        total = total + dot(stream_rows(far_ref, sizes, t), wf_ref[t], NN)
        put_stream(out_ref, sizes, t, total)


GELU_ROOT = 0.7978845608028654
GELU_CUBE = 0.044715


def mlp_kernel(sizes, sn_ref, sf_ref, mn_ref, mf_ref, un_ref, uf_ref, dn_ref, df_ref, h_ref, g_ref):
    for t in range(2):
        pre = dot(stream_rows(sn_ref, sizes, t), un_ref[t], NN)
        pre = pre + dot(stream_rows(sf_ref, sizes, t), uf_ref[t], NN)
        square = pre * pre
        bent = jnp.tanh(GELU_ROOT * pre * (1.0 + GELU_CUBE * square))
        half = 0.5 * (1.0 + bent)
        put_stream(h_ref, sizes, t, pre * half)
        back = dot(stream_rows(mn_ref, sizes, t), dn_ref[t], NN)
        back = back + dot(stream_rows(mf_ref, sizes, t), df_ref[t], NN)
        slope = half + 0.5 * pre * (1.0 - bent * bent) * (
            GELU_ROOT * (1.0 + 3.0 * GELU_CUBE * square)
        )
        put_stream(g_ref, sizes, t, back * slope)


def mlp(second, cot, up, down, sizes):
    rows, half = second[0].shape
    width = up[0].shape[2]
    tile = 384 if width % 384 == 0 else width
    whole = pl.BlockSpec((rows, half), lambda j: (0, 0))
    weight = pl.BlockSpec((2, half, tile), lambda j: (0, 0, j))
    out = pl.BlockSpec((rows, tile), lambda j: (0, j))
    return pl.pallas_call(
        functools.partial(mlp_kernel, sizes),
        grid=(width // tile,),
        in_specs=[whole] * 4 + [weight] * 4,
        out_specs=[out] * 2,
        out_shape=[jax.ShapeDtypeStruct((rows, width), BF16)] * 2,
        cost_estimate=pl.CostEstimate(flops=1 << 20, bytes_accessed=1 << 20, transcendentals=0),
        compiler_params=pltpu.CompilerParams(vmem_limit_bytes=56 << 20),
    )(*second, *cot, *up, *down)


SENT = ((2, 3), (1, 2))
KEPT = ((0, 1), (0, 3))


def project_kernel(sizes, rows_ref, *refs):
    weights, outs = refs[:2], refs[2:]
    per = rows_ref.shape[0] // 4
    for t in range(2):
        left = stream_rows(rows_ref, sizes, t)
        lo, hi = stream_parts(sizes, t)[0]
        for side in range(2):
            chunks = weights[side].shape[0] // 2
            depth = weights[side].shape[2]
            total = dot(left[:, :depth], weights[side][t * chunks], NT)
            for c in range(1, chunks):
                total = total + dot(
                    left[:, c * depth : (c + 1) * depth], weights[side][t * chunks + c], NT
                )
            count = hi - lo
            for k in range(2):
                b = SENT[side][k]
                outs[2 * side][k, lo:hi, :] = total[b * count : (b + 1) * count].astype(BF16)
                b = KEPT[side][k]
                outs[2 * side + 1][k, lo:hi, :] = total[b * count : (b + 1) * count]


def project(rows, near, far, sizes):
    count, depth = rows.shape
    chunks, half, inner = near.shape
    tile = 384 if half % 384 == 0 else half
    weight = pl.BlockSpec((chunks, tile, inner), lambda j: (0, j, 0))
    out = pl.BlockSpec((2, count // 4, tile), lambda j: (0, 0, j))
    shape = (2, count // 4, half)
    return pl.pallas_call(
        functools.partial(project_kernel, sizes),
        grid=(half // tile,),
        in_specs=[pl.BlockSpec((count, depth), lambda j: (0, 0)), weight, weight],
        out_specs=[out] * 4,
        out_shape=[jax.ShapeDtypeStruct(shape, d) for d in (BF16, F32, BF16, F32)],
        cost_estimate=pl.CostEstimate(flops=1 << 20, bytes_accessed=1 << 20, transcendentals=0),
        compiler_params=pltpu.CompilerParams(vmem_limit_bytes=56 << 20),
    )(rows, near, far)


def grad_kernel(sizes, add, left_ref, right_ref, *refs):
    for t in range(2):
        total = dot(stream_rows(left_ref, sizes, t), stream_rows(right_ref, sizes, t), TN)
        if add:
            total = total + refs[0][t].reshape(total.shape).astype(F32)
        refs[-1][t] = total.astype(BF16).reshape(refs[-1].shape[1:])


def stream_grads(left, right, sizes, split, other=None):
    rows, depth = left.shape
    width = right.shape[1]
    tile = 384 if width % 384 == 0 else width
    if split:
        out = pl.BlockSpec((2, 1, depth, tile), lambda j: (0, j, 0, 0))
        shape = (2, width // tile, depth, tile)
    else:
        out = pl.BlockSpec((2, depth, tile), lambda j: (0, 0, j))
        shape = (2, depth, width)
    extra = [] if other is None else [other]
    return pl.pallas_call(
        functools.partial(grad_kernel, sizes, bool(extra)),
        grid=(width // tile,),
        in_specs=[
            pl.BlockSpec((rows, depth), lambda j: (0, 0)),
            pl.BlockSpec((rows, tile), lambda j: (0, j)),
        ]
        + [out] * len(extra),
        out_specs=out,
        out_shape=jax.ShapeDtypeStruct(shape, BF16),
        cost_estimate=pl.CostEstimate(flops=1 << 20, bytes_accessed=1 << 20, transcendentals=0),
        compiler_params=pltpu.CompilerParams(vmem_limit_bytes=48 << 20),
    )(left, right, *extra)


def pair_grad(left, right, sizes, split=False):
    far = trade(stream_grads(left[1], right, sizes, split), "c")
    return stream_grads(left[0], right, sizes, split, far)


def shard_grad(total):
    return lax.psum_scatter(total, ("s", "h"), scatter_dimension=total.ndim - 2, tiled=True)


def own_grad(block):
    return cross(block).astype(F32)


def gather_rows(first, second):
    first_pair = jnp.stack([first, trade(first, "y")])
    second_pair = jnp.stack([second, trade(second, "l")])
    first_far = trade(first_pair, "l")
    second_far = trade(second_pair, "y")
    near = [first_pair[0], first_pair[1], first_far[1], first_far[0]]
    far = [second_pair[0], second_far[0], second_far[1], second_pair[1]]
    return jnp.concatenate(near), jnp.concatenate(far)


def reduce_rows(near_send, near_keep, far_send, far_keep):
    first_in = trade(near_send, "l")
    second_in = trade(far_send, "y")
    first_last = trade((near_keep[1] + first_in[0].astype(F32)).astype(BF16), "y")
    second_last = trade((far_keep[1] + second_in[1].astype(F32)).astype(BF16), "l")
    first = near_keep[0] + first_in[1].astype(F32) + first_last.astype(F32)
    second = far_keep[0] + second_in[0].astype(F32) + second_last.astype(F32)
    return jnp.concatenate([first, second], axis=1), (first_in, second_in)


def sequence_places(seq, sizes):
    img, txt, seqs = sizes
    per = seqs * (img + txt)
    places = [(pl.multiple_of(b * per + seq * img, 16), img) for b in range(4)]
    return places + [(pl.multiple_of(b * per + seqs * img + seq * txt, 16), txt) for b in range(4)]


def sequence_rows(ref, seq, sizes):
    return jnp.concatenate([ref[pl.ds(a, n), :] for a, n in sequence_places(seq, sizes)], axis=0)


def store_rows(ref, seq, sizes, value):
    at = 0
    for a, n in sequence_places(seq, sizes):
        ref[pl.ds(a, n), :] = value[at : at + n]
        at += n


def both_heads(rows, head_dim):
    lane = lax.broadcasted_iota(jnp.int32, rows.shape, 1)
    zero = jnp.zeros_like(rows)
    return jnp.concatenate(
        [jnp.where(lane < head_dim, rows, zero), jnp.where(lane >= head_dim, rows, zero)], axis=0
    )


def join_heads(stacked, head_dim):
    count = stacked.shape[0] // 2
    lane = lax.broadcasted_iota(jnp.int32, (count, stacked.shape[1]), 1)
    return jnp.where(lane < head_dim, stacked[:count], stacked[count:])


def attend_kernel(sizes, head_dim, *refs):
    q_ref, kv_refs = refs[0], refs[1:5]
    bias_ref, out_ref, norm_ref, peak_ref = refs[5:]
    seq = pl.program_id(1)
    query = both_heads(sequence_rows(q_ref, seq, sizes), head_dim)
    keys = jnp.concatenate([sequence_rows(r.at[0], seq, sizes) for r in kv_refs], axis=0)
    values = jnp.concatenate([sequence_rows(r.at[1], seq, sizes) for r in kv_refs], axis=0)
    scores = lax.dot_general(keys, query, NT, preferred_element_type=F32) + bias_ref[0]
    highest = jnp.max(scores, axis=0, keepdims=True)
    weights = jnp.exp(scores - highest)
    total = jnp.sum(weights, axis=0, keepdims=True)
    mixed = lax.dot_general(values, weights.astype(BF16), TN, preferred_element_type=F32)
    mixed = jnp.transpose(mixed * (1.0 / total))
    store_rows(out_ref, seq, sizes, join_heads(mixed, head_dim).astype(BF16))
    norm_ref[0] = highest + jnp.log(total)
    peak_ref[0] = highest


def attend_back_kernel(sizes, head_dim, *refs):
    q_ref, kv_refs = refs[0], refs[1:5]
    bias_ref, norm_ref, grad_ref = refs[5:8]
    gq_ref, gkv_refs = refs[8], refs[9:13]
    seq = pl.program_id(1)
    query = both_heads(sequence_rows(q_ref, seq, sizes), head_dim)
    grad = both_heads(sequence_rows(grad_ref, seq, sizes), head_dim)
    keys = jnp.concatenate([sequence_rows(r.at[0], seq, sizes) for r in kv_refs], axis=0)
    values = jnp.concatenate([sequence_rows(r.at[1], seq, sizes) for r in kv_refs], axis=0)
    scores = lax.dot_general(keys, query, NT, preferred_element_type=F32) + bias_ref[0]
    probs = jnp.exp(scores - norm_ref[0])
    grad_probs = lax.dot_general(values, grad, NT, preferred_element_type=F32)
    inner = jnp.sum(probs * grad_probs, axis=0, keepdims=True)
    grad_scores = (probs * (grad_probs - inner)).astype(BF16)
    grad_values = lax.dot_general(probs.astype(BF16), grad, NN, preferred_element_type=F32)
    grad_keys = lax.dot_general(grad_scores, query, NN, preferred_element_type=F32)
    grad_query = lax.dot_general(keys, grad_scores, TN, preferred_element_type=F32)
    store_rows(gq_ref, seq, sizes, join_heads(jnp.transpose(grad_query), head_dim))
    count = keys.shape[0] // 4
    for j in range(4):
        part = slice(j * count, (j + 1) * count)
        store_rows(gkv_refs[j].at[0], seq, sizes, grad_keys[part].astype(BF16))
        store_rows(gkv_refs[j].at[1], seq, sizes, grad_values[part].astype(BF16))


def attention_specs(rows, keys):
    q_spec = pl.BlockSpec((rows, 128), lambda p, s: (0, p))
    kv_specs = [pl.BlockSpec((2, rows, 128), lambda p, s: (0, 0, p)) for _ in range(4)]
    bias_spec = pl.BlockSpec((1, keys, 1), lambda p, s: (s, 0, 0))
    return q_spec, kv_specs, bias_spec


def attend(queries, key_values, bias, sizes, head_dim):
    rows, width = queries.shape
    seqs, keys = bias.shape[0], bias.shape[1]
    pairs = width // 128
    lanes = 2 * (keys // 4)
    q_spec, kv_specs, bias_spec = attention_specs(rows, keys)
    line = pl.BlockSpec((1, 1, lanes), lambda p, s: (p * seqs + s, 0, 0))
    return pl.pallas_call(
        functools.partial(attend_kernel, sizes, head_dim),
        grid=(pairs, seqs),
        in_specs=[q_spec, *kv_specs, bias_spec],
        out_specs=[q_spec, line, line],
        out_shape=[
            jax.ShapeDtypeStruct((rows, width), BF16),
            jax.ShapeDtypeStruct((pairs * seqs, 1, lanes), F32),
            jax.ShapeDtypeStruct((pairs * seqs, 1, lanes), F32),
        ],
        cost_estimate=pl.CostEstimate(
            flops=pairs * seqs * keys * lanes, bytes_accessed=rows * width, transcendentals=0
        ),
        compiler_params=pltpu.CompilerParams(vmem_limit_bytes=60 << 20),
    )(queries, *key_values, bias)


def attend_back(queries, key_values, bias, norms, grads, sizes, head_dim):
    rows, width = queries.shape
    seqs, keys = bias.shape[0], bias.shape[1]
    pairs = width // 128
    lanes = 2 * (keys // 4)
    q_spec, kv_specs, bias_spec = attention_specs(rows, keys)
    line = pl.BlockSpec((1, 1, lanes), lambda p, s: (p * seqs + s, 0, 0))
    out = pl.pallas_call(
        functools.partial(attend_back_kernel, sizes, head_dim),
        grid=(pairs, seqs),
        in_specs=[q_spec, *kv_specs, bias_spec, line, q_spec],
        out_specs=[q_spec, *kv_specs],
        out_shape=[jax.ShapeDtypeStruct((rows, width), F32)]
        + [jax.ShapeDtypeStruct((2, rows, width), BF16)] * 4,
        cost_estimate=pl.CostEstimate(
            flops=pairs * seqs * keys * lanes, bytes_accessed=rows * width, transcendentals=0
        ),
        compiler_params=pltpu.CompilerParams(vmem_limit_bytes=60 << 20),
    )(queries, *key_values, bias, norms, grads)
    return out[0], out[1:]


def local(
    x_img,
    x_txt,
    cond,
    lengths,
    mod_w,
    qkv_w,
    o_w,
    up_w,
    down_w,
    norm_gain,
    threshold,
    cot_img,
    cot_txt,
):
    shard_count = lax.axis_size("s")
    head_dim = norm_gain.shape[2]
    seqs, img_rows, width = x_img.shape
    txt_real = x_txt.shape[1]
    txt_rows = -(-txt_real // 16) * 16
    sizes = (img_rows, txt_rows, seqs)
    per = seqs * (img_rows + txt_rows)
    feat = mod_w.shape[3]
    block = mod_w.shape[1]
    heads = qkv_w.shape[3] // head_dim
    own = {name: lax.axis_index(name) for name in ("s", "h", "l", "y", "c")}

    source = feature_order(width, shard_count)
    order = one_hot(source)
    count_i = seqs * img_rows

    def arrange(image, text):
        text = jnp.pad(text, ((0, 0), (0, txt_rows - txt_real), (0, 0)))
        both = jnp.concatenate([image.reshape(-1, width), text.reshape(-1, width)], axis=0)
        return jnp.dot(both, order, preferred_element_type=BF16)

    inputs, cot = arrange(x_img, x_txt), arrange(cot_img, cot_txt)

    cond_float = cond.astype(F32)
    cond_act = jax.nn.silu(cond_float).astype(BF16)
    if shard_count == 2:
        cond_all = jnp.concatenate([cond_act, trade(cond_act, "s")], axis=0)
    else:
        cond_all = lax.all_gather(cond_act, "s", axis=0, tiled=True)
    cond_rows = lax.dynamic_index_in_dim(
        cond_all.reshape(cond_all.shape[0], -1, block),
        (own["s"] * 2 + own["h"]) * 2 + own["l"],
        axis=1,
        keepdims=False,
    )
    mod_part = jnp.einsum("sd,tdkf->stkf", cond_rows, mod_w, preferred_element_type=F32)
    if shard_count == 2:
        mod_sum = mod_part[:seqs] + trade(mod_part[seqs:], "s")
    else:
        mod_sum = lax.psum_scatter(mod_part, "s", scatter_dimension=0, tiled=True)
    mod_sum = total_over(mod_sum.reshape(seqs * 12, feat), ("h", "l"))
    mod_full = in_order(in_order(mod_sum, "c", 1), "y", 1)
    modulation = permute_exact(mod_full, order, ((1,), (0,)))

    half = width // 2
    halves = [((per, half), BF16)] * 2
    first_n, first_f, mlp_n, mlp_f = call(
        functools.partial(first_kernel, sizes), halves * 2, inputs, cot, modulation
    )
    first = gather_rows(first_n, first_f)
    cot_rows = gather_rows(mlp_n, mlp_f)
    qkv_near = gather_weight(after(qkv_w.reshape(6, block, -1), mod_sum))
    qkv_far = trade(after(qkv_near, first), "c")
    up_near = gather_weight(after(up_w, first))
    scales = jnp.array([QUERY_SCALE, 1.0], F32)
    gains = jnp.tile(norm_gain * scales[None, :, None], (1, 1, heads)).reshape(4, -1)
    queries, own_kv, raw = qkv_project(*first, qkv_near, qkv_far, gains, sizes, head_dim)
    o_near = gather_weight(after(jnp.swapaxes(o_w, 1, 2), first), own_kv)
    h_kv = trade(own_kv, "h")
    down_near = gather_weight(after(jnp.swapaxes(down_w, 1, 2), own_kv), h_kv)
    o_far = trade(after(o_near, h_kv), "c")
    key_values = [own_kv, trade(own_kv, "c"), h_kv, trade(h_kv, "c")]

    text_bias = []
    for jh, jc in ((0, 0), (0, 1), (1, 0), (1, 1)):
        member = [jnp.zeros((seqs, 4 * img_rows), F32)]
        for jy, jl in ((0, 0), (1, 0), (1, 1), (0, 1)):
            ctx_at = (own["h"] ^ jh) * 2 + (own["l"] ^ jl)
            tp_at = (own["y"] ^ jy) * 2 + (own["c"] ^ jc)
            row = jnp.arange(txt_rows, dtype=jnp.int32)
            slot = (ctx_at * 4 + tp_at) * txt_real + row
            allowed = (row < txt_real)[None, :] & (slot[None, :] < lengths[:, None])
            member.append(jnp.where(allowed, 0.0, MASKED))
        text_bias.append(jnp.concatenate(member, axis=1))
    bias = jnp.concatenate(text_bias, axis=1)[:, :, None]

    attended, log_norm, highest = attend(queries, key_values, bias, sizes, head_dim)
    attn_out, _ = reduce_rows(*project(attended, o_near, o_far, sizes))
    mid, second_n, second_f = call(
        functools.partial(middle_kernel, sizes),
        [((per, width), F32), *halves],
        inputs,
        attn_out,
        modulation,
    )
    second = gather_rows(second_n, second_f)
    up_far = trade(after(up_near, second_n), "c")
    down_far = trade(after(down_near, second), "c")
    hidden, pre_grad = mlp(second, cot_rows, (up_near, up_far), (down_near, down_far), sizes)

    second_parts = project(pre_grad, up_near, up_far, sizes)
    hidden, pre_grad = after((hidden, pre_grad), second_parts)
    down_far_grad = stream_grads(cot_rows[1], hidden, sizes, False)
    up_far_grad = stream_grads(second[1], after(pre_grad, down_far_grad), sizes, False)
    hidden = after(hidden, up_far_grad)
    down_total = stream_grads(cot_rows[0], hidden, sizes, False, trade(down_far_grad, "c"))
    up_total = stream_grads(second[0], pre_grad, sizes, False, trade(up_far_grad, "c"))
    second_grad, arrived = reduce_rows(*second_parts)
    down_shard = shard_grad(after(down_total, arrived))
    up_shard = shard_grad(after(up_total, arrived))
    mid_grad, attn_n, attn_f, two_sums = call(
        functools.partial(middle_back_kernel, sizes),
        [((per, width), F32), *halves, ((6 * seqs, width), F32)],
        mid,
        cot,
        second_grad,
        attn_out,
        modulation,
    )
    attn_rows = gather_rows(attn_n, attn_f)
    (mixed_grad,) = call(
        functools.partial(mixed_kernel, sizes),
        [(attended.shape, BF16)],
        *attn_rows,
        o_near,
        o_far,
    )
    mixed_grad = after(mixed_grad, (down_total, up_total))
    query_sum, kv_grads = attend_back(
        queries, key_values, bias, log_norm, mixed_grad, sizes, head_dim
    )
    h_low = (kv_grads[2].astype(F32) + trade(kv_grads[3], "c").astype(F32)).astype(BF16)
    h_grads = trade(h_low, "h")
    c_grads = trade(kv_grads[1], "c")

    mlp_out, _ = reduce_rows(*project(after(hidden, h_low), down_near, down_far, sizes))
    results, gate_sums = call(
        functools.partial(last_kernel, sizes),
        [((per, width), BF16), ((2 * seqs, width), F32)],
        mid,
        mlp_out,
        cot,
        modulation,
    )
    o_total = pair_grad(attn_rows, after(attended, query_sum), sizes)
    grad_down, grad_up = own_grad(down_shard), own_grad(up_shard)
    grad_o = own_grad(shard_grad(after(o_total, up_shard)))

    low_all, gain_sums = call(
        functools.partial(qkv_back_kernel, sizes, head_dim),
        [((4 * per, 3 * heads * head_dim), BF16), (gains.shape, F32)],
        after(query_sum, (mlp_out, o_total)),
        kv_grads[0],
        c_grads,
        h_grads,
        raw,
        gains,
    )
    gain_terms = jnp.sum(gain_sums.reshape(2, 2, heads, head_dim), axis=2) * scales[None, :, None]
    low_all = after(low_all, (grad_down, grad_up, mlp_out))
    grad_qkv = own_grad(shard_grad(pair_grad(first, low_all, sizes, True)))
    first_grad, _ = reduce_rows(*project(low_all, qkv_near, qkv_far, sizes))
    input_grads, one_sums = call(
        functools.partial(first_back_kernel, sizes),
        [((per, width), F32), ((4 * seqs, width), F32)],
        inputs,
        mid_grad,
        first_grad,
        modulation,
    )

    back = ((1,), (1,))

    def restore(moved):
        return (
            moved[:count_i].reshape(seqs, img_rows, width),
            moved[count_i:].reshape(seqs, txt_rows, width)[:, :txt_real],
        )

    out_img, out_txt = restore(
        lax.dot_general(results, order, (back, ((), ())), preferred_element_type=BF16)
    )
    grad_img, grad_txt = restore(permute_exact(input_grads, order, back))

    lanes = highest.shape[2] // 2
    row = jnp.arange(lanes, dtype=jnp.int32)
    valid = (row < 4 * img_rows) | ((row - 4 * img_rows) % txt_rows < txt_real)
    tops = highest.reshape(-1, seqs, 2, lanes)
    tops = jnp.max(jnp.where(valid, tops, -jnp.inf), axis=(1, 3)).reshape(1, heads)
    places = jnp.arange(4 * heads)[None, :] // heads
    tops = jnp.where(places == own["y"] * 2 + own["l"], jnp.tile(tops, (1, 4)), MASKED)

    count = 2 * seqs
    mod_low = jnp.concatenate(
        [one_sums, two_sums[2 * count :], two_sums[: 2 * count], gate_sums], axis=0
    ).astype(BF16)
    mod_count = mod_low.shape[0]
    mod_low = lax.dot_general(mod_low, order, (back, ((), ())), preferred_element_type=F32)
    extra = [gain_terms.reshape(1, -1), tops]
    extra = jnp.concatenate([jnp.pad(e, ((0, 0), (0, feat - e.shape[1]))) for e in extra])
    extra = jnp.pad(extra, ((0, -(mod_count + 2) % 8), (0, 0)))
    mod_low = jnp.concatenate([mod_low, jnp.tile(extra, (1, width // feat))], axis=0)
    is_top = jnp.arange(mod_low.shape[0])[:, None] == mod_count + 1

    def join(first, second):
        return jnp.where(is_top, jnp.maximum(first, second), first + second)

    quarters = [mod_low[:, k * feat : (k + 1) * feat] for k in range(width // feat)]
    at_c, at_y = own["c"] == 0, own["y"] == 0
    keep = [jnp.where(at_c, quarters[2 * k], quarters[2 * k + 1]) for k in range(2)]
    send = [jnp.where(at_c, quarters[2 * k + 1], quarters[2 * k]) for k in range(2)]
    pair = join(jnp.stack(keep), trade(jnp.stack(send), "c"))
    mod_sum = join(
        jnp.where(at_y, pair[0], pair[1]), trade(jnp.where(at_y, pair[1], pair[0]), "y")
    )
    for axis in ("l", "h"):
        mod_sum = join(mod_sum, trade(mod_sum, axis))
    if shard_count == 2:
        mod_members = jnp.stack([mod_sum, trade(mod_sum, "s")])
    else:
        mod_members = lax.all_gather(mod_sum, "s")
    gain_grad = jnp.sum(mod_members[:, mod_count], axis=0)[: 4 * head_dim]
    gain_grad = gain_grad.reshape(norm_gain.shape)
    tops = jnp.max(mod_members[:, mod_count + 1], axis=0)[: 4 * heads]
    peaks = lax.dynamic_slice_in_dim(tops, (own["y"] * 2 + own["c"]) * heads, heads)
    mod_seqs = mod_members[:, :mod_count].astype(BF16).reshape(-1, 6, 2, seqs, feat)
    mod_seqs = mod_seqs.transpose(2, 0, 3, 1, 4).reshape(2, -1, 6, feat)
    grad_mod = jnp.einsum("sd,tskf->tdkf", cond_rows, mod_seqs, preferred_element_type=F32)
    cond_part = jnp.einsum("tskf,tdkf->sd", mod_seqs, mod_w, preferred_element_type=F32)
    cond_part = in_order(in_order(total_over(cond_part, ("c", "y")), "l", 1), "h", 1)
    if shard_count == 2:
        mine, other = cond_part[:seqs], trade(cond_part[seqs:], "s")
        at_s = own["s"] == 0
        cond_total = jnp.concatenate(
            [jnp.where(at_s, mine, other), jnp.where(at_s, other, mine)], axis=1
        )
    else:
        cond_cols = lax.all_gather(cond_part, "s", axis=1, tiled=True)
        cond_total = lax.dynamic_slice_in_dim(cond_cols, own["s"] * seqs, seqs, axis=0)
    unused, silu_vjp = jax.vjp(jax.nn.silu, cond_float)
    grad_cond = silu_vjp(cond_total)[0]

    factor = jnp.sqrt(threshold / jnp.maximum(peaks, threshold))
    columns = jnp.repeat(factor, head_dim)
    clipped = qkv_w[:, :2].astype(F32) * columns
    return (
        out_img,
        out_txt,
        grad_img,
        grad_txt,
        grad_cond,
        grad_mod,
        grad_qkv,
        jnp.swapaxes(grad_o, 1, 2),
        grad_up,
        jnp.swapaxes(grad_down, 1, 2),
        gain_grad,
        clipped,
        peaks,
    )


def solution(mesh):
    shard, ctx, tp = (mesh.shape[name] for name in ("shard", "ctx", "tp"))
    fine = Mesh(mesh.devices.reshape(shard, ctx // 2, 2, tp // 2, 2), ("s", "h", "l", "y", "c"))
    ctx_axes, tp_axes = ("h", "l"), ("y", "c")
    rows = P("s", ctx_axes + tp_axes, None)
    weight = ("s",) + ctx_axes
    mod = P(None, weight, None, tp_axes)
    qkv = P(None, None, weight, tp_axes)
    inward = P(None, tp_axes, weight)
    outward = P(None, weight, tp_axes)
    return jax.shard_map(
        local,
        mesh=fine,
        in_specs=(
            rows,
            rows,
            P("s", None),
            P("s"),
            mod,
            qkv,
            inward,
            outward,
            inward,
            P(),
            P(),
            rows,
            rows,
        ),
        out_specs=(
            rows,
            rows,
            rows,
            rows,
            P("s", None),
            mod,
            qkv,
            inward,
            outward,
            inward,
            P(),
            qkv,
            P(tp_axes),
        ),
        check_vma=False,
    )
```

time: 1210 us -> 929 us (0.77)
  matrix products: 180 us -> 27.1 us
  blocking collectives: 147 us -> 0 us
  Pallas kernels: 45.7 us -> 173 us
  other arithmetic: 133 us -> 52.5 us
  waiting for transfers between devices: 448 us -> 518 us
  local copies, waits for them, and re-layouts: 102 us -> 43.5 us
  starting transfers between devices: 123 us -> 88 us
    dot_general x91 -> x3, matrix products: 161 us -> 9.56 us  [the longest x2 6.31 us: arrange(): return jnp.dot(both, order, preferred_element_type=BF16)]
    psum x1 -> x0, waiting for transfers between devices: 144 us -> none  [local(): lax.psum(mod_low, ('h', 'l', 'y', 'c')).astype(F32)]
    pallas_call x0 -> x21, Pallas kernels: none -> 127 us  [the longest x8 40.9 us: stream_grads(): pl.pallas_call(functools.partial(grad_kernel, sizes, bool(extra)), grid=(...]
    ppermute x8, waiting for transfers between devices: 2.95 us -> 87.6 us  [cross(): moved = lax.ppermute(values, ('l', 'c'), [(1, 2), (2, 1)])]
    reduce_scatter x0 -> x4, waiting for transfers between devices: none -> 65 us  [shard_grad(): lax.psum_scatter(total, ('s', 'h'), scatter_dimension=total.ndim - 2, til...]
    all_gather x4 -> x0, blocking collectives: 62.4 us -> none  [the longest x1 47.1 us: local(): cond_cols = lax.all_gather(cond_part, ('s', 'h', 'l'), axis=1, tiled=True)]
    psum x2 -> x0, blocking collectives: 52.5 us -> none  [the longest x1 41.8 us: local(): gain_grad = lax.psum(jnp.stack(gain_terms), ('s', 'h', 'l', 'y', 'c'))]
    ppermute x65 -> x62, waiting for transfers between devices: 301 us -> 348 us  [trade(): return lax.ppermute(values, axis, [(0, 1), (1, 0)])]
  transfers between devices with their start and end apart: 74 -> 78, of which waited for: 25 -> 48; matrix products, arithmetic and copies ran while one was open for 27% -> 9% of each run, Pallas kernels for 4% -> 13%
where the time goes in v2:
time: 929 us; the launch traced here: 918 us
  waiting for transfers between devices  518 us (56%)
  Pallas kernels  173 us (19%)
  starting transfers between devices  88 us (9%)
  other arithmetic  52.5 us (6%)
  local copies, waits for them, and re-layouts  43.5 us (5%)
  matrix products  27.1 us (3%)
  between operations  16.5 us (2%)
    ppermute x62, waiting for transfers between devices, trade(): return lax.ppermute(values, axis, [(0, 1), (1, 0)])  348 us
    ppermute x8, waiting for transfers between devices, cross(): moved = lax.ppermute(values, ('l', 'c'), [(1, 2), (2, 1)])  87.6 us
    reduce_scatter x4, waiting for transfers between devices, shard_grad(): lax.psum_scatter(total, ('s', 'h'), scatter_dimension=total.ndim - 2, til...  65 us
    ppermute x62, starting transfers between devices, trade(): return lax.ppermute(values, axis, [(0, 1), (1, 0)])  63.2 us
    pallas_call x8, Pallas kernels, stream_grads(): pl.pallas_call(functools.partial(grad_kernel, sizes, bool(extra)), grid=(...  40.9 us
    pallas_call x4, Pallas kernels, project(): pl.pallas_call(functools.partial(project_kernel, sizes), grid=(half // ti...  37.3 us
    unnamed x184, local copies, waits for them, and re-layouts  33.9 us
    pallas_call x1, Pallas kernels, attend_back(): pl.pallas_call(functools.partial(attend_back_kernel, sizes, head_dim), gr...  27.9 us
  transfers between devices with their start and end apart: 78, of which 48 were waited for; matrix products, arithmetic and copies ran while one was open for 9% of the time, Pallas kernels for 13%

profile of v2, /device:TPU:1, one launch (start us, length us, event | category | flops | bytes accessed | tf_op | source)
XLA Modules:
  0.0 918.5 jit_solution(12380637195466247239)
XLA Ops:
  23.8 7.7 collective-permute-start.10
  31.6 10.7 %collective-permute-done.10 = bf16[6,192,384]{2,1,0:T(8,128)(2,1)S(1)} collective-permute-done((bf16[6,192,384]{2,1,0:T(8,128)(2,1)S(1)}, bf16[6,192,384]{2,1,0:T(8,128)(2,1)S(1)}, u32[]{:S(2)}, u32[]{:S(2)}) %collective-permute-start.10) | collective-permute-done | bytes 884768 | tf_op jit(solution)/shard_map/ppermute | solution.py:25
  71.3 8.1 collective-permute-done.8
  79.7 23.2 %collective-permute-done.7 = bf16[2,240,768]{2,1,0:T(8,128)(2,1)S(1)} collective-permute-done((bf16[2,240,768]{2,1,0:T(8,128)(2,1)S(1)}, bf16[2,240,768]{2,1,0:T(8,128)(2,1)S(1)}, u32[]{:S(2)}, u32[]{:S(2)}) %collective-permute-start.7) | collective-permute-done | bytes 737312 | tf_op jit(solution)/shard_map/ppermute | solution.py:21
  104.4 17.1 %all-gather.5.cloned.1.call-done.refs_0_ = bf16[6,768,384]{2,1,0:T(8,128)(2,1)} async-done(((bf16[6,192,384]{2,1,0:T(8,128)(2,1)}), bf16[6,768,384]{2,1,0:T(8,128)(2,1)}) %all-gather.5.cloned.1.call-update) | async-done | bytes 3538960 | tf_op jit(solution)/shard_map/all_gather | solution.py:83
  133.8 9.8 %shard_map.238 = (bf16[960,384]{1,0:T(8,128)(2,1)S(1)}, bf16[2,960,384]{2,1,0:T(8,128)(2,1)S(1)}, f32[2,960,384]{2,1,0:T(8,128)}) custom-call(bf16[960,768]{1,0:T(8,128)(2,1)S(1)} %copy-done.6, bf16[960,768]{1,0:T(8,128)(2,1)S(1)} %pad_maximum_fusion.1.far_ref.left_ref, bf16[2,3,768,384]{3,2,1,0:T(8,128)(2,1)} %bitcast.151, ...), custom_call_target="tpu_custom_call" | custom-call | flops 1048576 | bytes 1048576 | tf_op jit(solution)/shard_map/pallas_call | solution.py:236
  147.5 33.3 %collective-permute-done.29 = bf16[2,192,1536]{2,1,0:T(8,128)(2,1)S(1)} collective-permute-done((bf16[2,192,1536]{2,1,0:T(8,128)(2,1)}, bf16[2,192,1536]{2,1,0:T(8,128)(2,1)S(1)}, u32[]{:S(2)}, u32[]{:S(2)}) %collective-permute-start.29) | collective-permute-done | bytes 1179680 | tf_op jit(solution)/shard_map/ppermute | solution.py:25
  186.4 26.4 %collective-permute-done.31 = bf16[2,192,1536]{2,1,0:T(8,128)(2,1)S(1)} collective-permute-done((bf16[2,192,1536]{2,1,0:T(8,128)(2,1)}, bf16[2,192,1536]{2,1,0:T(8,128)(2,1)S(1)}, u32[]{:S(2)}, u32[]{:S(2)}) %collective-permute-start.31) | collective-permute-done | bytes 1179680 | tf_op jit(solution)/shard_map/ppermute | solution.py:25
  214.0 41.7 %collective-permute-done.13.refs_3_ = bf16[2,960,384]{2,1,0:T(8,128)(2,1)} collective-permute-done((bf16[2,960,384]{2,1,0:T(8,128)(2,1)}, bf16[2,960,384]{2,1,0:T(8,128)(2,1)}, u32[]{:S(2)}, u32[]{:S(2)}) %collective-permute-start.13) | collective-permute-done | bytes 1474592 | tf_op jit(solution)/shard_map/ppermute | solution.py:21
  261.5 18.3 %shard_map.239 = (bf16[960,384]{1,0:T(8,128)(2,1)}, f32[9,1,640]{2,1,0:T(1,128)}, f32[9,1,640]{2,1,0:T(1,128)}) custom-call(bf16[960,384]{1,0:T(8,128)(2,1)} %copy-done.33, bf16[2,960,384]{2,1,0:T(8,128)(2,1)} %copy-done.25, bf16[2,960,384]{2,1,0:T(8,128)(2,1)} %collective-permute-done.12.refs_2_, bf16[2,960,384]{2,1,0:T(8,128)(2,1)} %collective-permute-done.13.refs_3_, ...), custom_call_target="tpu_custom_call" | custom-call | flops 7372800 | bytes 368640 | tf_op jit(solution)/shard_map/pallas_call | solution.py:534
  286.2 40.9 %collective-permute-done.17 = bf16[2,240,768]{2,1,0:T(8,128)(2,1)S(1)} collective-permute-done((bf16[2,240,768]{2,1,0:T(8,128)(2,1)}, bf16[2,240,768]{2,1,0:T(8,128)(2,1)S(1)}, u32[]{:S(2)}, u32[]{:S(2)}) %collective-permute-start.17) | collective-permute-done | bytes 737312 | tf_op jit(solution)/shard_map/ppermute | solution.py:21
  329.7 8.5 collective-permute-done.18
  338.4 12.6 %collective-permute-done.20 = bf16[240,768]{1,0:T(8,128)(2,1)S(1)} collective-permute-done((bf16[240,768]{1,0:T(8,128)(2,1)S(1)}, bf16[240,768]{1,0:T(8,128)(2,1)S(1)}, u32[]{:S(2)}, u32[]{:S(2)}) %collective-permute-start.20) | collective-permute-done | bytes 368672 | tf_op jit(solution)/shard_map/ppermute | solution.py:21
  353.2 15.2 %collective-permute-done.23 = bf16[240,768]{1,0:T(8,128)(2,1)S(1)} collective-permute-done((bf16[240,768]{1,0:T(8,128)(2,1)S(1)}, bf16[240,768]{1,0:T(8,128)(2,1)S(1)}, u32[]{:S(2)}, u32[]{:S(2)}) %collective-permute-start.23) | collective-permute-done | bytes 368672 | tf_op jit(solution)/shard_map/ppermute | solution.py:21
  375.5 10.6 %collective-permute-done.24 = bf16[2,240,768]{2,1,0:T(8,128)(2,1)} collective-permute-done((bf16[2,240,768]{2,1,0:T(8,128)(2,1)}, bf16[2,240,768]{2,1,0:T(8,128)(2,1)}, u32[]{:S(2)}, u32[]{:S(2)}) %collective-permute-start.24) | collective-permute-done | bytes 737312 | tf_op jit(solution)/shard_map/ppermute | solution.py:21
  388.5 19.1 %collective-permute-done.22 = bf16[2,240,768]{2,1,0:T(8,128)(2,1)} collective-permute-done((bf16[2,240,768]{2,1,0:T(8,128)(2,1)}, bf16[2,240,768]{2,1,0:T(8,128)(2,1)}, u32[]{:S(2)}, u32[]{:S(2)}) %collective-permute-start.22) | collective-permute-done | bytes 737312 | tf_op jit(solution)/shard_map/ppermute | solution.py:21
  414.2 9.2 collective-permute-done.25
  425.9 16.1 %collective-permute-done.26 = bf16[2,240,768]{2,1,0:T(8,128)(2,1)S(1)} collective-permute-done((bf16[2,240,768]{2,1,0:T(8,128)(2,1)S(1)}, bf16[2,240,768]{2,1,0:T(8,128)(2,1)S(1)}, u32[]{:S(2)}, u32[]{:S(2)}) %collective-permute-start.26) | collective-permute-done | bytes 737312 | tf_op jit(solution)/shard_map/ppermute | solution.py:21
  446.6 18.9 %shard_map.242 = (bf16[960,1536]{1,0:T(8,128)(2,1)}, bf16[960,1536]{1,0:T(8,128)(2,1)}) custom-call(bf16[960,768]{1,0:T(8,128)(2,1)} %pad_maximum_fusion.3.sn_ref.left_ref, bf16[960,768]{1,0:T(8,128)(2,1)} %pad_maximum_fusion.4.sf_ref.left_ref, bf16[960,768]{1,0:T(8,128)(2,1)} %pad_maximum_fusion.5.mn_ref.left_ref, ...), custom_call_target="tpu_custom_call" | custom-call | flops 1048576 | bytes 1048576 | tf_op jit(solution)/shard_map/pallas_call | solution.py:323
  465.6 11.2 %shard_map.243 = (bf16[2,240,768]{2,1,0:T(8,128)(2,1)}, f32[2,240,768]{2,1,0:T(8,128)}, bf16[2,240,768]{2,1,0:T(8,128)(2,1)}, f32[2,240,768]{2,1,0:T(8,128)}) custom-call(bf16[960,1536]{1,0:T(8,128)(2,1)} %get-tuple-element.113.rows_ref.right_ref, bf16[2,768,1536]{2,1,0:T(8,128)(2,1)} %all-gather.9.cloned.1.call-done.un_ref.refs_0_, ...), custom_call_target="tpu_custom_call" | custom-call | flops 1048576 | bytes 1048576 | tf_op jit(solution)/shard_map/pallas_call | solution.py:367
  510.5 7.7 collective-permute-done.41.refs_0_
  543.6 7.7 collective-permute-done.36
  569.1 7.4 collective-permute-done.39
  577.8 27.1 %collective-permute-done.38 = bf16[2,240,768]{2,1,0:T(8,128)(2,1)S(1)} collective-permute-done((bf16[2,240,768]{2,1,0:T(8,128)(2,1)S(1)}, bf16[2,240,768]{2,1,0:T(8,128)(2,1)S(1)}, u32[]{:S(2)}, u32[]{:S(2)}) %collective-permute-start.38) | collective-permute-done | bytes 737312 | tf_op jit(solution)/shard_map/ppermute | solution.py:21
  611.3 27.9 %shard_map.250 = (f32[960,384]{1,0:T(8,128)}, bf16[2,960,384]{2,1,0:T(8,128)(2,1)}, bf16[2,960,384]{2,1,0:T(8,128)(2,1)}, bf16[2,960,384]{2,1,0:T(8,128)(2,1)}, bf16[2,960,384]{2,1,0:T(8,128)(2,1)}) custom-call(bf16[960,384]{1,0:T(8,128)(2,1)} %copy-done.33, bf16[2,960,384]{2,1,0:T(8,128)(2,1)} %copy-done.25, ...), custom_call_target="tpu_custom_call" | custom-call | flops 7372800 | bytes 368640 | tf_op jit(solution)/shard_map/pallas_call | solution.py:558
  646.0 11.2 %shard_map.251 = (bf16[2,240,768]{2,1,0:T(8,128)(2,1)}, f32[2,240,768]{2,1,0:T(8,128)}, bf16[2,240,768]{2,1,0:T(8,128)(2,1)}, f32[2,240,768]{2,1,0:T(8,128)}) custom-call(bf16[960,1536]{1,0:T(8,128)(2,1)} %get-tuple-element.121.right_ref.rows_ref, bf16[2,768,1536]{2,1,0:T(8,128)(2,1)} %all-gather.11.cloned.1.call-done.dn_ref.refs_0_, ...), custom_call_target="tpu_custom_call" | custom-call | flops 1048576 | bytes 1048576 | tf_op jit(solution)/shard_map/pallas_call | solution.py:367
  662.5 28.5 %collective-permute-done.44 = bf16[2,240,768]{2,1,0:T(8,128)(2,1)S(1)} collective-permute-done((bf16[2,240,768]{2,1,0:T(8,128)(2,1)}, bf16[2,240,768]{2,1,0:T(8,128)(2,1)S(1)}, u32[]{:S(2)}, u32[]{:S(2)}) %collective-permute-start.44) | collective-permute-done | bytes 737312 | tf_op jit(solution)/shard_map/ppermute | solution.py:21
  702.1 44.2 %reduce-scatter.5.cloned.1.call-done = bf16[2,192,1536]{2,1,0:T(8,128)(2,1)} async-done(((bf16[2,768,1536]{2,1,0:T(8,128)(2,1)}), bf16[2,192,1536]{2,1,0:T(8,128)(2,1)}) %reduce-scatter.5.cloned.1.call-update) | async-done | bytes 1179664 | tf_op jit(solution)/shard_map/reduce_scatter | solution.py:418
  754.9 10.6 %shard_map.255 = (bf16[960,1152]{1,0:T(8,128)(2,1)}, f32[4,384]{1,0:T(4,128)S(1)}) custom-call(f32[960,384]{1,0:T(8,128)S(1)} %copy-done.34, bf16[2,960,384]{2,1,0:T(8,128)(2,1)S(1)} %copy-done.35, bf16[2,960,384]{2,1,0:T(8,128)(2,1)} %collective-permute-done.49.c_ref, bf16[2,960,384]{2,1,0:T(8,128)(2,1)} %collective-permute-done.50.h_ref, ...), custom_call_target="tpu_custom_call" | custom-call | flops 1048576 | bytes 1048576 | tf_op jit(solution)/shard_map/pallas_call | solution.py:194
  775.4 9.9 %shard_map.256 = (bf16[2,240,768]{2,1,0:T(8,128)(2,1)}, f32[2,240,768]{2,1,0:T(8,128)}, bf16[2,240,768]{2,1,0:T(8,128)(2,1)}, f32[2,240,768]{2,1,0:T(8,128)}) custom-call(bf16[960,1152]{1,0:T(8,128)(2,1)} %get-tuple-element.137.rows_ref.right_ref, bf16[6,768,384]{2,1,0:T(8,128)(2,1)} %all-gather.5.cloned.1.call-done.refs_0_, ...), custom_call_target="tpu_custom_call" | custom-call | flops 1048576 | bytes 1048576 | tf_op jit(solution)/shard_map/pallas_call | solution.py:367
  874.6 20.8 %reduce-scatter.9.cloned.1.call-done = bf16[2,3,192,384]{3,2,1,0:T(8,128)(2,1)} async-done(((bf16[2,3,768,384]{3,2,1,0:T(8,128)(2,1)}), bf16[2,3,192,384]{3,2,1,0:T(8,128)(2,1)}) %reduce-scatter.9.cloned.1.call-update) | async-done | bytes 884752 | tf_op jit(solution)/shard_map/reduce_scatter | solution.py:418
  899.0 11.1 %collective-permute-done.68 = bf16[2,3,192,384]{3,2,1,0:T(8,128)(2,1)S(1)} collective-permute-done((bf16[2,3,192,384]{3,2,1,0:T(8,128)(2,1)}, bf16[2,3,192,384]{3,2,1,0:T(8,128)(2,1)S(1)}, u32[]{:S(2)}, u32[]{:S(2)}) %collective-permute-start.68) | collective-permute-done | bytes 884768 | tf_op jit(solution)/shard_map/ppermute | solution.py:25
  (488 shorter events, 329.3 us)
Async XLA Ops:
  7.2 114.3 %all-gather.5.cloned.1.call-start = ((), (), s32[]{:S(2)}) async-start(), calls=%async_computation.4 | async-start | bytes 4423680 | tf_op jit(solution)/shard_map/all_gather | solution.py:83
  43.3 213.0 %all-gather.7.cloned.1.call-start = ((), (), s32[]{:S(2)}) async-start(), calls=%async_computation.5 | async-start | bytes 1474560 | tf_op jit(solution)/shard_map/all_gather | solution.py:83
  68.6 34.3 %collective-permute-start.7 = (bf16[2,240,768]{2,1,0:T(8,128)(2,1)S(1)}, bf16[2,240,768]{2,1,0:T(8,128)(2,1)S(1)}, u32[]{:S(2)}, u32[]{:S(2)}) collective-permute-start(bf16[2,240,768]{2,1,0:T(8,128)(2,1)S(1)} %pad_maximum_fusion.12), channel_id=1, source_target_pairs={{0,4},{4,0},{1,5},{5,1},{2,6},{6,2},{3,7},{7,3},{8,12},{12,8},{9,1... | collective-permute-start | bytes 2211848 | tf_op jit(solution)/shard_map/ppermute | solution.py:21
  79.5 24.8 %collective-permute-start.9 = (bf16[2,240,768]{2,1,0:T(8,128)(2,1)S(1)}, bf16[2,240,768]{2,1,0:T(8,128)(2,1)S(1)}, u32[]{:S(2)}, u32[]{:S(2)}) collective-permute-start(bf16[2,240,768]{2,1,0:T(8,128)(2,1)S(1)} %pad_maximum_fusion.13), channel_id=1, source_target_pairs={{0,2},{2,0},{1,3},{3,1},{4,6},{6,4},{5,7},{7,5},{8,10},{10,8},{9,1... | collective-permute-start | bytes 2211848 | tf_op jit(solution)/shard_map/ppermute | solution.py:21
  145.5 228.0 %all-gather.9.cloned.1.call-start = ((), (), s32[]{:S(2)}) async-start(), calls=%async_computation.6 | async-start | bytes 5898240 | tf_op jit(solution)/shard_map/all_gather | solution.py:83
  145.6 35.3 %collective-permute-start.29 = (bf16[2,192,1536]{2,1,0:T(8,128)(2,1)}, bf16[2,192,1536]{2,1,0:T(8,128)(2,1)S(1)}, u32[]{:S(2)}, u32[]{:S(2)}) collective-permute-start(bf16[2,192,1536]{2,1,0:T(8,128)(2,1)} %param.21), channel_id=1, source_target_pairs={{1,4},{4,1},{3,6},{6,3},{9,12},{12,9},{11,14},{14,11},{17,20},{20,... | collective-permute-start | bytes 3538952 | tf_op jit(solution)/shard_map/ppermute | solution.py:25
  182.0 228.0 %all-gather.11.cloned.1.call-start = ((), (), s32[]{:S(2)}) async-start(), calls=%async_computation.7 | async-start | bytes 5898240 | tf_op jit(solution)/shard_map/all_gather | solution.py:83
  182.1 30.8 %collective-permute-start.31 = (bf16[2,192,1536]{2,1,0:T(8,128)(2,1)}, bf16[2,192,1536]{2,1,0:T(8,128)(2,1)S(1)}, u32[]{:S(2)}, u32[]{:S(2)}) collective-permute-start(bf16[2,192,1536]{2,1,0:T(8,128)(2,1)} %bitcast.165), channel_id=1, source_target_pairs={{1,4},{4,1},{3,6},{6,3},{9,12},{12,9},{11,14},{14,11},{17,20},{20,... | collective-permute-start | bytes 3538952 | tf_op jit(solution)/shard_map/ppermute | solution.py:25
  186.3 69.3 %collective-permute-start.13 = (bf16[2,960,384]{2,1,0:T(8,128)(2,1)}, bf16[2,960,384]{2,1,0:T(8,128)(2,1)}, u32[]{:S(2)}, u32[]{:S(2)}) collective-permute-start(bf16[2,960,384]{2,1,0:T(8,128)(2,1)} %copy-done.25), channel_id=1, source_target_pairs={{0,8},{8,0},{1,9},{9,1},{2,10},{10,2},{3,11},{11,3},{4,12},{12,4},... | collective-permute-start | bytes 4423688 | tf_op jit(solution)/shard_map/ppermute | solution.py:21
  255.7 437.7 %reduce-scatter.7.cloned.1.call-start = ((), (), s32[]{:S(2)}) async-start(), calls=%async_computation.9 | async-start | bytes 5898240 | tf_op jit(solution)/shard_map/reduce_scatter | solution.py:418
  256.3 23.5 %collective-permute-start.16 = (bf16[2,768,384]{2,1,0:T(8,128)(2,1)}, bf16[2,768,384]{2,1,0:T(8,128)(2,1)}, u32[]{:S(2)}, u32[]{:S(2)}) collective-permute-start(bf16[2,768,384]{2,1,0:T(8,128)(2,1)} %all-gather.7.cloned.1.call-done.refs_0_.wn_ref), channel_id=1, source_target_pairs={{0,1},{1,0},{2,3},{3,2},{4,5},{5,4},{6,7},{7,6},{8,9},{9,8},{10,11... | collective-permute-start | bytes 3538952 | tf_op jit(solution)/shard_map/ppermute | solution.py:21
  284.8 42.2 %collective-permute-start.17 = (bf16[2,240,768]{2,1,0:T(8,128)(2,1)}, bf16[2,240,768]{2,1,0:T(8,128)(2,1)S(1)}, u32[]{:S(2)}, u32[]{:S(2)}) collective-permute-start(bf16[2,240,768]{2,1,0:T(8,128)(2,1)} %get-tuple-element.92), channel_id=1, source_target_pairs={{0,4},{4,0},{1,5},{5,1},{2,6},{6,2},{3,7},{7,3},{8,12},{12,8},{9,1... | collective-permute-start | bytes 2211848 | tf_op jit(solution)/shard_map/ppermute | solution.py:21
  284.8 44.7 %collective-permute-start.19 = (bf16[2,240,768]{2,1,0:T(8,128)(2,1)}, bf16[2,240,768]{2,1,0:T(8,128)(2,1)S(1)}, u32[]{:S(2)}, u32[]{:S(2)}) collective-permute-start(bf16[2,240,768]{2,1,0:T(8,128)(2,1)} %get-tuple-element.94), channel_id=1, source_target_pairs={{0,2},{2,0},{1,3},{3,1},{4,6},{6,4},{5,7},{7,5},{8,10},{10,8},{9,1... | collective-permute-start | bytes 2211848 | tf_op jit(solution)/shard_map/ppermute | solution.py:21
  371.2 36.4 %collective-permute-start.22 = (bf16[2,240,768]{2,1,0:T(8,128)(2,1)}, bf16[2,240,768]{2,1,0:T(8,128)(2,1)}, u32[]{:S(2)}, u32[]{:S(2)}) collective-permute-start(bf16[2,240,768]{2,1,0:T(8,128)(2,1)} %pad_maximum_fusion.14), channel_id=1, source_target_pairs={{0,4},{4,0},{1,5},{5,1},{2,6},{6,2},{3,7},{7,3},{8,12},{12,8},{9,1... | collective-permute-start | bytes 2211848 | tf_op jit(solution)/shard_map/ppermute | solution.py:21
  373.6 70.9 %collective-permute-start.30 = (bf16[2,768,1536]{2,1,0:T(8,128)(2,1)}, bf16[2,768,1536]{2,1,0:T(8,128)(2,1)}, u32[]{:S(2)}, u32[]{:S(2)}) collective-permute-start(bf16[2,768,1536]{2,1,0:T(8,128)(2,1)} %all-gather.9.cloned.1.call-done.un_ref.refs_0_), channel_id=1, source_target_pairs={{0,1},{1,0},{2,3},{3,2},{4,5},{5,4},{6,7},{7,6},{8,9},{9,8},{10,11... | collective-permute-start | bytes 14155784 | tf_op jit(solution)/shard_map/ppermute | solution.py:21
  410.0 34.5 %collective-permute-start.32 = (bf16[2,768,1536]{2,1,0:T(8,128)(2,1)}, bf16[2,768,1536]{2,1,0:T(8,128)(2,1)S(1)}, u32[]{:S(2)}, u32[]{:S(2)}) collective-permute-start(bf16[2,768,1536]{2,1,0:T(8,128)(2,1)} %all-gather.11.cloned.1.call-done.dn_ref.refs_0_), channel_id=1, source_target_pairs={{0,1},{1,0},{2,3},{3,2},{4,5},{5,4},{6,7},{7,6},{8,9},{9,8},{10,11... | collective-permute-start | bytes 14155784 | tf_op jit(solution)/shard_map/ppermute | solution.py:21
  509.3 237.0 %reduce-scatter.5.cloned.1.call-start = ((), (), s32[]{:S(2)}) async-start(), calls=%async_computation.8 | async-start | bytes 5898240 | tf_op jit(solution)/shard_map/reduce_scatter | solution.py:418
  531.1 329.8 %reduce-scatter.11.cloned.1.call-start = ((), (), s32[]{:S(2)}) async-start(), calls=%async_computation.11 | async-start | bytes 1474560 | tf_op jit(solution)/shard_map/reduce_scatter | solution.py:418
  567.0 38.0 %collective-permute-start.38 = (bf16[2,240,768]{2,1,0:T(8,128)(2,1)S(1)}, bf16[2,240,768]{2,1,0:T(8,128)(2,1)S(1)}, u32[]{:S(2)}, u32[]{:S(2)}) collective-permute-start(bf16[2,240,768]{2,1,0:T(8,128)(2,1)S(1)} %pad_maximum_fusion.18), channel_id=1, source_target_pairs={{0,4},{4,0},{1,5},{5,1},{2,6},{6,2},{3,7},{7,3},{8,12},{12,8},{9,1... | collective-permute-start | bytes 2211848 | tf_op jit(solution)/shard_map/ppermute | solution.py:21
  576.6 28.5 %collective-permute-start.40 = (bf16[2,240,768]{2,1,0:T(8,128)(2,1)S(1)}, bf16[2,240,768]{2,1,0:T(8,128)(2,1)S(1)}, u32[]{:S(2)}, u32[]{:S(2)}) collective-permute-start(bf16[2,240,768]{2,1,0:T(8,128)(2,1)S(1)} %pad_maximum_fusion.19), channel_id=1, source_target_pairs={{0,2},{2,0},{1,3},{3,1},{4,6},{6,4},{5,7},{7,5},{8,10},{10,8},{9,1... | collective-permute-start | bytes 2211848 | tf_op jit(solution)/shard_map/ppermute | solution.py:21
  657.2 33.8 %collective-permute-start.44 = (bf16[2,240,768]{2,1,0:T(8,128)(2,1)}, bf16[2,240,768]{2,1,0:T(8,128)(2,1)S(1)}, u32[]{:S(2)}, u32[]{:S(2)}) collective-permute-start(bf16[2,240,768]{2,1,0:T(8,128)(2,1)} %get-tuple-element.123), channel_id=1, source_target_pairs={{0,4},{4,0},{1,5},{5,1},{2,6},{6,2},{3,7},{7,3},{8,12},{12,8},{9,1... | collective-permute-start | bytes 2211848 | tf_op jit(solution)/shard_map/ppermute | solution.py:21
  659.2 38.2 %collective-permute-start.48 = (bf16[2,768,384]{2,1,0:T(8,128)(2,1)}, bf16[2,768,384]{2,1,0:T(8,128)(2,1)}, u32[]{:S(2)}, u32[]{:S(2)}) collective-permute-start(bf16[2,768,384]{2,1,0:T(8,128)(2,1)} %shard_map.253), channel_id=1, source_target_pairs={{0,1},{1,0},{2,3},{3,2},{4,5},{5,4},{6,7},{7,6},{8,9},{9,8},{10,11... | collective-permute-start | bytes 3538952 | tf_op jit(solution)/shard_map/ppermute | solution.py:21
  659.7 33.7 %collective-permute-start.46 = (bf16[2,240,768]{2,1,0:T(8,128)(2,1)S(1)}, bf16[2,240,768]{2,1,0:T(8,128)(2,1)}, u32[]{:S(2)}, u32[]{:S(2)}) collective-permute-start(bf16[2,240,768]{2,1,0:T(8,128)(2,1)S(1)} %copy-done.88), channel_id=1, source_target_pairs={{0,2},{2,0},{1,3},{3,1},{4,6},{6,4},{5,7},{7,5},{8,10},{10,8},{9,1... | collective-permute-start | bytes 2211848 | tf_op jit(solution)/shard_map/ppermute | solution.py:21
  660.7 92.0 %collective-permute-start.49 = (bf16[2,960,384]{2,1,0:T(8,128)(2,1)}, bf16[2,960,384]{2,1,0:T(8,128)(2,1)}, u32[]{:S(2)}, u32[]{:S(2)}) collective-permute-start(bf16[2,960,384]{2,1,0:T(8,128)(2,1)} %get-tuple-element.132), channel_id=1, source_target_pairs={{0,1},{1,0},{2,3},{3,2},{4,5},{5,4},{6,7},{7,6},{8,9},{9,8},{10,11... | collective-permute-start | bytes 4423688 | tf_op jit(solution)/shard_map/ppermute | solution.py:21
  660.9 94.0 %collective-permute-start.50 = (bf16[2,960,384]{2,1,0:T(8,128)(2,1)}, bf16[2,960,384]{2,1,0:T(8,128)(2,1)}, u32[]{:S(2)}, u32[]{:S(2)}) collective-permute-start(bf16[2,960,384]{2,1,0:T(8,128)(2,1)} %add_convert_fusion), channel_id=1, source_target_pairs={{0,8},{8,0},{1,9},{9,1},{2,10},{10,2},{3,11},{11,3},{4,12},{12,4},... | collective-permute-start | bytes 4423688 | tf_op jit(solution)/shard_map/ppermute | solution.py:21
  693.4 72.1 %collective-permute-start.52 = (bf16[2,192,1536]{2,1,0:T(8,128)(2,1)}, bf16[2,192,1536]{2,1,0:T(8,128)(2,1)}, u32[]{:S(2)}, u32[]{:S(2)}) collective-permute-start(bf16[2,192,1536]{2,1,0:T(8,128)(2,1)} %reduce-scatter.7.cloned.1.call-done), channel_id=1, source_target_pairs={{1,4},{4,1},{3,6},{6,3},{9,12},{12,9},{11,14},{14,11},{17,20},{20,... | collective-permute-start | bytes 3538952 | tf_op jit(solution)/shard_map/ppermute | solution.py:25
  697.5 52.7 %collective-permute-start.47 = (bf16[240,768]{1,0:T(8,128)(2,1)}, bf16[240,768]{1,0:T(8,128)(2,1)}, u32[]{:S(2)}, u32[]{:S(2)}) collective-permute-start(bf16[240,768]{1,0:T(8,128)(2,1)} %fusion.42), channel_id=1, source_target_pairs={{0,4},{4,0},{1,5},{5,1},{2,6},{6,2},{3,7},{7,3},{8,12},{12,8},{9,1... | collective-permute-start | bytes 1105928 | tf_op jit(solution)/shard_map/ppermute | solution.py:21
  775.3 120.1 %reduce-scatter.9.cloned.1.call-start = ((), (), s32[]{:S(2)}) async-start(), calls=%async_computation.10 | async-start | bytes 4423680 | tf_op jit(solution)/shard_map/reduce_scatter | solution.py:418
  785.2 24.9 %collective-permute-start.53 = (bf16[2,240,768]{2,1,0:T(8,128)(2,1)}, bf16[2,240,768]{2,1,0:T(8,128)(2,1)}, u32[]{:S(2)}, u32[]{:S(2)}) collective-permute-start(bf16[2,240,768]{2,1,0:T(8,128)(2,1)} %get-tuple-element.139), channel_id=1, source_target_pairs={{0,4},{4,0},{1,5},{5,1},{2,6},{6,2},{3,7},{7,3},{8,12},{12,8},{9,1... | collective-permute-start | bytes 2211848 | tf_op jit(solution)/shard_map/ppermute | solution.py:21
  786.3 26.5 %collective-permute-start.55 = (bf16[2,240,768]{2,1,0:T(8,128)(2,1)}, bf16[2,240,768]{2,1,0:T(8,128)(2,1)}, u32[]{:S(2)}, u32[]{:S(2)}) collective-permute-start(bf16[2,240,768]{2,1,0:T(8,128)(2,1)} %get-tuple-element.141), channel_id=1, source_target_pairs={{0,2},{2,0},{1,3},{3,1},{4,6},{6,4},{5,7},{7,5},{8,10},{10,8},{9,1... | collective-permute-start | bytes 2211848 | tf_op jit(solution)/shard_map/ppermute | solution.py:21
  860.9 36.6 %collective-permute-start.69 = (bf16[2,192,384]{2,1,0:T(8,128)(2,1)}, bf16[2,192,384]{2,1,0:T(8,128)(2,1)S(1)}, u32[]{:S(2)}, u32[]{:S(2)}) collective-permute-start(bf16[2,192,384]{2,1,0:T(8,128)(2,1)} %reduce-scatter.11.cloned.1.call-done), channel_id=1, source_target_pairs={{1,4},{4,1},{3,6},{6,3},{9,12},{12,9},{11,14},{14,11},{17,20},{20,... | collective-permute-start | bytes 884744 | tf_op jit(solution)/shard_map/ppermute | solution.py:25
  873.4 24.9 %collective-permute-start.66 = (f32[3,768]{1,0:T(4,128)S(1)}, f32[3,768]{1,0:T(4,128)S(1)}, u32[]{:S(2)}, u32[]{:S(2)}) collective-permute-start(f32[3,768]{1,0:T(4,128)S(1)} %pad_maximum_fusion.27), channel_id=1, source_target_pairs={{0,16},{16,0},{1,17},{17,1},{2,18},{18,2},{3,19},{19,3},{4,20},{20... | collective-permute-start | bytes 27656 | tf_op jit(solution)/shard_map/ppermute | solution.py:21
  (135 other events, 1207.5 us)
Sparse Core Ops, SparseCore 0:
  43.4 77.9 all-gather.4
  145.6 50.0 all-gather.6
  198.1 111.8 all-gather.8
  312.3 94.7 all-gather.10
  509.4 94.7 reduce-scatter.6
  607.0 139.1 reduce-scatter.4
  775.4 38.4 reduce-scatter.10
  817.0 78.3 reduce-scatter.8

commit v3 on v2

--- a/solution.py
+++ b/solution.py
@@ -675,16 +675,14 @@
     down_far = trade(after(down_near, second), "c")
     hidden, pre_grad = mlp(second, cot_rows, (up_near, up_far), (down_near, down_far), sizes)
 
-    second_parts = project(pre_grad, up_near, up_far, sizes)
-    hidden, pre_grad = after((hidden, pre_grad), second_parts)
     down_far_grad = stream_grads(cot_rows[1], hidden, sizes, False)
     up_far_grad = stream_grads(second[1], after(pre_grad, down_far_grad), sizes, False)
     hidden = after(hidden, up_far_grad)
     down_total = stream_grads(cot_rows[0], hidden, sizes, False, trade(down_far_grad, "c"))
     up_total = stream_grads(second[0], pre_grad, sizes, False, trade(up_far_grad, "c"))
-    second_grad, arrived = reduce_rows(*second_parts)
-    down_shard = shard_grad(after(down_total, arrived))
-    up_shard = shard_grad(after(up_total, arrived))
+    pre_grad = after(pre_grad, (down_total, up_total))
+    second_grad, _ = reduce_rows(*project(pre_grad, up_near, up_far, sizes))
+    down_shard, up_shard = shard_grad(down_total), shard_grad(up_total)
     mid_grad, attn_n, attn_f, two_sums = call(
         functools.partial(middle_back_kernel, sizes),
         [((per, width), F32), *halves, ((6 * seqs, width), F32)],

time: 929 us -> 917 us (0.987)
    reduce_scatter x4, waiting for transfers between devices: 65 us -> 21 us  [shard_grad(): lax.psum_scatter(total, ('s', 'h'), scatter_dimension=total.ndim - 2, til...]
    all_gather x4, waiting for transfers between devices: 17.1 us -> 37.1 us  [gather_weight(): return lax.all_gather(own, ('s', 'h'), axis=1, tiled=True)]
    ppermute x62, waiting for transfers between devices: 348 us -> 361 us  [trade(): return lax.ppermute(values, axis, [(0, 1), (1, 0)])]
  transfers between devices with their start and end apart: 78 -> 78, of which waited for: 48 -> 52; matrix products, arithmetic and copies ran while one was open for 9% -> 9% of each run, Pallas kernels for 13% -> 14%
where the time goes in v3:
time: 917 us; the launch traced here: 906 us
  waiting for transfers between devices  510 us (56%)
  Pallas kernels  174 us (19%)
  starting transfers between devices  86.6 us (9%)
  other arithmetic  49.6 us (5%)
  local copies, waits for them, and re-layouts  42.2 us (5%)
  matrix products  27.1 us (3%)
  between operations  16.4 us (2%)
    ppermute x62, waiting for transfers between devices, trade(): return lax.ppermute(values, axis, [(0, 1), (1, 0)])  361 us
    ppermute x8, waiting for transfers between devices, cross(): moved = lax.ppermute(values, ('l', 'c'), [(1, 2), (2, 1)])  91 us
    ppermute x62, starting transfers between devices, trade(): return lax.ppermute(values, axis, [(0, 1), (1, 0)])  58.8 us
    pallas_call x8, Pallas kernels, stream_grads(): pl.pallas_call(functools.partial(grad_kernel, sizes, bool(extra)), grid=(...  40.9 us
    pallas_call x4, Pallas kernels, project(): pl.pallas_call(functools.partial(project_kernel, sizes), grid=(half // ti...  38.4 us
    all_gather x4, waiting for transfers between devices, gather_weight(): return lax.all_gather(own, ('s', 'h'), axis=1, tiled=True)  37.1 us
    unnamed x184, local copies, waits for them, and re-layouts  33.2 us
    ppermute x8, starting transfers between devices, cross(): moved = lax.ppermute(values, ('l', 'c'), [(1, 2), (2, 1)])  27.5 us
  transfers between devices with their start and end apart: 78, of which 52 were waited for; matrix products, arithmetic and copies ran while one was open for 9% of the time, Pallas kernels for 14%

profile of v3, /device:TPU:1, one launch (start us, length us, event | category | flops | bytes accessed | tf_op | source)
XLA Modules:
  0.0 906.0 jit_solution(16047104026377811178)
XLA Ops:
  31.6 10.7 %collective-permute-done.10 = bf16[6,192,384]{2,1,0:T(8,128)(2,1)S(1)} collective-permute-done((bf16[6,192,384]{2,1,0:T(8,128)(2,1)S(1)}, bf16[6,192,384]{2,1,0:T(8,128)(2,1)S(1)}, u32[]{:S(2)}, u32[]{:S(2)}) %collective-permute-start.10) | collective-permute-done | bytes 884768 | tf_op jit(solution)/shard_map/ppermute | solution.py:25
  71.3 8.1 collective-permute-done.8
  79.7 23.2 %collective-permute-done.7 = bf16[2,240,768]{2,1,0:T(8,128)(2,1)S(1)} collective-permute-done((bf16[2,240,768]{2,1,0:T(8,128)(2,1)S(1)}, bf16[2,240,768]{2,1,0:T(8,128)(2,1)S(1)}, u32[]{:S(2)}, u32[]{:S(2)}) %collective-permute-start.7) | collective-permute-done | bytes 737312 | tf_op jit(solution)/shard_map/ppermute | solution.py:21
  104.4 17.1 %all-gather.5.cloned.1.call-done.refs_0_ = bf16[6,768,384]{2,1,0:T(8,128)(2,1)} async-done(((bf16[6,192,384]{2,1,0:T(8,128)(2,1)}), bf16[6,768,384]{2,1,0:T(8,128)(2,1)}) %all-gather.5.cloned.1.call-update) | async-done | bytes 3538960 | tf_op jit(solution)/shard_map/all_gather | solution.py:83
  133.8 9.8 %shard_map.238 = (bf16[960,384]{1,0:T(8,128)(2,1)S(1)}, bf16[2,960,384]{2,1,0:T(8,128)(2,1)S(1)}, f32[2,960,384]{2,1,0:T(8,128)}) custom-call(bf16[960,768]{1,0:T(8,128)(2,1)S(1)} %copy-done.7, bf16[960,768]{1,0:T(8,128)(2,1)S(1)} %pad_maximum_fusion.1.far_ref.left_ref, bf16[2,3,768,384]{3,2,1,0:T(8,128)(2,1)} %bitcast.151, ...), custom_call_target="tpu_custom_call" | custom-call | flops 1048576 | bytes 1048576 | tf_op jit(solution)/shard_map/pallas_call | solution.py:236
  147.5 33.3 %collective-permute-done.29 = bf16[2,192,1536]{2,1,0:T(8,128)(2,1)S(1)} collective-permute-done((bf16[2,192,1536]{2,1,0:T(8,128)(2,1)}, bf16[2,192,1536]{2,1,0:T(8,128)(2,1)S(1)}, u32[]{:S(2)}, u32[]{:S(2)}) %collective-permute-start.29) | collective-permute-done | bytes 1179680 | tf_op jit(solution)/shard_map/ppermute | solution.py:25
  186.5 26.4 %collective-permute-done.31 = bf16[2,192,1536]{2,1,0:T(8,128)(2,1)S(1)} collective-permute-done((bf16[2,192,1536]{2,1,0:T(8,128)(2,1)}, bf16[2,192,1536]{2,1,0:T(8,128)(2,1)S(1)}, u32[]{:S(2)}, u32[]{:S(2)}) %collective-permute-start.31) | collective-permute-done | bytes 1179680 | tf_op jit(solution)/shard_map/ppermute | solution.py:25
  214.0 41.7 %collective-permute-done.13.refs_3_ = bf16[2,960,384]{2,1,0:T(8,128)(2,1)} collective-permute-done((bf16[2,960,384]{2,1,0:T(8,128)(2,1)}, bf16[2,960,384]{2,1,0:T(8,128)(2,1)}, u32[]{:S(2)}, u32[]{:S(2)}) %collective-permute-start.13) | collective-permute-done | bytes 1474592 | tf_op jit(solution)/shard_map/ppermute | solution.py:21
  261.6 18.2 %shard_map.239 = (bf16[960,384]{1,0:T(8,128)(2,1)}, f32[9,1,640]{2,1,0:T(1,128)}, f32[9,1,640]{2,1,0:T(1,128)}) custom-call(bf16[960,384]{1,0:T(8,128)(2,1)} %copy-done.34, bf16[2,960,384]{2,1,0:T(8,128)(2,1)} %copy-done.26, bf16[2,960,384]{2,1,0:T(8,128)(2,1)} %collective-permute-done.12.refs_2_, bf16[2,960,384]{2,1,0:T(8,128)(2,1)} %collective-permute-done.13.refs_3_, ...), custom_call_target="tpu_custom_call" | custom-call | flops 7372800 | bytes 368640 | tf_op jit(solution)/shard_map/pallas_call | solution.py:534
  286.2 16.9 %collective-permute-done.19 = bf16[2,240,768]{2,1,0:T(8,128)(2,1)S(1)} collective-permute-done((bf16[2,240,768]{2,1,0:T(8,128)(2,1)}, bf16[2,240,768]{2,1,0:T(8,128)(2,1)S(1)}, u32[]{:S(2)}, u32[]{:S(2)}) %collective-permute-start.19) | collective-permute-done | bytes 737312 | tf_op jit(solution)/shard_map/ppermute | solution.py:21
  304.5 22.6 %collective-permute-done.17 = bf16[2,240,768]{2,1,0:T(8,128)(2,1)S(1)} collective-permute-done((bf16[2,240,768]{2,1,0:T(8,128)(2,1)}, bf16[2,240,768]{2,1,0:T(8,128)(2,1)S(1)}, u32[]{:S(2)}, u32[]{:S(2)}) %collective-permute-start.17) | collective-permute-done | bytes 737312 | tf_op jit(solution)/shard_map/ppermute | solution.py:21
  340.1 7.8 collective-permute-done.21
  349.0 9.4 %collective-permute-done.23 = bf16[240,768]{1,0:T(8,128)(2,1)S(1)} collective-permute-done((bf16[240,768]{1,0:T(8,128)(2,1)S(1)}, bf16[240,768]{1,0:T(8,128)(2,1)S(1)}, u32[]{:S(2)}, u32[]{:S(2)}) %collective-permute-start.23) | collective-permute-done | bytes 368672 | tf_op jit(solution)/shard_map/ppermute | solution.py:21
  362.3 20.0 %collective-permute-done.22 = bf16[2,240,768]{2,1,0:T(8,128)(2,1)} collective-permute-done((bf16[2,240,768]{2,1,0:T(8,128)(2,1)}, bf16[2,240,768]{2,1,0:T(8,128)(2,1)}, u32[]{:S(2)}, u32[]{:S(2)}) %collective-permute-start.22) | collective-permute-done | bytes 737312 | tf_op jit(solution)/shard_map/ppermute | solution.py:21
  387.3 20.0 %all-gather.11.cloned.1.call-done.dn_ref.refs_0_ = bf16[2,768,1536]{2,1,0:T(8,128)(2,1)} async-done(((bf16[2,192,1536]{2,1,0:T(8,128)(2,1)}), bf16[2,768,1536]{2,1,0:T(8,128)(2,1)}) %all-gather.11.cloned.1.call-update) | async-done | bytes 4718608 | tf_op jit(solution)/shard_map/all_gather | solution.py:83
  409.3 9.2 %collective-permute-done.25 = bf16[240,768]{1,0:T(8,128)(2,1)S(1)} collective-permute-done((bf16[240,768]{1,0:T(8,128)(2,1)}, bf16[240,768]{1,0:T(8,128)(2,1)S(1)}, u32[]{:S(2)}, u32[]{:S(2)}) %collective-permute-start.25) | collective-permute-done | bytes 368672 | tf_op jit(solution)/shard_map/ppermute | solution.py:21
  421.0 15.8 %collective-permute-done.26 = bf16[2,240,768]{2,1,0:T(8,128)(2,1)S(1)} collective-permute-done((bf16[2,240,768]{2,1,0:T(8,128)(2,1)S(1)}, bf16[2,240,768]{2,1,0:T(8,128)(2,1)S(1)}, u32[]{:S(2)}, u32[]{:S(2)}) %collective-permute-start.26) | collective-permute-done | bytes 737312 | tf_op jit(solution)/shard_map/ppermute | solution.py:21
  441.5 18.9 %shard_map.242 = (bf16[960,1536]{1,0:T(8,128)(2,1)}, bf16[960,1536]{1,0:T(8,128)(2,1)}) custom-call(bf16[960,768]{1,0:T(8,128)(2,1)} %pad_maximum_fusion.3.sn_ref.left_ref, bf16[960,768]{1,0:T(8,128)(2,1)} %pad_maximum_fusion.4.sf_ref.left_ref, bf16[960,768]{1,0:T(8,128)(2,1)} %pad_maximum_fusion.5.mn_ref.left_ref, ...), custom_call_target="tpu_custom_call" | custom-call | flops 1048576 | bytes 1048576 | tf_op jit(solution)/shard_map/pallas_call | solution.py:323
  507.3 11.1 %shard_map.247 = (bf16[2,240,768]{2,1,0:T(8,128)(2,1)}, f32[2,240,768]{2,1,0:T(8,128)}, bf16[2,240,768]{2,1,0:T(8,128)(2,1)}, f32[2,240,768]{2,1,0:T(8,128)}) custom-call(bf16[960,1536]{1,0:T(8,128)(2,1)} %get-tuple-element.107.right_ref.rows_ref, bf16[2,768,1536]{2,1,0:T(8,128)(2,1)} %all-gather.9.cloned.1.call-done.un_ref.refs_0_, ...), custom_call_target="tpu_custom_call" | custom-call | flops 1048576 | bytes 1048576 | tf_op jit(solution)/shard_map/pallas_call | solution.py:367
  520.3 16.2 %collective-permute-done.37 = bf16[2,240,768]{2,1,0:T(8,128)(2,1)S(1)} collective-permute-done((bf16[2,240,768]{2,1,0:T(8,128)(2,1)}, bf16[2,240,768]{2,1,0:T(8,128)(2,1)S(1)}, u32[]{:S(2)}, u32[]{:S(2)}) %collective-permute-start.37) | collective-permute-done | bytes 737312 | tf_op jit(solution)/shard_map/ppermute | solution.py:21
  538.2 17.7 %collective-permute-done.35 = bf16[2,240,768]{2,1,0:T(8,128)(2,1)S(1)} collective-permute-done((bf16[2,240,768]{2,1,0:T(8,128)(2,1)}, bf16[2,240,768]{2,1,0:T(8,128)(2,1)S(1)}, u32[]{:S(2)}, u32[]{:S(2)}) %collective-permute-start.35) | collective-permute-done | bytes 737312 | tf_op jit(solution)/shard_map/ppermute | solution.py:21
  588.6 17.8 %collective-permute-done.40 = bf16[2,240,768]{2,1,0:T(8,128)(2,1)S(1)} collective-permute-done((bf16[2,240,768]{2,1,0:T(8,128)(2,1)S(1)}, bf16[2,240,768]{2,1,0:T(8,128)(2,1)S(1)}, u32[]{:S(2)}, u32[]{:S(2)}) %collective-permute-start.40) | collective-permute-done | bytes 737312 | tf_op jit(solution)/shard_map/ppermute | solution.py:21
  612.8 27.5 %shard_map.250 = (f32[960,384]{1,0:T(8,128)}, bf16[2,960,384]{2,1,0:T(8,128)(2,1)}, bf16[2,960,384]{2,1,0:T(8,128)(2,1)}, bf16[2,960,384]{2,1,0:T(8,128)(2,1)}, bf16[2,960,384]{2,1,0:T(8,128)(2,1)}) custom-call(bf16[960,384]{1,0:T(8,128)(2,1)} %copy-done.34, bf16[2,960,384]{2,1,0:T(8,128)(2,1)} %copy-done.26, ...), custom_call_target="tpu_custom_call" | custom-call | flops 7372800 | bytes 368640 | tf_op jit(solution)/shard_map/pallas_call | solution.py:558
  646.8 12.3 %shard_map.251 = (bf16[2,240,768]{2,1,0:T(8,128)(2,1)}, f32[2,240,768]{2,1,0:T(8,128)}, bf16[2,240,768]{2,1,0:T(8,128)(2,1)}, f32[2,240,768]{2,1,0:T(8,128)}) custom-call(bf16[960,1536]{1,0:T(8,128)(2,1)} %get-tuple-element.117.right_ref.rows_ref, bf16[2,768,1536]{2,1,0:T(8,128)(2,1)} %all-gather.11.cloned.1.call-done.dn_ref.refs_0_, ...), custom_call_target="tpu_custom_call" | custom-call | flops 1048576 | bytes 1048576 | tf_op jit(solution)/shard_map/pallas_call | solution.py:367
  668.4 8.7 collective-permute-done.46
  680.3 20.6 %collective-permute-done.44 = bf16[2,240,768]{2,1,0:T(8,128)(2,1)} collective-permute-done((bf16[2,240,768]{2,1,0:T(8,128)(2,1)S(1)}, bf16[2,240,768]{2,1,0:T(8,128)(2,1)}, u32[]{:S(2)}, u32[]{:S(2)}) %collective-permute-start.44) | collective-permute-done | bytes 737312 | tf_op jit(solution)/shard_map/ppermute | solution.py:21
  709.4 10.9 %collective-permute-done.47 = bf16[240,768]{1,0:T(8,128)(2,1)} collective-permute-done((bf16[240,768]{1,0:T(8,128)(2,1)}, bf16[240,768]{1,0:T(8,128)(2,1)}, u32[]{:S(2)}, u32[]{:S(2)}) %collective-permute-start.47) | collective-permute-done | bytes 368672 | tf_op jit(solution)/shard_map/ppermute | solution.py:21
  729.7 10.8 %collective-permute-done.50.h_ref = bf16[2,960,384]{2,1,0:T(8,128)(2,1)} collective-permute-done((bf16[2,960,384]{2,1,0:T(8,128)(2,1)}, bf16[2,960,384]{2,1,0:T(8,128)(2,1)}, u32[]{:S(2)}, u32[]{:S(2)}) %collective-permute-start.50) | collective-permute-done | bytes 1474592 | tf_op jit(solution)/shard_map/ppermute | solution.py:21
  740.5 10.6 %shard_map.255 = (bf16[960,1152]{1,0:T(8,128)(2,1)}, f32[4,384]{1,0:T(4,128)S(1)}) custom-call(f32[960,384]{1,0:T(8,128)S(1)} %copy-done.35, bf16[2,960,384]{2,1,0:T(8,128)(2,1)S(1)} %copy-done.36, bf16[2,960,384]{2,1,0:T(8,128)(2,1)} %collective-permute-done.49.c_ref, bf16[2,960,384]{2,1,0:T(8,128)(2,1)} %collective-permute-done.50.h_ref, ...), custom_call_target="tpu_custom_call" | custom-call | flops 1048576 | bytes 1048576 | tf_op jit(solution)/shard_map/pallas_call | solution.py:194
  763.5 9.9 %shard_map.256 = (bf16[2,240,768]{2,1,0:T(8,128)(2,1)}, f32[2,240,768]{2,1,0:T(8,128)}, bf16[2,240,768]{2,1,0:T(8,128)(2,1)}, f32[2,240,768]{2,1,0:T(8,128)}) custom-call(bf16[960,1152]{1,0:T(8,128)(2,1)} %get-tuple-element.131.rows_ref.right_ref, bf16[6,768,384]{2,1,0:T(8,128)(2,1)} %all-gather.5.cloned.1.call-done.refs_0_, ...), custom_call_target="tpu_custom_call" | custom-call | flops 1048576 | bytes 1048576 | tf_op jit(solution)/shard_map/pallas_call | solution.py:367
  862.0 21.0 %reduce-scatter.9.cloned.1.call-done = bf16[2,3,192,384]{3,2,1,0:T(8,128)(2,1)} async-done(((bf16[2,3,768,384]{3,2,1,0:T(8,128)(2,1)}), bf16[2,3,192,384]{3,2,1,0:T(8,128)(2,1)}) %reduce-scatter.9.cloned.1.call-update) | async-done | bytes 884752 | tf_op jit(solution)/shard_map/reduce_scatter | solution.py:418
  886.5 11.1 %collective-permute-done.68 = bf16[2,3,192,384]{3,2,1,0:T(8,128)(2,1)S(1)} collective-permute-done((bf16[2,3,192,384]{3,2,1,0:T(8,128)(2,1)}, bf16[2,3,192,384]{3,2,1,0:T(8,128)(2,1)S(1)}, u32[]{:S(2)}, u32[]{:S(2)}) %collective-permute-start.68) | collective-permute-done | bytes 884768 | tf_op jit(solution)/shard_map/ppermute | solution.py:25
  (489 shorter events, 354.3 us)
Async XLA Ops:
  7.2 114.3 %all-gather.5.cloned.1.call-start = ((), (), s32[]{:S(2)}) async-start(), calls=%async_computation.4 | async-start | bytes 4423680 | tf_op jit(solution)/shard_map/all_gather | solution.py:83
  43.3 213.1 %all-gather.7.cloned.1.call-start = ((), (), s32[]{:S(2)}) async-start(), calls=%async_computation.5 | async-start | bytes 1474560 | tf_op jit(solution)/shard_map/all_gather | solution.py:83
  68.6 34.3 %collective-permute-start.7 = (bf16[2,240,768]{2,1,0:T(8,128)(2,1)S(1)}, bf16[2,240,768]{2,1,0:T(8,128)(2,1)S(1)}, u32[]{:S(2)}, u32[]{:S(2)}) collective-permute-start(bf16[2,240,768]{2,1,0:T(8,128)(2,1)S(1)} %pad_maximum_fusion.12), channel_id=1, source_target_pairs={{0,4},{4,0},{1,5},{5,1},{2,6},{6,2},{3,7},{7,3},{8,12},{12,8},{9,1... | collective-permute-start | bytes 2211848 | tf_op jit(solution)/shard_map/ppermute | solution.py:21
  79.5 24.8 %collective-permute-start.9 = (bf16[2,240,768]{2,1,0:T(8,128)(2,1)S(1)}, bf16[2,240,768]{2,1,0:T(8,128)(2,1)S(1)}, u32[]{:S(2)}, u32[]{:S(2)}) collective-permute-start(bf16[2,240,768]{2,1,0:T(8,128)(2,1)S(1)} %pad_maximum_fusion.13), channel_id=1, source_target_pairs={{0,2},{2,0},{1,3},{3,1},{4,6},{6,4},{5,7},{7,5},{8,10},{10,8},{9,1... | collective-permute-start | bytes 2211848 | tf_op jit(solution)/shard_map/ppermute | solution.py:21
  145.6 215.8 %all-gather.9.cloned.1.call-start = ((), (), s32[]{:S(2)}) async-start(), calls=%async_computation.6 | async-start | bytes 5898240 | tf_op jit(solution)/shard_map/all_gather | solution.py:83
  145.6 35.3 %collective-permute-start.29 = (bf16[2,192,1536]{2,1,0:T(8,128)(2,1)}, bf16[2,192,1536]{2,1,0:T(8,128)(2,1)S(1)}, u32[]{:S(2)}, u32[]{:S(2)}) collective-permute-start(bf16[2,192,1536]{2,1,0:T(8,128)(2,1)} %param.21), channel_id=1, source_target_pairs={{1,4},{4,1},{3,6},{6,3},{9,12},{12,9},{11,14},{14,11},{17,20},{20,... | collective-permute-start | bytes 3538952 | tf_op jit(solution)/shard_map/ppermute | solution.py:25
  182.0 225.2 %all-gather.11.cloned.1.call-start = ((), (), s32[]{:S(2)}) async-start(), calls=%async_computation.7 | async-start | bytes 5898240 | tf_op jit(solution)/shard_map/all_gather | solution.py:83
  182.1 30.8 %collective-permute-start.31 = (bf16[2,192,1536]{2,1,0:T(8,128)(2,1)}, bf16[2,192,1536]{2,1,0:T(8,128)(2,1)S(1)}, u32[]{:S(2)}, u32[]{:S(2)}) collective-permute-start(bf16[2,192,1536]{2,1,0:T(8,128)(2,1)} %bitcast.165), channel_id=1, source_target_pairs={{1,4},{4,1},{3,6},{6,3},{9,12},{12,9},{11,14},{14,11},{17,20},{20,... | collective-permute-start | bytes 3538952 | tf_op jit(solution)/shard_map/ppermute | solution.py:25
  186.4 69.3 %collective-permute-start.13 = (bf16[2,960,384]{2,1,0:T(8,128)(2,1)}, bf16[2,960,384]{2,1,0:T(8,128)(2,1)}, u32[]{:S(2)}, u32[]{:S(2)}) collective-permute-start(bf16[2,960,384]{2,1,0:T(8,128)(2,1)} %copy-done.26), channel_id=1, source_target_pairs={{0,8},{8,0},{1,9},{9,1},{2,10},{10,2},{3,11},{11,3},{4,12},{12,4},... | collective-permute-start | bytes 4423688 | tf_op jit(solution)/shard_map/ppermute | solution.py:21
  255.7 445.1 %reduce-scatter.5.cloned.1.call-start = ((), (), s32[]{:S(2)}) async-start(), calls=%async_computation.8 | async-start | bytes 5898240 | tf_op jit(solution)/shard_map/reduce_scatter | solution.py:418
  286.2 40.9 %collective-permute-start.17 = (bf16[2,240,768]{2,1,0:T(8,128)(2,1)}, bf16[2,240,768]{2,1,0:T(8,128)(2,1)S(1)}, u32[]{:S(2)}, u32[]{:S(2)}) collective-permute-start(bf16[2,240,768]{2,1,0:T(8,128)(2,1)} %get-tuple-element.89), channel_id=1, source_target_pairs={{0,4},{4,0},{1,5},{5,1},{2,6},{6,2},{3,7},{7,3},{8,12},{12,8},{9,1... | collective-permute-start | bytes 2211848 | tf_op jit(solution)/shard_map/ppermute | solution.py:21
  304.4 30.6 %collective-permute-start.20 = (bf16[240,768]{1,0:T(8,128)(2,1)S(1)}, bf16[240,768]{1,0:T(8,128)(2,1)S(1)}, u32[]{:S(2)}, u32[]{:S(2)}) collective-permute-start(bf16[240,768]{1,0:T(8,128)(2,1)S(1)} %fusion.38), channel_id=1, source_target_pairs={{0,4},{4,0},{1,5},{5,1},{2,6},{6,2},{3,7},{7,3},{8,12},{12,8},{9,1... | collective-permute-start | bytes 1105928 | tf_op jit(solution)/shard_map/ppermute | solution.py:21
  349.0 33.3 %collective-permute-start.22 = (bf16[2,240,768]{2,1,0:T(8,128)(2,1)}, bf16[2,240,768]{2,1,0:T(8,128)(2,1)}, u32[]{:S(2)}, u32[]{:S(2)}) collective-permute-start(bf16[2,240,768]{2,1,0:T(8,128)(2,1)} %pad_maximum_fusion.14), channel_id=1, source_target_pairs={{0,4},{4,0},{1,5},{5,1},{2,6},{6,2},{3,7},{7,3},{8,12},{12,8},{9,1... | collective-permute-start | bytes 2211848 | tf_op jit(solution)/shard_map/ppermute | solution.py:21
  360.1 24.6 %collective-permute-start.24 = (bf16[2,240,768]{2,1,0:T(8,128)(2,1)}, bf16[2,240,768]{2,1,0:T(8,128)(2,1)}, u32[]{:S(2)}, u32[]{:S(2)}) collective-permute-start(bf16[2,240,768]{2,1,0:T(8,128)(2,1)} %pad_maximum_fusion.15), channel_id=1, source_target_pairs={{0,2},{2,0},{1,3},{3,1},{4,6},{6,4},{5,7},{7,5},{8,10},{10,8},{9,1... | collective-permute-start | bytes 2211848 | tf_op jit(solution)/shard_map/ppermute | solution.py:21
  361.4 78.0 %collective-permute-start.30 = (bf16[2,768,1536]{2,1,0:T(8,128)(2,1)}, bf16[2,768,1536]{2,1,0:T(8,128)(2,1)}, u32[]{:S(2)}, u32[]{:S(2)}) collective-permute-start(bf16[2,768,1536]{2,1,0:T(8,128)(2,1)} %all-gather.9.cloned.1.call-done.un_ref.refs_0_), channel_id=1, source_target_pairs={{0,1},{1,0},{2,3},{3,2},{4,5},{5,4},{6,7},{7,6},{8,9},{9,8},{10,11... | collective-permute-start | bytes 14155784 | tf_op jit(solution)/shard_map/ppermute | solution.py:21
  407.3 32.1 %collective-permute-start.32 = (bf16[2,768,1536]{2,1,0:T(8,128)(2,1)}, bf16[2,768,1536]{2,1,0:T(8,128)(2,1)S(1)}, u32[]{:S(2)}, u32[]{:S(2)}) collective-permute-start(bf16[2,768,1536]{2,1,0:T(8,128)(2,1)} %all-gather.11.cloned.1.call-done.dn_ref.refs_0_), channel_id=1, source_target_pairs={{0,1},{1,0},{2,3},{3,2},{4,5},{5,4},{6,7},{7,6},{8,9},{9,8},{10,11... | collective-permute-start | bytes 14155784 | tf_op jit(solution)/shard_map/ppermute | solution.py:21
  486.2 234.1 %reduce-scatter.7.cloned.1.call-start = ((), (), s32[]{:S(2)}) async-start(), calls=%async_computation.9 | async-start | bytes 5898240 | tf_op jit(solution)/shard_map/reduce_scatter | solution.py:418
  507.2 341.2 %reduce-scatter.11.cloned.1.call-start = ((), (), s32[]{:S(2)}) async-start(), calls=%async_computation.11 | async-start | bytes 1474560 | tf_op jit(solution)/shard_map/reduce_scatter | solution.py:418
  519.6 36.2 %collective-permute-start.35 = (bf16[2,240,768]{2,1,0:T(8,128)(2,1)}, bf16[2,240,768]{2,1,0:T(8,128)(2,1)S(1)}, u32[]{:S(2)}, u32[]{:S(2)}) collective-permute-start(bf16[2,240,768]{2,1,0:T(8,128)(2,1)} %get-tuple-element.109), channel_id=1, source_target_pairs={{0,4},{4,0},{1,5},{5,1},{2,6},{6,2},{3,7},{7,3},{8,12},{12,8},{9,1... | collective-permute-start | bytes 2211848 | tf_op jit(solution)/shard_map/ppermute | solution.py:21
  537.7 26.0 %collective-permute-start.38 = (bf16[240,768]{1,0:T(8,128)(2,1)S(1)}, bf16[240,768]{1,0:T(8,128)(2,1)S(1)}, u32[]{:S(2)}, u32[]{:S(2)}) collective-permute-start(bf16[240,768]{1,0:T(8,128)(2,1)S(1)} %fusion.40), channel_id=1, source_target_pairs={{0,4},{4,0},{1,5},{5,1},{2,6},{6,2},{3,7},{7,3},{8,12},{12,8},{9,1... | collective-permute-start | bytes 1105928 | tf_op jit(solution)/shard_map/ppermute | solution.py:21
  580.4 26.1 %collective-permute-start.40 = (bf16[2,240,768]{2,1,0:T(8,128)(2,1)S(1)}, bf16[2,240,768]{2,1,0:T(8,128)(2,1)S(1)}, u32[]{:S(2)}, u32[]{:S(2)}) collective-permute-start(bf16[2,240,768]{2,1,0:T(8,128)(2,1)S(1)} %pad_maximum_fusion.18), channel_id=1, source_target_pairs={{0,4},{4,0},{1,5},{5,1},{2,6},{6,2},{3,7},{7,3},{8,12},{12,8},{9,1... | collective-permute-start | bytes 2211848 | tf_op jit(solution)/shard_map/ppermute | solution.py:21
  662.3 42.6 %collective-permute-start.48 = (bf16[2,768,384]{2,1,0:T(8,128)(2,1)}, bf16[2,768,384]{2,1,0:T(8,128)(2,1)}, u32[]{:S(2)}, u32[]{:S(2)}) collective-permute-start(bf16[2,768,384]{2,1,0:T(8,128)(2,1)} %shard_map.253), channel_id=1, source_target_pairs={{0,1},{1,0},{2,3},{3,2},{4,5},{5,4},{6,7},{7,6},{8,9},{9,8},{10,11... | collective-permute-start | bytes 3538952 | tf_op jit(solution)/shard_map/ppermute | solution.py:21
  663.1 37.8 %collective-permute-start.44 = (bf16[2,240,768]{2,1,0:T(8,128)(2,1)S(1)}, bf16[2,240,768]{2,1,0:T(8,128)(2,1)}, u32[]{:S(2)}, u32[]{:S(2)}) collective-permute-start(bf16[2,240,768]{2,1,0:T(8,128)(2,1)S(1)} %copy-done.88), channel_id=1, source_target_pairs={{0,4},{4,0},{1,5},{5,1},{2,6},{6,2},{3,7},{7,3},{8,12},{12,8},{9,1... | collective-permute-start | bytes 2211848 | tf_op jit(solution)/shard_map/ppermute | solution.py:21
  664.8 64.9 %collective-permute-start.49 = (bf16[2,960,384]{2,1,0:T(8,128)(2,1)}, bf16[2,960,384]{2,1,0:T(8,128)(2,1)}, u32[]{:S(2)}, u32[]{:S(2)}) collective-permute-start(bf16[2,960,384]{2,1,0:T(8,128)(2,1)} %get-tuple-element.128), channel_id=1, source_target_pairs={{0,1},{1,0},{2,3},{3,2},{4,5},{5,4},{6,7},{7,6},{8,9},{9,8},{10,11... | collective-permute-start | bytes 4423688 | tf_op jit(solution)/shard_map/ppermute | solution.py:21
  665.1 75.4 %collective-permute-start.50 = (bf16[2,960,384]{2,1,0:T(8,128)(2,1)}, bf16[2,960,384]{2,1,0:T(8,128)(2,1)}, u32[]{:S(2)}, u32[]{:S(2)}) collective-permute-start(bf16[2,960,384]{2,1,0:T(8,128)(2,1)} %add_convert_fusion), channel_id=1, source_target_pairs={{0,8},{8,0},{1,9},{9,1},{2,10},{10,2},{3,11},{11,3},{4,12},{12,4},... | collective-permute-start | bytes 4423688 | tf_op jit(solution)/shard_map/ppermute | solution.py:21
  678.1 42.2 %collective-permute-start.47 = (bf16[240,768]{1,0:T(8,128)(2,1)}, bf16[240,768]{1,0:T(8,128)(2,1)}, u32[]{:S(2)}, u32[]{:S(2)}) collective-permute-start(bf16[240,768]{1,0:T(8,128)(2,1)} %fusion.42), channel_id=1, source_target_pairs={{0,4},{4,0},{1,5},{5,1},{2,6},{6,2},{3,7},{7,3},{8,12},{12,8},{9,1... | collective-permute-start | bytes 1105928 | tf_op jit(solution)/shard_map/ppermute | solution.py:21
  700.9 50.3 %collective-permute-start.51 = (bf16[2,192,1536]{2,1,0:T(8,128)(2,1)}, bf16[2,192,1536]{2,1,0:T(8,128)(2,1)}, u32[]{:S(2)}, u32[]{:S(2)}) collective-permute-start(bf16[2,192,1536]{2,1,0:T(8,128)(2,1)} %reduce-scatter.5.cloned.1.call-done), channel_id=1, source_target_pairs={{1,4},{4,1},{3,6},{6,3},{9,12},{12,9},{11,14},{14,11},{17,20},{20,... | collective-permute-start | bytes 3538952 | tf_op jit(solution)/shard_map/ppermute | solution.py:25
  720.3 37.2 %collective-permute-start.52 = (bf16[2,192,1536]{2,1,0:T(8,128)(2,1)}, bf16[2,192,1536]{2,1,0:T(8,128)(2,1)S(1)}, u32[]{:S(2)}, u32[]{:S(2)}) collective-permute-start(bf16[2,192,1536]{2,1,0:T(8,128)(2,1)} %reduce-scatter.7.cloned.1.call-done), channel_id=1, source_target_pairs={{1,4},{4,1},{3,6},{6,3},{9,12},{12,9},{11,14},{14,11},{17,20},{20,... | collective-permute-start | bytes 3538952 | tf_op jit(solution)/shard_map/ppermute | solution.py:25
  763.4 119.5 %reduce-scatter.9.cloned.1.call-start = ((), (), s32[]{:S(2)}) async-start(), calls=%async_computation.10 | async-start | bytes 4423680 | tf_op jit(solution)/shard_map/reduce_scatter | solution.py:418
  774.9 26.0 %collective-permute-start.53 = (bf16[2,240,768]{2,1,0:T(8,128)(2,1)}, bf16[2,240,768]{2,1,0:T(8,128)(2,1)}, u32[]{:S(2)}, u32[]{:S(2)}) collective-permute-start(bf16[2,240,768]{2,1,0:T(8,128)(2,1)} %get-tuple-element.133), channel_id=1, source_target_pairs={{0,4},{4,0},{1,5},{5,1},{2,6},{6,2},{3,7},{7,3},{8,12},{12,8},{9,1... | collective-permute-start | bytes 2211848 | tf_op jit(solution)/shard_map/ppermute | solution.py:21
  848.4 36.5 %collective-permute-start.69 = (bf16[2,192,384]{2,1,0:T(8,128)(2,1)}, bf16[2,192,384]{2,1,0:T(8,128)(2,1)S(1)}, u32[]{:S(2)}, u32[]{:S(2)}) collective-permute-start(bf16[2,192,384]{2,1,0:T(8,128)(2,1)} %reduce-scatter.11.cloned.1.call-done), channel_id=1, source_target_pairs={{1,4},{4,1},{3,6},{6,3},{9,12},{12,9},{11,14},{14,11},{17,20},{20,... | collective-permute-start | bytes 884744 | tf_op jit(solution)/shard_map/ppermute | solution.py:25
  861.0 24.9 %collective-permute-start.66 = (f32[3,768]{1,0:T(4,128)S(1)}, f32[3,768]{1,0:T(4,128)S(1)}, u32[]{:S(2)}, u32[]{:S(2)}) collective-permute-start(f32[3,768]{1,0:T(4,128)S(1)} %pad_maximum_fusion.27), channel_id=1, source_target_pairs={{0,16},{16,0},{1,17},{17,1},{2,18},{18,2},{3,19},{19,3},{4,20},{20... | collective-permute-start | bytes 27656 | tf_op jit(solution)/shard_map/ppermute | solution.py:21
  (136 other events, 1282.8 us)
Sparse Core Ops, SparseCore 0:
  43.4 77.9 all-gather.4
  145.7 50.0 all-gather.6
  198.2 111.8 all-gather.8
  312.4 94.8 all-gather.10
  486.3 94.3 reduce-scatter.4
  583.5 101.6 reduce-scatter.6
  763.5 36.4 reduce-scatter.10
  803.2 79.7 reduce-scatter.8

commit v4 on v3

--- a/solution.py
+++ b/solution.py
@@ -719,7 +719,8 @@
     )
     o_total = pair_grad(attn_rows, after(attended, query_sum), sizes)
     grad_down, grad_up = own_grad(down_shard), own_grad(up_shard)
-    grad_o = own_grad(shard_grad(after(o_total, up_shard)))
+    o_shard = shard_grad(after(o_total, up_shard))
+    grad_o = own_grad(o_shard)
 
     low_all, gain_sums = call(
         functools.partial(qkv_back_kernel, sizes, head_dim),
@@ -732,7 +733,7 @@
         gains,
     )
     gain_terms = jnp.sum(gain_sums.reshape(2, 2, heads, head_dim), axis=2) * scales[None, :, None]
-    low_all = after(low_all, (grad_down, grad_up, mlp_out))
+    low_all = after(low_all, (grad_down, grad_up, mlp_out, o_shard))
     grad_qkv = own_grad(shard_grad(pair_grad(first, low_all, sizes, True)))
     first_grad, _ = reduce_rows(*project(low_all, qkv_near, qkv_far, sizes))
     input_grads, one_sums = call(

time: 917 us -> 933 us (1.017)
  starting transfers between devices: 86.6 us -> 107 us
  waiting for transfers between devices: 510 us -> 499 us
    ppermute x62, waiting for transfers between devices: 361 us -> 333 us  [trade(): return lax.ppermute(values, axis, [(0, 1), (1, 0)])]
    ppermute x62, starting transfers between devices: 58.8 us -> 75.5 us  [trade(): return lax.ppermute(values, axis, [(0, 1), (1, 0)])]
    reduce_scatter x4, waiting for transfers between devices: 21 us -> 34.6 us  [shard_grad(): lax.psum_scatter(total, ('s', 'h'), scatter_dimension=total.ndim - 2, til...]
    unnamed x184 -> x174, local copies, waits for them, and re-layouts: 33.2 us -> 37.1 us
  transfers between devices with their start and end apart: 78 -> 78, of which waited for: 52 -> 48; matrix products, arithmetic and copies ran while one was open for 9% -> 9% of each run, Pallas kernels for 14% -> 13%
where the time goes in v4:
time: 933 us; the launch traced here: 918 us
  waiting for transfers between devices  499 us (53%)
  Pallas kernels  171 us (18%)
  starting transfers between devices  107 us (11%)
  other arithmetic  50.6 us (5%)
  local copies, waits for them, and re-layouts  46.8 us (5%)
  matrix products  26.9 us (3%)
  between operations  16.4 us (2%)
    ppermute x62, waiting for transfers between devices, trade(): return lax.ppermute(values, axis, [(0, 1), (1, 0)])  333 us
    ppermute x8, waiting for transfers between devices, cross(): moved = lax.ppermute(values, ('l', 'c'), [(1, 2), (2, 1)])  93.7 us
    ppermute x62, starting transfers between devices, trade(): return lax.ppermute(values, axis, [(0, 1), (1, 0)])  75.5 us
    pallas_call x8, Pallas kernels, stream_grads(): pl.pallas_call(functools.partial(grad_kernel, sizes, bool(extra)), grid=(...  38.6 us
    pallas_call x4, Pallas kernels, project(): pl.pallas_call(functools.partial(project_kernel, sizes), grid=(half // ti...  37.8 us
    all_gather x4, waiting for transfers between devices, gather_weight(): return lax.all_gather(own, ('s', 'h'), axis=1, tiled=True)  37.2 us
    unnamed x174, local copies, waits for them, and re-layouts  37.1 us
    reduce_scatter x4, waiting for transfers between devices, shard_grad(): lax.psum_scatter(total, ('s', 'h'), scatter_dimension=total.ndim - 2, til...  34.6 us
  transfers between devices with their start and end apart: 78, of which 48 were waited for; matrix products, arithmetic and copies ran while one was open for 9% of the time, Pallas kernels for 13%

profile of v4, /device:TPU:1, one launch (start us, length us, event | category | flops | bytes accessed | tf_op | source)
XLA Modules:
  0.0 917.6 jit_solution(2269940960491670944)
XLA Ops:
  31.6 10.7 %collective-permute-done.10 = bf16[6,192,384]{2,1,0:T(8,128)(2,1)S(1)} collective-permute-done((bf16[6,192,384]{2,1,0:T(8,128)(2,1)S(1)}, bf16[6,192,384]{2,1,0:T(8,128)(2,1)S(1)}, u32[]{:S(2)}, u32[]{:S(2)}) %collective-permute-start.10) | collective-permute-done | bytes 884768 | tf_op jit(solution)/shard_map/ppermute | solution.py:25
  71.3 8.1 collective-permute-done.8
  79.7 23.2 %collective-permute-done.7 = bf16[2,240,768]{2,1,0:T(8,128)(2,1)S(1)} collective-permute-done((bf16[2,240,768]{2,1,0:T(8,128)(2,1)S(1)}, bf16[2,240,768]{2,1,0:T(8,128)(2,1)S(1)}, u32[]{:S(2)}, u32[]{:S(2)}) %collective-permute-start.7) | collective-permute-done | bytes 737312 | tf_op jit(solution)/shard_map/ppermute | solution.py:21
  104.4 17.1 %all-gather.5.cloned.1.call-done.refs_0_ = bf16[6,768,384]{2,1,0:T(8,128)(2,1)} async-done(((bf16[6,192,384]{2,1,0:T(8,128)(2,1)}), bf16[6,768,384]{2,1,0:T(8,128)(2,1)}) %all-gather.5.cloned.1.call-update) | async-done | bytes 3538960 | tf_op jit(solution)/shard_map/all_gather | solution.py:83
  133.8 9.8 %shard_map.238 = (bf16[960,384]{1,0:T(8,128)(2,1)S(1)}, bf16[2,960,384]{2,1,0:T(8,128)(2,1)S(1)}, f32[2,960,384]{2,1,0:T(8,128)}) custom-call(bf16[960,768]{1,0:T(8,128)(2,1)S(1)} %copy-done.6, bf16[960,768]{1,0:T(8,128)(2,1)S(1)} %pad_maximum_fusion.1.far_ref.left_ref, bf16[2,3,768,384]{3,2,1,0:T(8,128)(2,1)} %bitcast.151, ...), custom_call_target="tpu_custom_call" | custom-call | flops 1048576 | bytes 1048576 | tf_op jit(solution)/shard_map/pallas_call | solution.py:236
  147.5 33.3 %collective-permute-done.29 = bf16[2,192,1536]{2,1,0:T(8,128)(2,1)S(1)} collective-permute-done((bf16[2,192,1536]{2,1,0:T(8,128)(2,1)}, bf16[2,192,1536]{2,1,0:T(8,128)(2,1)S(1)}, u32[]{:S(2)}, u32[]{:S(2)}) %collective-permute-start.29) | collective-permute-done | bytes 1179680 | tf_op jit(solution)/shard_map/ppermute | solution.py:25
  186.4 26.4 %collective-permute-done.31 = bf16[2,192,1536]{2,1,0:T(8,128)(2,1)S(1)} collective-permute-done((bf16[2,192,1536]{2,1,0:T(8,128)(2,1)}, bf16[2,192,1536]{2,1,0:T(8,128)(2,1)S(1)}, u32[]{:S(2)}, u32[]{:S(2)}) %collective-permute-start.31) | collective-permute-done | bytes 1179680 | tf_op jit(solution)/shard_map/ppermute | solution.py:25
  214.0 41.7 %collective-permute-done.13.refs_3_ = bf16[2,960,384]{2,1,0:T(8,128)(2,1)} collective-permute-done((bf16[2,960,384]{2,1,0:T(8,128)(2,1)}, bf16[2,960,384]{2,1,0:T(8,128)(2,1)}, u32[]{:S(2)}, u32[]{:S(2)}) %collective-permute-start.13) | collective-permute-done | bytes 1474592 | tf_op jit(solution)/shard_map/ppermute | solution.py:21
  261.6 17.8 %shard_map.239 = (bf16[960,384]{1,0:T(8,128)(2,1)}, f32[9,1,640]{2,1,0:T(1,128)}, f32[9,1,640]{2,1,0:T(1,128)}) custom-call(bf16[960,384]{1,0:T(8,128)(2,1)} %copy-done.33, bf16[2,960,384]{2,1,0:T(8,128)(2,1)} %copy-done.25, bf16[2,960,384]{2,1,0:T(8,128)(2,1)} %collective-permute-done.12.refs_2_, bf16[2,960,384]{2,1,0:T(8,128)(2,1)} %collective-permute-done.13.refs_3_, ...), custom_call_target="tpu_custom_call" | custom-call | flops 7372800 | bytes 368640 | tf_op jit(solution)/shard_map/pallas_call | solution.py:534
  285.7 17.0 %collective-permute-done.19 = bf16[2,240,768]{2,1,0:T(8,128)(2,1)S(1)} collective-permute-done((bf16[2,240,768]{2,1,0:T(8,128)(2,1)}, bf16[2,240,768]{2,1,0:T(8,128)(2,1)S(1)}, u32[]{:S(2)}, u32[]{:S(2)}) %collective-permute-start.19) | collective-permute-done | bytes 737312 | tf_op jit(solution)/shard_map/ppermute | solution.py:21
  304.0 23.0 %collective-permute-done.17 = bf16[2,240,768]{2,1,0:T(8,128)(2,1)S(1)} collective-permute-done((bf16[2,240,768]{2,1,0:T(8,128)(2,1)}, bf16[2,240,768]{2,1,0:T(8,128)(2,1)S(1)}, u32[]{:S(2)}, u32[]{:S(2)}) %collective-permute-start.17) | collective-permute-done | bytes 737312 | tf_op jit(solution)/shard_map/ppermute | solution.py:21
  340.1 7.8 collective-permute-done.21
  349.0 9.4 %collective-permute-done.23 = bf16[240,768]{1,0:T(8,128)(2,1)S(1)} collective-permute-done((bf16[240,768]{1,0:T(8,128)(2,1)S(1)}, bf16[240,768]{1,0:T(8,128)(2,1)S(1)}, u32[]{:S(2)}, u32[]{:S(2)}) %collective-permute-start.23) | collective-permute-done | bytes 368672 | tf_op jit(solution)/shard_map/ppermute | solution.py:21
  362.2 20.0 %collective-permute-done.22 = bf16[2,240,768]{2,1,0:T(8,128)(2,1)} collective-permute-done((bf16[2,240,768]{2,1,0:T(8,128)(2,1)}, bf16[2,240,768]{2,1,0:T(8,128)(2,1)}, u32[]{:S(2)}, u32[]{:S(2)}) %collective-permute-start.22) | collective-permute-done | bytes 737312 | tf_op jit(solution)/shard_map/ppermute | solution.py:21
  387.2 20.0 %all-gather.11.cloned.1.call-done.dn_ref.refs_0_ = bf16[2,768,1536]{2,1,0:T(8,128)(2,1)} async-done(((bf16[2,192,1536]{2,1,0:T(8,128)(2,1)}), bf16[2,768,1536]{2,1,0:T(8,128)(2,1)}) %all-gather.11.cloned.1.call-update) | async-done | bytes 4718608 | tf_op jit(solution)/shard_map/all_gather | solution.py:83
  409.3 9.2 collective-permute-done.25
  421.0 15.8 %collective-permute-done.26 = bf16[2,240,768]{2,1,0:T(8,128)(2,1)S(1)} collective-permute-done((bf16[2,240,768]{2,1,0:T(8,128)(2,1)S(1)}, bf16[2,240,768]{2,1,0:T(8,128)(2,1)S(1)}, u32[]{:S(2)}, u32[]{:S(2)}) %collective-permute-start.26) | collective-permute-done | bytes 737312 | tf_op jit(solution)/shard_map/ppermute | solution.py:21
  439.4 19.2 %shard_map.242 = (bf16[960,1536]{1,0:T(8,128)(2,1)}, bf16[960,1536]{1,0:T(8,128)(2,1)}) custom-call(bf16[960,768]{1,0:T(8,128)(2,1)} %pad_maximum_fusion.3.sn_ref.left_ref, bf16[960,768]{1,0:T(8,128)(2,1)} %pad_maximum_fusion.4.sf_ref.left_ref, bf16[960,768]{1,0:T(8,128)(2,1)} %pad_maximum_fusion.5.mn_ref.left_ref, ...), custom_call_target="tpu_custom_call" | custom-call | flops 1048576 | bytes 1048576 | tf_op jit(solution)/shard_map/pallas_call | solution.py:323
  511.5 11.2 %shard_map.247 = (bf16[2,240,768]{2,1,0:T(8,128)(2,1)}, f32[2,240,768]{2,1,0:T(8,128)}, bf16[2,240,768]{2,1,0:T(8,128)(2,1)}, f32[2,240,768]{2,1,0:T(8,128)}) custom-call(bf16[960,1536]{1,0:T(8,128)(2,1)} %get-tuple-element.107.right_ref.rows_ref, bf16[2,768,1536]{2,1,0:T(8,128)(2,1)} %all-gather.9.cloned.1.call-done.un_ref.refs_0_, ...), custom_call_target="tpu_custom_call" | custom-call | flops 1048576 | bytes 1048576 | tf_op jit(solution)/shard_map/pallas_call | solution.py:367
  524.6 16.1 %collective-permute-done.37 = bf16[2,240,768]{2,1,0:T(8,128)(2,1)S(1)} collective-permute-done((bf16[2,240,768]{2,1,0:T(8,128)(2,1)}, bf16[2,240,768]{2,1,0:T(8,128)(2,1)S(1)}, u32[]{:S(2)}, u32[]{:S(2)}) %collective-permute-start.37) | collective-permute-done | bytes 737312 | tf_op jit(solution)/shard_map/ppermute | solution.py:21
  542.6 17.5 %collective-permute-done.35 = bf16[2,240,768]{2,1,0:T(8,128)(2,1)S(1)} collective-permute-done((bf16[2,240,768]{2,1,0:T(8,128)(2,1)}, bf16[2,240,768]{2,1,0:T(8,128)(2,1)S(1)}, u32[]{:S(2)}, u32[]{:S(2)}) %collective-permute-start.35) | collective-permute-done | bytes 737312 | tf_op jit(solution)/shard_map/ppermute | solution.py:21
  593.0 17.8 %collective-permute-done.40 = bf16[2,240,768]{2,1,0:T(8,128)(2,1)S(1)} collective-permute-done((bf16[2,240,768]{2,1,0:T(8,128)(2,1)S(1)}, bf16[2,240,768]{2,1,0:T(8,128)(2,1)S(1)}, u32[]{:S(2)}, u32[]{:S(2)}) %collective-permute-start.40) | collective-permute-done | bytes 737312 | tf_op jit(solution)/shard_map/ppermute | solution.py:21
  617.2 27.5 %shard_map.250 = (f32[960,384]{1,0:T(8,128)}, bf16[2,960,384]{2,1,0:T(8,128)(2,1)}, bf16[2,960,384]{2,1,0:T(8,128)(2,1)}, bf16[2,960,384]{2,1,0:T(8,128)(2,1)}, bf16[2,960,384]{2,1,0:T(8,128)(2,1)}) custom-call(bf16[960,384]{1,0:T(8,128)(2,1)} %copy-done.33, bf16[2,960,384]{2,1,0:T(8,128)(2,1)} %copy-done.25, ...), custom_call_target="tpu_custom_call" | custom-call | flops 7372800 | bytes 368640 | tf_op jit(solution)/shard_map/pallas_call | solution.py:558
  650.5 11.5 %shard_map.251 = (bf16[2,240,768]{2,1,0:T(8,128)(2,1)}, f32[2,240,768]{2,1,0:T(8,128)}, bf16[2,240,768]{2,1,0:T(8,128)(2,1)}, f32[2,240,768]{2,1,0:T(8,128)}) custom-call(bf16[960,1536]{1,0:T(8,128)(2,1)} %get-tuple-element.117.right_ref.rows_ref, bf16[2,768,1536]{2,1,0:T(8,128)(2,1)} %all-gather.11.cloned.1.call-done.dn_ref.refs_0_, ...), custom_call_target="tpu_custom_call" | custom-call | flops 1048576 | bytes 1048576 | tf_op jit(solution)/shard_map/pallas_call | solution.py:367
  670.0 10.4 %collective-permute-done.46 = bf16[2,240,768]{2,1,0:T(8,128)(2,1)S(1)} collective-permute-done((bf16[2,240,768]{2,1,0:T(8,128)(2,1)}, bf16[2,240,768]{2,1,0:T(8,128)(2,1)S(1)}, u32[]{:S(2)}, u32[]{:S(2)}) %collective-permute-start.46) | collective-permute-done | bytes 737312 | tf_op jit(solution)/shard_map/ppermute | solution.py:21
  689.5 34.6 %reduce-scatter.5.cloned.1.call-done = bf16[2,192,1536]{2,1,0:T(8,128)(2,1)} async-done(((bf16[2,768,1536]{2,1,0:T(8,128)(2,1)}), bf16[2,192,1536]{2,1,0:T(8,128)(2,1)}) %reduce-scatter.5.cloned.1.call-update) | async-done | bytes 1179664 | tf_op jit(solution)/shard_map/reduce_scatter | solution.py:418
  740.8 16.8 %collective-permute-done.50.h_ref = bf16[2,960,384]{2,1,0:T(8,128)(2,1)} collective-permute-done((bf16[2,960,384]{2,1,0:T(8,128)(2,1)}, bf16[2,960,384]{2,1,0:T(8,128)(2,1)}, u32[]{:S(2)}, u32[]{:S(2)}) %collective-permute-start.50) | collective-permute-done | bytes 1474592 | tf_op jit(solution)/shard_map/ppermute | solution.py:21
  757.6 10.6 %shard_map.255 = (bf16[960,1152]{1,0:T(8,128)(2,1)}, f32[4,384]{1,0:T(4,128)S(1)}) custom-call(f32[960,384]{1,0:T(8,128)S(1)} %copy-done.34, bf16[2,960,384]{2,1,0:T(8,128)(2,1)S(1)} %copy-done.35, bf16[2,960,384]{2,1,0:T(8,128)(2,1)} %collective-permute-done.49.c_ref, bf16[2,960,384]{2,1,0:T(8,128)(2,1)} %collective-permute-done.50.h_ref, ...), custom_call_target="tpu_custom_call" | custom-call | flops 1048576 | bytes 1048576 | tf_op jit(solution)/shard_map/pallas_call | solution.py:194
  769.8 9.5 %collective-permute-done.52 = bf16[2,192,1536]{2,1,0:T(8,128)(2,1)S(1)} collective-permute-done((bf16[2,192,1536]{2,1,0:T(8,128)(2,1)}, bf16[2,192,1536]{2,1,0:T(8,128)(2,1)S(1)}, u32[]{:S(2)}, u32[]{:S(2)}) %collective-permute-start.52) | collective-permute-done | bytes 1179680 | tf_op jit(solution)/shard_map/ppermute | solution.py:25
  787.2 9.9 %shard_map.256 = (bf16[2,240,768]{2,1,0:T(8,128)(2,1)}, f32[2,240,768]{2,1,0:T(8,128)}, bf16[2,240,768]{2,1,0:T(8,128)(2,1)}, f32[2,240,768]{2,1,0:T(8,128)}) custom-call(bf16[960,1152]{1,0:T(8,128)(2,1)} %get-tuple-element.132.rows_ref.right_ref, bf16[6,768,384]{2,1,0:T(8,128)(2,1)} %all-gather.5.cloned.1.call-done.refs_0_, ...), custom_call_target="tpu_custom_call" | custom-call | flops 1048576 | bytes 1048576 | tf_op jit(solution)/shard_map/pallas_call | solution.py:367
  819.3 10.0 %collective-permute-done.56 = bf16[240,768]{1,0:T(8,128)(2,1)S(1)} collective-permute-done((bf16[240,768]{1,0:T(8,128)(2,1)S(1)}, bf16[240,768]{1,0:T(8,128)(2,1)S(1)}, u32[]{:S(2)}, u32[]{:S(2)}) %collective-permute-start.56) | collective-permute-done | bytes 368672 | tf_op jit(solution)/shard_map/ppermute | solution.py:21
  866.8 8.4 collective-permute-start.62
  (479 shorter events, 359.8 us)
Async XLA Ops:
  7.2 114.3 %all-gather.5.cloned.1.call-start = ((), (), s32[]{:S(2)}) async-start(), calls=%async_computation.4 | async-start | bytes 4423680 | tf_op jit(solution)/shard_map/all_gather | solution.py:83
  43.3 213.0 %all-gather.7.cloned.1.call-start = ((), (), s32[]{:S(2)}) async-start(), calls=%async_computation.5 | async-start | bytes 1474560 | tf_op jit(solution)/shard_map/all_gather | solution.py:83
  68.6 34.3 %collective-permute-start.7 = (bf16[2,240,768]{2,1,0:T(8,128)(2,1)S(1)}, bf16[2,240,768]{2,1,0:T(8,128)(2,1)S(1)}, u32[]{:S(2)}, u32[]{:S(2)}) collective-permute-start(bf16[2,240,768]{2,1,0:T(8,128)(2,1)S(1)} %pad_maximum_fusion.12), channel_id=1, source_target_pairs={{0,4},{4,0},{1,5},{5,1},{2,6},{6,2},{3,7},{7,3},{8,12},{12,8},{9,1... | collective-permute-start | bytes 2211848 | tf_op jit(solution)/shard_map/ppermute | solution.py:21
  79.4 24.7 %collective-permute-start.9 = (bf16[2,240,768]{2,1,0:T(8,128)(2,1)S(1)}, bf16[2,240,768]{2,1,0:T(8,128)(2,1)S(1)}, u32[]{:S(2)}, u32[]{:S(2)}) collective-permute-start(bf16[2,240,768]{2,1,0:T(8,128)(2,1)S(1)} %pad_maximum_fusion.13), channel_id=1, source_target_pairs={{0,2},{2,0},{1,3},{3,1},{4,6},{6,4},{5,7},{7,5},{8,10},{10,8},{9,1... | collective-permute-start | bytes 2211848 | tf_op jit(solution)/shard_map/ppermute | solution.py:21
  145.5 215.8 %all-gather.9.cloned.1.call-start = ((), (), s32[]{:S(2)}) async-start(), calls=%async_computation.6 | async-start | bytes 5898240 | tf_op jit(solution)/shard_map/all_gather | solution.py:83
  145.6 35.3 %collective-permute-start.29 = (bf16[2,192,1536]{2,1,0:T(8,128)(2,1)}, bf16[2,192,1536]{2,1,0:T(8,128)(2,1)S(1)}, u32[]{:S(2)}, u32[]{:S(2)}) collective-permute-start(bf16[2,192,1536]{2,1,0:T(8,128)(2,1)} %param.21), channel_id=1, source_target_pairs={{1,4},{4,1},{3,6},{6,3},{9,12},{12,9},{11,14},{14,11},{17,20},{20,... | collective-permute-start | bytes 3538952 | tf_op jit(solution)/shard_map/ppermute | solution.py:25
  182.0 225.3 %all-gather.11.cloned.1.call-start = ((), (), s32[]{:S(2)}) async-start(), calls=%async_computation.7 | async-start | bytes 5898240 | tf_op jit(solution)/shard_map/all_gather | solution.py:83
  182.1 30.8 %collective-permute-start.31 = (bf16[2,192,1536]{2,1,0:T(8,128)(2,1)}, bf16[2,192,1536]{2,1,0:T(8,128)(2,1)S(1)}, u32[]{:S(2)}, u32[]{:S(2)}) collective-permute-start(bf16[2,192,1536]{2,1,0:T(8,128)(2,1)} %bitcast.165), channel_id=1, source_target_pairs={{1,4},{4,1},{3,6},{6,3},{9,12},{12,9},{11,14},{14,11},{17,20},{20,... | collective-permute-start | bytes 3538952 | tf_op jit(solution)/shard_map/ppermute | solution.py:25
  186.3 69.3 %collective-permute-start.13 = (bf16[2,960,384]{2,1,0:T(8,128)(2,1)}, bf16[2,960,384]{2,1,0:T(8,128)(2,1)}, u32[]{:S(2)}, u32[]{:S(2)}) collective-permute-start(bf16[2,960,384]{2,1,0:T(8,128)(2,1)} %copy-done.25), channel_id=1, source_target_pairs={{0,8},{8,0},{1,9},{9,1},{2,10},{10,2},{3,11},{11,3},{4,12},{12,4},... | collective-permute-start | bytes 4423688 | tf_op jit(solution)/shard_map/ppermute | solution.py:21
  255.7 433.7 %reduce-scatter.7.cloned.1.call-start = ((), (), s32[]{:S(2)}) async-start(), calls=%async_computation.9 | async-start | bytes 5898240 | tf_op jit(solution)/shard_map/reduce_scatter | solution.py:418
  256.3 23.0 %collective-permute-start.16 = (bf16[2,768,384]{2,1,0:T(8,128)(2,1)}, bf16[2,768,384]{2,1,0:T(8,128)(2,1)}, u32[]{:S(2)}, u32[]{:S(2)}) collective-permute-start(bf16[2,768,384]{2,1,0:T(8,128)(2,1)} %all-gather.7.cloned.1.call-done.refs_0_.wn_ref), channel_id=1, source_target_pairs={{0,1},{1,0},{2,3},{3,2},{4,5},{5,4},{6,7},{7,6},{8,9},{9,8},{10,11... | collective-permute-start | bytes 3538952 | tf_op jit(solution)/shard_map/ppermute | solution.py:21
  285.7 41.3 %collective-permute-start.17 = (bf16[2,240,768]{2,1,0:T(8,128)(2,1)}, bf16[2,240,768]{2,1,0:T(8,128)(2,1)S(1)}, u32[]{:S(2)}, u32[]{:S(2)}) collective-permute-start(bf16[2,240,768]{2,1,0:T(8,128)(2,1)} %get-tuple-element.89), channel_id=1, source_target_pairs={{0,4},{4,0},{1,5},{5,1},{2,6},{6,2},{3,7},{7,3},{8,12},{12,8},{9,1... | collective-permute-start | bytes 2211848 | tf_op jit(solution)/shard_map/ppermute | solution.py:21
  304.0 31.0 %collective-permute-start.20 = (bf16[240,768]{1,0:T(8,128)(2,1)S(1)}, bf16[240,768]{1,0:T(8,128)(2,1)S(1)}, u32[]{:S(2)}, u32[]{:S(2)}) collective-permute-start(bf16[240,768]{1,0:T(8,128)(2,1)S(1)} %fusion.38), channel_id=1, source_target_pairs={{0,4},{4,0},{1,5},{5,1},{2,6},{6,2},{3,7},{7,3},{8,12},{12,8},{9,1... | collective-permute-start | bytes 1105928 | tf_op jit(solution)/shard_map/ppermute | solution.py:21
  349.0 33.3 %collective-permute-start.22 = (bf16[2,240,768]{2,1,0:T(8,128)(2,1)}, bf16[2,240,768]{2,1,0:T(8,128)(2,1)}, u32[]{:S(2)}, u32[]{:S(2)}) collective-permute-start(bf16[2,240,768]{2,1,0:T(8,128)(2,1)} %pad_maximum_fusion.14), channel_id=1, source_target_pairs={{0,4},{4,0},{1,5},{5,1},{2,6},{6,2},{3,7},{7,3},{8,12},{12,8},{9,1... | collective-permute-start | bytes 2211848 | tf_op jit(solution)/shard_map/ppermute | solution.py:21
  360.1 24.6 %collective-permute-start.24 = (bf16[2,240,768]{2,1,0:T(8,128)(2,1)}, bf16[2,240,768]{2,1,0:T(8,128)(2,1)}, u32[]{:S(2)}, u32[]{:S(2)}) collective-permute-start(bf16[2,240,768]{2,1,0:T(8,128)(2,1)} %pad_maximum_fusion.15), channel_id=1, source_target_pairs={{0,2},{2,0},{1,3},{3,1},{4,6},{6,4},{5,7},{7,5},{8,10},{10,8},{9,1... | collective-permute-start | bytes 2211848 | tf_op jit(solution)/shard_map/ppermute | solution.py:21
  361.3 78.1 %collective-permute-start.30 = (bf16[2,768,1536]{2,1,0:T(8,128)(2,1)}, bf16[2,768,1536]{2,1,0:T(8,128)(2,1)}, u32[]{:S(2)}, u32[]{:S(2)}) collective-permute-start(bf16[2,768,1536]{2,1,0:T(8,128)(2,1)} %all-gather.9.cloned.1.call-done.un_ref.refs_0_), channel_id=1, source_target_pairs={{0,1},{1,0},{2,3},{3,2},{4,5},{5,4},{6,7},{7,6},{8,9},{9,8},{10,11... | collective-permute-start | bytes 14155784 | tf_op jit(solution)/shard_map/ppermute | solution.py:21
  407.3 32.2 %collective-permute-start.32 = (bf16[2,768,1536]{2,1,0:T(8,128)(2,1)}, bf16[2,768,1536]{2,1,0:T(8,128)(2,1)}, u32[]{:S(2)}, u32[]{:S(2)}) collective-permute-start(bf16[2,768,1536]{2,1,0:T(8,128)(2,1)} %all-gather.11.cloned.1.call-done.dn_ref.refs_0_), channel_id=1, source_target_pairs={{0,1},{1,0},{2,3},{3,2},{4,5},{5,4},{6,7},{7,6},{8,9},{9,8},{10,11... | collective-permute-start | bytes 14155784 | tf_op jit(solution)/shard_map/ppermute | solution.py:21
  490.5 233.5 %reduce-scatter.5.cloned.1.call-start = ((), (), s32[]{:S(2)}) async-start(), calls=%async_computation.8 | async-start | bytes 5898240 | tf_op jit(solution)/shard_map/reduce_scatter | solution.py:418
  511.5 269.4 %reduce-scatter.9.cloned.1.call-start = ((), (), s32[]{:S(2)}) async-start(), calls=%async_computation.10 | async-start | bytes 1474560 | tf_op jit(solution)/shard_map/reduce_scatter | solution.py:418
  524.0 36.2 %collective-permute-start.35 = (bf16[2,240,768]{2,1,0:T(8,128)(2,1)}, bf16[2,240,768]{2,1,0:T(8,128)(2,1)S(1)}, u32[]{:S(2)}, u32[]{:S(2)}) collective-permute-start(bf16[2,240,768]{2,1,0:T(8,128)(2,1)} %get-tuple-element.109), channel_id=1, source_target_pairs={{0,4},{4,0},{1,5},{5,1},{2,6},{6,2},{3,7},{7,3},{8,12},{12,8},{9,1... | collective-permute-start | bytes 2211848 | tf_op jit(solution)/shard_map/ppermute | solution.py:21
  542.0 26.0 %collective-permute-start.38 = (bf16[240,768]{1,0:T(8,128)(2,1)S(1)}, bf16[240,768]{1,0:T(8,128)(2,1)S(1)}, u32[]{:S(2)}, u32[]{:S(2)}) collective-permute-start(bf16[240,768]{1,0:T(8,128)(2,1)S(1)} %fusion.40), channel_id=1, source_target_pairs={{0,4},{4,0},{1,5},{5,1},{2,6},{6,2},{3,7},{7,3},{8,12},{12,8},{9,1... | collective-permute-start | bytes 1105928 | tf_op jit(solution)/shard_map/ppermute | solution.py:21
  584.7 26.1 %collective-permute-start.40 = (bf16[2,240,768]{2,1,0:T(8,128)(2,1)S(1)}, bf16[2,240,768]{2,1,0:T(8,128)(2,1)S(1)}, u32[]{:S(2)}, u32[]{:S(2)}) collective-permute-start(bf16[2,240,768]{2,1,0:T(8,128)(2,1)S(1)} %pad_maximum_fusion.18), channel_id=1, source_target_pairs={{0,4},{4,0},{1,5},{5,1},{2,6},{6,2},{3,7},{7,3},{8,12},{12,8},{9,1... | collective-permute-start | bytes 2211848 | tf_op jit(solution)/shard_map/ppermute | solution.py:21
  591.7 19.3 %collective-permute-start.42 = (bf16[2,240,768]{2,1,0:T(8,128)(2,1)S(1)}, bf16[2,240,768]{2,1,0:T(8,128)(2,1)S(1)}, u32[]{:S(2)}, u32[]{:S(2)}) collective-permute-start(bf16[2,240,768]{2,1,0:T(8,128)(2,1)S(1)} %pad_maximum_fusion.19), channel_id=1, source_target_pairs={{0,2},{2,0},{1,3},{3,1},{4,6},{6,4},{5,7},{7,5},{8,10},{10,8},{9,1... | collective-permute-start | bytes 2211848 | tf_op jit(solution)/shard_map/ppermute | solution.py:21
  648.6 36.5 %collective-permute-start.48 = (bf16[2,768,384]{2,1,0:T(8,128)(2,1)S(1)}, bf16[2,768,384]{2,1,0:T(8,128)(2,1)S(1)}, u32[]{:S(2)}, u32[]{:S(2)}) collective-permute-start(bf16[2,768,384]{2,1,0:T(8,128)(2,1)S(1)} %shard_map.253), channel_id=1, source_target_pairs={{0,1},{1,0},{2,3},{3,2},{4,5},{5,4},{6,7},{7,6},{8,9},{9,8},{10,11... | collective-permute-start | bytes 3538952 | tf_op jit(solution)/shard_map/ppermute | solution.py:21
  663.1 63.0 %collective-permute-start.44 = (bf16[2,240,768]{2,1,0:T(8,128)(2,1)}, bf16[2,240,768]{2,1,0:T(8,128)(2,1)}, u32[]{:S(2)}, u32[]{:S(2)}) collective-permute-start(bf16[2,240,768]{2,1,0:T(8,128)(2,1)} %get-tuple-element.119), channel_id=1, source_target_pairs={{0,4},{4,0},{1,5},{5,1},{2,6},{6,2},{3,7},{7,3},{8,12},{12,8},{9,1... | collective-permute-start | bytes 2211848 | tf_op jit(solution)/shard_map/ppermute | solution.py:21
  665.4 75.4 %collective-permute-start.49 = (bf16[2,960,384]{2,1,0:T(8,128)(2,1)}, bf16[2,960,384]{2,1,0:T(8,128)(2,1)}, u32[]{:S(2)}, u32[]{:S(2)}) collective-permute-start(bf16[2,960,384]{2,1,0:T(8,128)(2,1)} %get-tuple-element.128), channel_id=1, source_target_pairs={{0,1},{1,0},{2,3},{3,2},{4,5},{5,4},{6,7},{7,6},{8,9},{9,8},{10,11... | collective-permute-start | bytes 4423688 | tf_op jit(solution)/shard_map/ppermute | solution.py:21
  666.0 91.6 %collective-permute-start.50 = (bf16[2,960,384]{2,1,0:T(8,128)(2,1)}, bf16[2,960,384]{2,1,0:T(8,128)(2,1)}, u32[]{:S(2)}, u32[]{:S(2)}) collective-permute-start(bf16[2,960,384]{2,1,0:T(8,128)(2,1)} %add_convert_fusion), channel_id=1, source_target_pairs={{0,8},{8,0},{1,9},{9,1},{2,10},{10,2},{3,11},{11,3},{4,12},{12,4},... | collective-permute-start | bytes 4423688 | tf_op jit(solution)/shard_map/ppermute | solution.py:21
  682.6 46.9 %collective-permute-start.47 = (bf16[240,768]{1,0:T(8,128)(2,1)}, bf16[240,768]{1,0:T(8,128)(2,1)}, u32[]{:S(2)}, u32[]{:S(2)}) collective-permute-start(bf16[240,768]{1,0:T(8,128)(2,1)} %fusion.42), channel_id=1, source_target_pairs={{0,4},{4,0},{1,5},{5,1},{2,6},{6,2},{3,7},{7,3},{8,12},{12,8},{9,1... | collective-permute-start | bytes 1105928 | tf_op jit(solution)/shard_map/ppermute | solution.py:21
  689.4 202.9 %reduce-scatter.11.cloned.1.call-start = ((), (), s32[]{:S(2)}) async-start(), calls=%async_computation.11 | async-start | bytes 4423680 | tf_op jit(solution)/shard_map/reduce_scatter | solution.py:418
  724.0 44.2 %collective-permute-start.51 = (bf16[2,192,1536]{2,1,0:T(8,128)(2,1)}, bf16[2,192,1536]{2,1,0:T(8,128)(2,1)S(1)}, u32[]{:S(2)}, u32[]{:S(2)}) collective-permute-start(bf16[2,192,1536]{2,1,0:T(8,128)(2,1)} %reduce-scatter.5.cloned.1.call-done), channel_id=1, source_target_pairs={{1,4},{4,1},{3,6},{6,3},{9,12},{12,9},{11,14},{14,11},{17,20},{20,... | collective-permute-start | bytes 3538952 | tf_op jit(solution)/shard_map/ppermute | solution.py:25
  729.5 49.7 %collective-permute-start.52 = (bf16[2,192,1536]{2,1,0:T(8,128)(2,1)}, bf16[2,192,1536]{2,1,0:T(8,128)(2,1)S(1)}, u32[]{:S(2)}, u32[]{:S(2)}) collective-permute-start(bf16[2,192,1536]{2,1,0:T(8,128)(2,1)} %reduce-scatter.7.cloned.1.call-done), channel_id=1, source_target_pairs={{1,4},{4,1},{3,6},{6,3},{9,12},{12,9},{11,14},{14,11},{17,20},{20,... | collective-permute-start | bytes 3538952 | tf_op jit(solution)/shard_map/ppermute | solution.py:25
  787.2 18.7 %collective-permute-start.67 = (bf16[2,3,768,384]{3,2,1,0:T(8,128)(2,1)}, bf16[2,3,768,384]{3,2,1,0:T(8,128)(2,1)}, u32[]{:S(2)}, u32[]{:S(2)}) collective-permute-start(bf16[2,3,768,384]{3,2,1,0:T(8,128)(2,1)} %shard_map.258), channel_id=1, source_target_pairs={{0,1},{1,0},{2,3},{3,2},{4,5},{5,4},{6,7},{7,6},{8,9},{9,8},{10,11... | collective-permute-start | bytes 10616840 | tf_op jit(solution)/shard_map/ppermute | solution.py:21
  (131 other events, 1253.9 us)
Sparse Core Ops, SparseCore 0:
  43.4 77.9 all-gather.4
  145.7 50.0 all-gather.6
  198.1 111.8 all-gather.8
  312.3 94.8 all-gather.10
  490.6 94.3 reduce-scatter.6
  587.9 136.1 reduce-scatter.4
  727.5 43.9 reduce-scatter.8
  813.8 75.2 reduce-scatter.10
